TPU v7x, 128 devices: a whole 4x4x4 slice. The times are simulated.
128 devices in a mesh: row: 64 (over z, y, x), col: 2 (over core).
Axes of the slice: x: 4, y: 4, z: 4, core: 2. Of those that a mesh axis runs over, the one named last changes fastest.
Arguments:
- vectors_in: bfloat16 [131072, 2048], P('row', 'col'), may hold values from -6 to 6
- panel: bfloat16 [131072, 256], P('row', 'col'), may hold values from -0.015625 to 0.015625
- factor: float32 [256, 256], replicated, may hold values from -3 to 8, as said below
- atom_basis: int32 [64, 128], P('row'), may hold values from 1 to 24, 2048 in all within a row
- proj_count: int32 [8192], P('row'), may hold values from 1 to 16
- coupling: bfloat16 [8192, 9, 384], P('row'), may hold values from -0.4375 to 0.4375
- block_present: int32 [8192, 9], P('row'), may hold values 0 or 1
- occ_mask: int32 [2048], P('col'), may hold values 0 or 1
- occ_weight: float32 [2048], P('col'), may hold values from 0.5 to 2
Outputs:
- vectors: bfloat16 [131072, 2048], P('row', 'col')
- density: float32 [8192, 256], P(('row', 'col'))
Inputs may be any that keep to these rules, and one draw needn't show every extreme that they name: `factor`: zero below the diagonal; the diagonal lies in 4 to 8. `atom_basis`: each row sums to 2048, and 24 is reached in each row.
All inputs are finite; a program needn't handle non-finite values. No bound on the sum of `block_present` or of `occ_mask` on one device may be relied on, other than what follows from the above.
Results may differ from a plain program's by a relative error of at most 0.0075.
Values may be sent and summed in bfloat16 or wider, within the bound.
No kernel may reach another device: no remote copies, remote signals or barrier semaphores. Data moves between devices by JAX's collectives and lax.ppermute only.
A program may use at most 192 MiB of HBM per device.

v0:
```python
import jax
import jax.numpy as jnp
from jax import lax
from jax.sharding import PartitionSpec as P

NPMAX = 16
BMAX = 24
K = 9


def with_halo(array, sides, width):
    for axis, dim in sides:
        devices, length = (lax.axis_size(axis), array.shape[dim])
        up = [(i, (i + 1) % devices) for i in range(devices)]
        down = [(j, i) for i, j in up]
        last = lax.slice_in_dim(array, length - width, length, axis=dim)
        first = lax.slice_in_dim(array, 0, width, axis=dim)
        before = lax.ppermute(last, axis, up)
        after = lax.ppermute(first, axis, down)
        array = jnp.concatenate([before, array, after], axis=dim)
    return array


def panel_product(fragment, columns):
    return lax.dot_general(
        fragment, columns, (((0,), (0,)), ((), ())), preferred_element_type=jnp.float32
    )


def local(
    vectors_in, panel, factor, atom_basis, proj_count, coupling, block_present, occ_mask, occ_weight
):
    rows_here = vectors_in.shape[0]
    cols_here = vectors_in.shape[1]
    whole_panel = lax.all_gather(panel, "col", axis=1, tiled=True)
    inner_products = panel_product(whole_panel, vectors_in)
    inner_products = lax.psum(inner_products, "row")
    mixing = jnp.dot(factor.T, inner_products, precision=lax.Precision.HIGHEST).astype(jnp.bfloat16)
    update = jnp.dot(whole_panel, mixing, preferred_element_type=jnp.float32)
    vectors = (vectors_in.astype(jnp.float32) - update).astype(jnp.bfloat16)
    counts = atom_basis[0]
    atoms_here = counts.shape[0]
    starts = jnp.cumsum(counts) - counts
    slot_rank = jnp.arange(BMAX, dtype=jnp.int32)
    row_index = jnp.where(
        slot_rank[None, :] < counts[:, None], starts[:, None] + slot_rank[None, :], rows_here
    )
    padded = jnp.take(vectors, row_index.reshape(-1), axis=0, mode="fill", fill_value=0).reshape(
        atoms_here, BMAX, cols_here
    )
    rim_width = (K - 1) // 2
    extended = with_halo(padded, (("row", 0),), rim_width)
    projections = jnp.zeros((atoms_here, NPMAX, cols_here), jnp.float32)
    for relative in range(K):
        blocks = coupling[:, relative].reshape(atoms_here, NPMAX, BMAX)
        blocks = jnp.where(
            block_present[:, relative, None, None] > 0, blocks, jnp.zeros_like(blocks)
        )
        neighbours = extended[relative : relative + atoms_here]
        projections = projections + jnp.einsum(
            "aij,ajn->ain", blocks, neighbours, preferred_element_type=jnp.float32
        )
    kept_rows = (jnp.arange(NPMAX, dtype=jnp.int32)[None, :] < proj_count[:, None]).astype(
        jnp.float32
    )
    rounded = (projections * kept_rows[:, :, None]).astype(jnp.bfloat16)
    column_total = cols_here * lax.axis_size("col")
    weights = occ_mask.astype(jnp.float32) * occ_weight / column_total
    weighted = (rounded * weights[None, None, :]).astype(jnp.bfloat16)
    partial_value = jnp.einsum(
        "ain,ajn->aij", weighted, rounded, preferred_element_type=jnp.float32
    )
    partial_value = partial_value.reshape(atoms_here, NPMAX * NPMAX)
    summed = lax.psum(partial_value.astype(jnp.bfloat16), "col").astype(jnp.float32)
    per_device = atoms_here // lax.axis_size("col")
    density = lax.dynamic_slice_in_dim(summed, lax.axis_index("col") * per_device, per_device, 0)
    return (vectors, density)


def solution(mesh):
    placed = (
        P("row", "col"),
        P("row", "col"),
        P(),
        P("row", None),
        P("row"),
        P("row", None, None),
        P("row", None),
        P("col"),
        P("col"),
    )
    return jax.shard_map(
        local,
        mesh=mesh,
        in_specs=placed,
        out_specs=(P("row", "col"), P(("row", "col"), None)),
        check_vma=False,
    )
```

profile of v0, /device:TPU:1, one launch (start us, length us, event | category | flops | bytes accessed | tf_op | source)
XLA Modules:
  0.0 322.8 jit_solution(1924844101190805468)
XLA Ops:
  8.0 0.8 copy.17
  9.7 0.8 add_select_fusion
  10.6 1.4 fusion.48
  12.2 1.0 compare_bitcast_fusion.7
  13.7 6.4 %copy.15 = bf16[2048,1024]{0,1:T(8,128)(2,1)} copy(bf16[2048,1024]{1,0:T(8,128)(2,1)} %param.9) | data formatting | bytes 8388608 | tf_op args[0]
  20.5 1.2 copy.19
  21.7 1.2 copy.21
  23.6 1.2 copy.29
  24.8 1.2 copy.31
  26.3 1.2 copy.33
  28.7 4.9 %fusion.51 = f32[256,1024]{1,0:T(8,128)} fusion(bf16[2048,256]{1,0:T(8,128)(2,1)} %all-gather.2.cloned.1.call-done, bf16[2048,1024]{1,0:T(8,128)(2,1)} %param.9), kind=kOutput, calls=%fused_computation.89 | convolution fusion | flops 1073741824 | bytes 6291456 | tf_op jit(solution)/shard_map/dot_general | solution.py:25
  33.7 130.9 %all-reduce.3.cloned.1.call-done = f32[256,1024]{1,0:T(8,128)} async-done(((f32[256,1024]{1,0:T(8,128)}), f32[256,1024]{1,0:T(8,128)}) %all-reduce.3.cloned.1.call-update) | async-done | bytes 1048592 | tf_op jit(solution)/shard_map/psum | solution.py:37
  164.7 3.0 convolution_convert_fusion
  167.7 5.4 %fusion = bf16[2048,1024]{0,1:T(8,128)(2,1)} fusion(bf16[2048,1024]{0,1:T(8,128)(2,1)} %copy.15, bf16[1024,256]{1,0:T(8,128)(2,1)S(1)} %convolution_convert_fusion, bf16[2048,256]{1,0:T(8,128)(2,1)S(1)} %copy-done.4), kind=kOutput, calls=%fused_computation.8 | convolution fusion | flops 1080033280 | bytes 9961472 | tf_op jit(solution)/shard_map/dot_general | solution.py:39
  173.2 6.4 %copy.37 = bf16[2048,1024]{1,0:T(8,128)(2,1)} copy(bf16[2048,1024]{0,1:T(8,128)(2,1)} %fusion) | data formatting | bytes 8388608
  179.5 18.7 %gather_fusion = bf16[3072,1024]{1,0:T(8,128)(2,1)} fusion(bf16[2048,1024]{1,0:T(8,128)(2,1)} %copy.37, s32[3072]{0:T(1024)S(1)} %broadcast_clamp_fusion), kind=kCustom, calls=%fused_computation | custom fusion | bytes 12595200 | tf_op jit(solution)/shard_map/jit(_take)/gather | solution.py:48
  198.2 4.1 %broadcast_select_fusion = bf16[3072,1024]{1,0:T(8,128)(2,1)S(1)} fusion(bf16[3072,1024]{1,0:T(8,128)(2,1)} %gather_fusion, pred[3072]{0:T(1024)(128)(4,1)S(1)} %compare_and_fusion.1), kind=kLoop, calls=%fused_computation.36 | loop fusion | flops 3145728 | bytes 12585984 | tf_op jit(solution)/shard_map/jit(_take)/select_n | solution.py:48
  202.3 0.8 collective-permute-start
  203.1 6.2 %collective-permute-start.1 = (bf16[4,24,1024]{2,1,0:T(8,128)(2,1)S(1)}, bf16[4,24,1024]{2,1,0:T(8,128)(2,1)S(1)}, u32[]{:S(2)}, u32[]{:S(2)}) collective-permute-start(bf16[4,24,1024]{2,1,0:T(8,128)(2,1)S(1)} %bitcast.68), channel_id=1, source_target_pairs={{2,0},{4,2},{6,4},{8,6},{10,8},{12,10},{14,12},{16,14},{18,16},{20... | collective-permute-start | bytes 589832 | tf_op jit(solution)/shard_map/ppermute | solution.py:19
  210.0 2.3 collective-permute-done
  212.3 4.3 %fusion.12 = f32[128,16,1024]{2,1,0:T(8,128)} fusion(bf16[128,16,24]{2,1,0:T(8,128)(2,1)S(1)} %copy.23, bf16[4,24,1024]{2,1,0:T(8,128)(2,1)S(1)} %collective-permute-done, bf16[128,24,1024]{2,1,0:T(8,128)(2,1)S(1)} %broadcast_select_fusion.1), kind=kOutput, calls=%fused_computation.19 | convolution fusion | flops 103809024 | bytes 14974976 | tf_op jit(solution)/shard_map/aij,ajn->ain/dot_general | solution.py:60
  216.6 4.3 %fusion.15 = f32[128,16,1024]{2,1,0:T(8,128)} fusion(bf16[128,16,24]{2,1,0:T(8,128)(2,1)S(1)} %copy-done.5, bf16[4,24,1024]{2,1,0:T(8,128)(2,1)S(1)} %collective-permute-done, bf16[128,24,1024]{2,1,0:T(8,128)(2,1)S(1)} %broadcast_select_fusion.1), kind=kOutput, calls=%fused_computation.21 | convolution fusion | flops 103809024 | bytes 14974976 | tf_op jit(solution)/shard_map/aij,ajn->ain/dot_general | solution.py:60
  220.9 4.3 %fusion.18 = f32[128,16,1024]{2,1,0:T(8,128)} fusion(bf16[128,16,24]{2,1,0:T(8,128)(2,1)S(1)} %copy-done.6, bf16[4,24,1024]{2,1,0:T(8,128)(2,1)S(1)} %collective-permute-done, bf16[128,24,1024]{2,1,0:T(8,128)(2,1)S(1)} %broadcast_select_fusion.1), kind=kOutput, calls=%fused_computation.23 | convolution fusion | flops 103809024 | bytes 14974976 | tf_op jit(solution)/shard_map/aij,ajn->ain/dot_general | solution.py:60
  225.2 4.3 %fusion.25 = f32[128,16,1024]{2,1,0:T(8,128)} fusion(bf16[128,16,24]{2,1,0:T(8,128)(2,1)S(1)} %copy.25, bf16[128,24,1024]{2,1,0:T(8,128)(2,1)S(1)} %broadcast_select_fusion.1, bf16[4,24,1024]{2,1,0:T(8,128)(2,1)S(1)} %collective-permute-done), kind=kOutput, calls=%fused_computation.31 | convolution fusion | flops 103809024 | bytes 14974976 | tf_op jit(solution)/shard_map/aij,ajn->ain/dot_general | solution.py:60
  229.5 4.3 %fusion.6 = f32[128,16,1024]{2,1,0:T(8,128)} fusion(bf16[128,16,24]{2,1,0:T(8,128)(2,1)S(1)} %copy-done.7, bf16[4,24,1024]{2,1,0:T(8,128)(2,1)S(1)} %collective-permute-done.1, bf16[128,24,1024]{2,1,0:T(8,128)(2,1)S(1)} %broadcast_select_fusion.1), kind=kOutput, calls=%fused_computation.15 | convolution fusion | flops 103809024 | bytes 14974976 | tf_op jit(solution)/shard_map/aij,ajn->ain/dot_general | solution.py:60
  233.8 4.3 %fusion.9 = f32[128,16,1024]{2,1,0:T(8,128)} fusion(bf16[128,16,24]{2,1,0:T(8,128)(2,1)S(1)} %copy-done.8, bf16[4,24,1024]{2,1,0:T(8,128)(2,1)S(1)} %collective-permute-done.1, bf16[128,24,1024]{2,1,0:T(8,128)(2,1)S(1)} %broadcast_select_fusion.1), kind=kOutput, calls=%fused_computation.17 | convolution fusion | flops 103809024 | bytes 14974976 | tf_op jit(solution)/shard_map/aij,ajn->ain/dot_general | solution.py:60
  238.1 4.3 %fusion.3 = f32[128,16,1024]{2,1,0:T(8,128)} fusion(bf16[128,16,24]{2,1,0:T(8,128)(2,1)S(1)} %copy-done.9, bf16[4,24,1024]{2,1,0:T(8,128)(2,1)S(1)} %collective-permute-done.1, bf16[128,24,1024]{2,1,0:T(8,128)(2,1)S(1)} %broadcast_select_fusion.1), kind=kOutput, calls=%fused_computation.13 | convolution fusion | flops 103809024 | bytes 14974976 | tf_op jit(solution)/shard_map/aij,ajn->ain/dot_general | solution.py:60
  242.4 4.3 %fusion.20 = f32[128,16,1024]{2,1,0:T(8,128)} fusion(bf16[128,16,24]{2,1,0:T(8,128)(2,1)S(1)} %copy.35, bf16[4,24,1024]{2,1,0:T(8,128)(2,1)S(1)} %collective-permute-done.1, bf16[128,24,1024]{2,1,0:T(8,128)(2,1)S(1)} %broadcast_select_fusion.1), kind=kOutput, calls=%fused_computation.25 | convolution fusion | flops 103809024 | bytes 14974976 | tf_op jit(solution)/shard_map/aij,ajn->ain/dot_general | solution.py:60
  246.7 46.4 %fusion.37 = bf16[128,16,16]{2,1,0:T(8,128)(2,1)S(1)} fusion(f32[128,16,1024]{2,1,0:T(8,128)} %fusion.20, f32[128,16,1024]{2,1,0:T(8,128)} %fusion.3, f32[128,16,1024]{2,1,0:T(8,128)} %fusion.9, f32[128,16,1024]{2,1,0:T(8,128)} %fusion.6, f32[128,16,1024]{2,1,0:T(8,128)} %fusion.25, f32[128,16,1024]{2,1,0:T(8,128)} %fusion.12, ...), kind=kOutput, calls=%fused_computation.46 | convolution fusion | flops 316702720 | bytes 73576448 | tf_op jit(solution)/shard_map/ain,ajn->aij/dot_general | solution.py:70
  293.0 1.1 copy.36
  294.1 20.5 %all-reduce.5.cloned.1.call-done = bf16[128,256]{0,1:T(8,128)(2,1)} async-done(((bf16[128,256]{0,1:T(8,128)(2,1)}), bf16[128,256]{0,1:T(8,128)(2,1)}) %all-reduce.5.cloned.1.call-update) | async-done | bytes 65552 | tf_op jit(solution)/shard_map/psum | solution.py:74
  314.6 0.9 dynamic-slice_convert_fusion
  (68 shorter events, 6.6 us)
Async XLA Ops:
  7.2 157.5 %copy-start = (f32[256,256]{1,0:T(8,128)S(1)}, f32[256,256]{1,0:T(8,128)}, u32[]{:S(2)}) copy-start(f32[256,256]{1,0:T(8,128)} %param.11) | copy-start | bytes 786436
  7.2 21.5 %all-gather.2.cloned.1.call-start = ((), (), s32[]{:S(2)}) async-start(), calls=%async_computation | async-start | bytes 1572864 | tf_op jit(solution)/shard_map/all_gather | solution.py:35
  7.9 156.8 %all-reduce.3.cloned.1.call-start = ((), (), s32[]{:S(2)}) async-start(), calls=%async_computation.1 | async-start | bytes 2097152 | tf_op jit(solution)/shard_map/psum | solution.py:37
  13.7 14.8 %copy-start.11 = (f32[1024]{0:T(1024)S(1)}, f32[1024]{0:T(1024)}, u32[]{:S(2)}) copy-start(f32[1024]{0:T(1024)} %param.17) | copy-start | bytes 12292
  13.7 14.8 %copy-start.12 = (s32[1024]{0:T(1024)S(1)}, s32[1024]{0:T(1024)}, u32[]{:S(2)}) copy-start(s32[1024]{0:T(1024)} %param.16) | copy-start | bytes 12292
  13.7 14.8 %copy-start.10 = (s32[1,128]{1,0:T(1,128)S(1)}, s32[1,128]{1,0:T(1,128)}, u32[]{:S(2)}) copy-start(s32[1,128]{1,0:T(1,128)} %param.12) | copy-start | bytes 1540
  24.8 8.9 %copy-start.13 = (s32[128]{0:T(128)S(1)}, s32[128]{0:T(128)}, u32[]{:S(2)}) copy-start(s32[128]{0:T(128)} %param.13) | copy-start | bytes 1540
  28.7 139.0 %copy-start.4 = (bf16[2048,256]{1,0:T(8,128)(2,1)S(1)}, bf16[2048,256]{1,0:T(8,128)(2,1)}, u32[]{:S(2)}) copy-start(bf16[2048,256]{1,0:T(8,128)(2,1)} %all-gather.2.cloned.1.call-done) | copy-start | bytes 3145732
  33.6 281.0 %all-reduce.5.cloned.1.call-start = ((), (), s32[]{:S(2)}) async-start(), calls=%async_computation.2 | async-start | bytes 131072 | tf_op jit(solution)/shard_map/psum | solution.py:74
  198.2 11.1 %copy-start.3 = (bf16[3072,1024]{1,0:T(8,128)(2,1)S(1)}, bf16[3072,1024]{1,0:T(8,128)(2,1)}, u32[]{:S(2)}) copy-start(bf16[3072,1024]{1,0:T(8,128)(2,1)} %gather_fusion) | copy-start | bytes 18874372
  202.3 10.0 %collective-permute-start = (bf16[4,24,1024]{2,1,0:T(8,128)(2,1)S(1)}, bf16[4,24,1024]{2,1,0:T(8,128)(2,1)S(1)}, u32[]{:S(2)}, u32[]{:S(2)}) collective-permute-start(bf16[4,24,1024]{2,1,0:T(8,128)(2,1)S(1)} %bitcast.69), channel_id=1, source_target_pairs={{0,2},{2,4},{4,6},{6,8},{8,10},{10,12},{12,14},{14,16},{16,18},{18... | collective-permute-start | bytes 589832 | tf_op jit(solution)/shard_map/ppermute | solution.py:18
  203.1 26.4 %collective-permute-start.1 = (bf16[4,24,1024]{2,1,0:T(8,128)(2,1)S(1)}, bf16[4,24,1024]{2,1,0:T(8,128)(2,1)S(1)}, u32[]{:S(2)}, u32[]{:S(2)}) collective-permute-start(bf16[4,24,1024]{2,1,0:T(8,128)(2,1)S(1)} %bitcast.68), channel_id=1, source_target_pairs={{2,0},{4,2},{6,4},{8,6},{10,8},{12,10},{14,12},{16,14},{18,16},{20... | collective-permute-start | bytes 589832 | tf_op jit(solution)/shard_map/ppermute | solution.py:19
  210.0 32.4 %copy-start.2 = (bf16[128,24,1024]{2,1,0:T(8,128)(2,1)}, bf16[128,24,1024]{2,1,0:T(8,128)(2,1)S(1)}, u32[]{:S(2)}) copy-start(bf16[128,24,1024]{2,1,0:T(8,128)(2,1)S(1)} %broadcast_select_fusion.1) | copy-start | bytes 18874372
  210.0 6.6 %copy-start.5 = (bf16[128,16,24]{2,1,0:T(8,128)(2,1)S(1)}, bf16[128,16,24]{2,1,0:T(8,128)(2,1)}, u32[]{:S(2)}) copy-start(bf16[128,16,24]{2,1,0:T(8,128)(2,1)} %copy.19) | copy-start | bytes 294916
  216.6 4.3 %copy-start.6 = (bf16[128,16,24]{2,1,0:T(8,128)(2,1)S(1)}, bf16[128,16,24]{2,1,0:T(8,128)(2,1)}, u32[]{:S(2)}) copy-start(bf16[128,16,24]{2,1,0:T(8,128)(2,1)} %copy.21) | copy-start | bytes 294916
  225.2 4.3 %copy-start.7 = (bf16[128,16,24]{2,1,0:T(8,128)(2,1)S(1)}, bf16[128,16,24]{2,1,0:T(8,128)(2,1)}, u32[]{:S(2)}) copy-start(bf16[128,16,24]{2,1,0:T(8,128)(2,1)} %copy.29) | copy-start | bytes 294916
  229.5 4.3 %copy-start.8 = (bf16[128,16,24]{2,1,0:T(8,128)(2,1)S(1)}, bf16[128,16,24]{2,1,0:T(8,128)(2,1)}, u32[]{:S(2)}) copy-start(bf16[128,16,24]{2,1,0:T(8,128)(2,1)} %copy.31) | copy-start | bytes 294916
  233.8 4.3 %copy-start.9 = (bf16[128,16,24]{2,1,0:T(8,128)(2,1)S(1)}, bf16[128,16,24]{2,1,0:T(8,128)(2,1)}, u32[]{:S(2)}) copy-start(bf16[128,16,24]{2,1,0:T(8,128)(2,1)} %copy.33) | copy-start | bytes 294916
  246.7 69.6 %copy-start.1 = (f32[256,256]{1,0:T(8,128)S(1)}, f32[256,256]{1,0:T(8,128)}, u32[]{:S(2)}) copy-start(f32[256,256]{1,0:T(8,128)} %param.11) | copy-start | bytes 786436
Sparse Core Ops, SparseCore 0:
  9.7 15.3 all-gather.1
  33.7 130.9 all-reduce.2
  294.2 20.3 all-reduce.4
where the time goes:
time: 323 us
  waiting for transfers between devices  154 us (48%)
  matrix products  94 us (29%)
  local copies, waits for them, and re-layouts  44.5 us (14%)
  between operations  14.1 us (4%)
  other arithmetic  8.7 us (3%)
  starting transfers between devices  7.08 us (2%)
    psum x1, waiting for transfers between devices, local(): inner_products = lax.psum(inner_products, 'row')  131 us
    dot_general x1, matrix products, local(): jnp.einsum('ain,ajn->aij', weighted, rounded, preferred_element_type=jnp....  46.4 us
    dot_general x8, matrix products, local(): jnp.einsum('aij,ajn->ain', blocks, neighbours, preferred_element_type=jnp...  34.3 us
    psum x1, waiting for transfers between devices, local(): lax.psum(partial_value.astype(jnp.bfloat16), 'col').astype(jnp.float32)  20.5 us
    gather x1, local copies, waits for them, and re-layouts, local(): jnp.take(vectors, row_index.reshape(-1), axis=0, mode='fill', fill_value=0)  18.7 us
    unnamed x40, local copies, waits for them, and re-layouts  14.7 us
    select_n x9, local copies, waits for them, and re-layouts, local(): jnp.where(block_present[:, relative, None, None] > 0, blocks, jnp.zeros_l...  7.69 us
  transfers between devices with their start and end apart: 5, of which 3 were waited for; matrix products, arithmetic and copies ran while one was open for 12% of the time, Pallas kernels for 0%

commit v1 on v0

v1 whole, which is shorter than its diff:
```python
import functools

import jax
import jax.numpy as jnp
from jax import lax
from jax.experimental import pallas as pl
from jax.experimental.pallas import tpu as pltpu
from jax.sharding import PartitionSpec as P

NPMAX = 16
BMAX = 24
K = 9
RIM = 4
EDGE = RIM * BMAX
GROUP = 16
SPAN = GROUP + 2 * RIM
WIDE = 640
ALIGN = 64
MIB = 1024 * 1024

VM = pltpu.MemorySpace.VMEM
SM = pltpu.MemorySpace.SMEM
NT = (((1,), (1,)), ((), ()))
NN = (((1,), (0,)), ((), ()))


def dot(a, b, dims=NN, **kw):
    return lax.dot_general(a, b, dims, preferred_element_type=jnp.float32, **kw)


def iota(shape, dim):
    return lax.broadcasted_iota(jnp.int32, shape, dim)


def padded_rows(counts_ref, first_atom, first_row, base_row, sources):
    depth = sources[0].shape[0]
    slot = iota((EDGE, 1), 0)
    target = jnp.full((EDGE, 1), -1, jnp.int32)
    row = first_row - base_row
    for t in range(RIM):
        count = counts_ref[first_atom + t]
        u = slot - t * BMAX
        target = jnp.where((u >= 0) & (u < count), row + u, target)
        row = row + count
    pick = (iota((EDGE, depth), 1) == target).astype(jnp.float32).astype(jnp.bfloat16)
    return [dot(pick, s).astype(jnp.bfloat16) for s in sources]


def halo_kernel(counts_ref, v_top, v_end, own_top, own_end, other_top, other_end, to_next, to_last):
    atoms = counts_ref.shape[0]
    rows = EDGE + 32
    tail = counts_ref[atoms - 1]
    for t in range(1, RIM):
        tail = tail + counts_ref[atoms - 1 - t]
    cols = v_top.shape[1]
    half = own_top.shape[1]
    last = padded_rows(
        counts_ref, atoms - RIM, rows - tail, 0, [v_end[...], own_end[...], other_end[...]]
    )
    first = padded_rows(counts_ref, 0, 0, 0, [v_top[...], own_top[...], other_top[...]])
    for out, pieces in ((to_next, last), (to_last, first)):
        out[:, :cols] = pieces[0]
        out[:, cols : cols + half] = pieces[1]
        out[:, cols + half :] = pieces[2]


def band_kernel(counts_ref, cm_ref, band_ref, start_ref, pos_ref, cp_ref):
    atoms = counts_ref.shape[0]
    groups = atoms // GROUP
    rows = groups * 256
    for t in range(RIM):
        pos_ref[t] = t * BMAX
        pos_ref[RIM + atoms + t] = EDGE + rows + t * BMAX

    def add(t, at):
        pos_ref[RIM + t] = at
        return at + counts_ref[t]

    lax.fori_loop(0, atoms, add, jnp.int32(EDGE))
    lane = iota((8, WIDE), 1)
    which = lane // BMAX
    slot = lane - which * BMAX
    sub = iota((GROUP, NPMAX * BMAX), 1) // BMAX
    for g in range(groups):
        first = pos_ref[g * GROUP]
        start = jnp.minimum((first // ALIGN) * ALIGN, rows + 2 * EDGE - WIDE)
        start_ref[g] = start
        target = jnp.full((8, WIDE), -1, jnp.int32)
        for t in range(SPAN):
            atom = g * GROUP + t - RIM
            count = counts_ref[atom] if 0 <= atom < atoms else BMAX
            at = pos_ref[atom + RIM] - start
            target = jnp.where((which == t) & (slot < count), at + slot, target)
        pick = (iota((WIDE, WIDE), 0) == target[:1]).astype(jnp.float32).astype(jnp.bfloat16)
        x = [cm_ref[k, g * GROUP : (g + 1) * GROUP, :].astype(jnp.float32) for k in range(K)]
        x += [None] * (NPMAX - K)
        lanes = NPMAX * BMAX
        for bit in (1, 2, 4, 8):
            low = (sub // bit) % 2 == 0
            new = list(x)
            for p in range(NPMAX):
                q = p + bit
                if p & bit or (x[p] is None and x[q] is None):
                    continue
                a, b = x[p], x[q]
                zero = jnp.zeros((GROUP, lanes), jnp.float32)
                b_up = zero if b is None else pltpu.roll(b, bit * BMAX, 1)
                a_down = zero if a is None else pltpu.roll(a, lanes - bit * BMAX, 1)
                new[p] = jnp.where(low, zero if a is None else a, b_up)
                new[q] = jnp.where(low, a_down, zero if b is None else b)
            x = new
        pad = jnp.zeros((GROUP, WIDE - lanes), jnp.float32)
        for i in range(NPMAX):
            wide = jnp.concatenate([x[i], pad], axis=1)
            halves = [wide[:8], pltpu.roll(wide[8:], 8 * BMAX, 1)]
            for _ in range(2):
                halves = [pltpu.roll(h, 0, 1, stride=BMAX // 2, stride_axis=0) for h in halves]
            skew = jnp.concatenate(halves, axis=0)
            cp_ref[i * GROUP : (i + 1) * GROUP, :] = skew.astype(jnp.bfloat16)
        band_ref[g] = dot(cp_ref[...], pick, NT).astype(jnp.bfloat16)


def inner_kernel(own_ref, other_ref, v_ref, out_ref, pt_ref):
    half = own_ref.shape[1]

    @pl.when(pl.program_id(0) == 0)
    def _():
        pt_ref[:half, :] = own_ref[...].T
        pt_ref[half:, :] = other_ref[...].T

    out_ref[...] = dot(pt_ref[...], v_ref[...]).T


def mix_kernel(parts_ref, factor_ref, out_ref):
    total = jnp.sum(parts_ref[...], axis=0)
    mixed = dot(total, factor_ref[...], precision=lax.Precision.HIGHEST).astype(jnp.bfloat16)
    out_ref[...] = jnp.broadcast_to(mixed[None], out_ref.shape)


def main_kernel(
    col_ref,
    start_ref,
    mix_ref,
    before_ref,
    after_ref,
    weight_ref,
    own_ref,
    other_ref,
    v_hbm,
    band_hbm,
    vectors_hbm,
    own_out,
    other_out,
    v_ref,
    band_ref,
    e_ref,
    v_sem,
    band_sem,
    out_sem,
):
    rows, cols = v_hbm.shape
    blocks = rows // 256
    groups = band_ref.shape[0]
    v_copies, out_copies = [], []
    for b in range(blocks):
        at = pl.ds(b * 256, 256)
        v_copies.append(pltpu.make_async_copy(v_hbm.at[at], v_ref.at[at], v_sem.at[b]))
        out_copies.append(
            pltpu.make_async_copy(
                e_ref.at[pl.ds(EDGE + b * 256, 256)], vectors_hbm.at[at], out_sem.at[b]
            )
        )
        v_copies[-1].start()
    band_copy = pltpu.make_async_copy(band_hbm, band_ref, band_sem)
    band_copy.start()
    mix = mix_ref[...]

    def rotated(vectors, panel):
        return (vectors.astype(jnp.float32) - dot(panel, mix, NT)).astype(jnp.bfloat16)

    e_ref[:EDGE, :] = rotated(before_ref[:, :cols], before_ref[:, cols:])
    e_ref[EDGE + rows :, :] = rotated(after_ref[:, :cols], after_ref[:, cols:])
    for b in range(blocks):
        v_copies[b].wait()
        at = slice(b * 256, (b + 1) * 256)
        panel = jnp.concatenate([own_ref[at, :], other_ref[at, :]], axis=1)
        e_ref[EDGE + b * 256 : EDGE + (b + 1) * 256, :] = rotated(v_ref[at, :], panel)
        out_copies[b].start()
    band_copy.wait()
    weight = weight_ref[...]
    down, along = iota((256, 256), 0), iota((256, 256), 1)
    same_atom = (down % GROUP) == (along % GROUP)
    spread = ((down // GROUP) == (along % NPMAX)).astype(jnp.float32).astype(jnp.bfloat16)
    same_i = (down // GROUP) == (along // NPMAX)
    per = groups // 2
    col = col_ref[0]
    for turn in range(2):
        out = other_out if turn == 0 else own_out
        side = (1 - col) if turn == 0 else col
        for step in range(per):
            g = side * per + step
            window = e_ref[pl.ds(pl.multiple_of(start_ref[g], ALIGN), WIDE), :]
            rounded = dot(band_ref[g], window).astype(jnp.bfloat16)
            weighted = (rounded.astype(jnp.float32) * weight).astype(jnp.bfloat16)
            pairs = jnp.where(same_atom, dot(weighted, rounded, NT), 0.0)
            high = pairs.astype(jnp.bfloat16)
            low = (pairs - high.astype(jnp.float32)).astype(jnp.bfloat16)
            spreaded = jnp.where(same_i, dot(high, spread) + dot(low, spread), 0.0)
            total = spreaded[:GROUP]
            for i in range(1, NPMAX):
                total = total + spreaded[i * GROUP : (i + 1) * GROUP]
            out[step * GROUP : (step + 1) * GROUP, :] = total
    for c in out_copies:
        c.wait()


def call(kernel, out_shape, in_specs, out_specs, flops, nbytes, mib, **kw):
    return pl.pallas_call(
        kernel,
        out_shape=out_shape,
        in_specs=in_specs,
        out_specs=out_specs,
        compiler_params=pltpu.CompilerParams(vmem_limit_bytes=mib * MIB),
        cost_estimate=pl.CostEstimate(flops=flops, bytes_accessed=nbytes, transcendentals=0),
        **kw,
    )


def local(
    vectors_in, panel, factor, atom_basis, proj_count, coupling, block_present, occ_mask, occ_weight
):
    rows, cols = vectors_in.shape
    half = panel.shape[1]
    npan = 2 * half
    counts = atom_basis[0]
    atoms = counts.shape[0]
    groups = atoms // GROUP
    n_row = lax.axis_size("row")
    n_col = lax.axis_size("col")
    col = lax.axis_index("col")
    vmem = pl.BlockSpec(memory_space=VM)
    smem = pl.BlockSpec(memory_space=SM)
    hbm = pl.BlockSpec(memory_space=pltpu.MemorySpace.HBM)
    bf16, f32 = jnp.bfloat16, jnp.float32

    other = lax.ppermute(panel, "col", [(0, 1), (1, 0)])

    tile = 256
    partial = pl.pallas_call(
        inner_kernel,
        out_shape=jax.ShapeDtypeStruct((cols, npan), f32),
        grid=(cols // tile,),
        in_specs=[
            pl.BlockSpec((rows, half), lambda c: (0, 0)),
            pl.BlockSpec((rows, half), lambda c: (0, 0)),
            pl.BlockSpec((rows, tile), lambda c: (0, c)),
        ],
        out_specs=pl.BlockSpec((tile, npan), lambda c: (c, 0)),
        scratch_shapes=[pltpu.VMEM((npan, rows), bf16)],
        compiler_params=pltpu.CompilerParams(vmem_limit_bytes=16 * MIB),
        cost_estimate=pl.CostEstimate(
            flops=2 * rows * cols * npan, bytes_accessed=6 << 20, transcendentals=0
        ),
    )(panel, other, vectors_in)
    slices = lax.all_to_all(partial, "row", 0, 0, tiled=True)
    slices = slices.reshape(n_row, cols // n_row, npan)
    flipped = jnp.roll(jnp.roll(factor, half, axis=0), half, axis=1)
    ordered = jnp.where(col == 0, factor, flipped)
    copies = call(
        mix_kernel,
        jax.ShapeDtypeStruct((n_row, cols // n_row, npan), bf16),
        [vmem, vmem],
        vmem,
        1 << 24,
        2 << 20,
        8,
    )(slices, ordered)
    mixing = lax.all_to_all(copies.reshape(cols, npan), "row", 0, 0, tiled=True)

    edge = EDGE + 32
    to_next, to_last = call(
        halo_kernel,
        [jax.ShapeDtypeStruct((EDGE, cols + npan), bf16)] * 2,
        [smem] + [vmem] * 6,
        [vmem, vmem],
        1 << 26,
        2 << 20,
        8,
    )(
        counts,
        vectors_in[:edge],
        vectors_in[rows - edge :],
        panel[:edge],
        panel[rows - edge :],
        other[:edge],
        other[rows - edge :],
    )
    up = [(i, (i + 1) % n_row) for i in range(n_row)]
    before = lax.ppermute(to_next, "row", up)
    after = lax.ppermute(to_last, "row", [(j, i) for i, j in up])

    which = jnp.arange(NPMAX * BMAX, dtype=jnp.int32) // BMAX
    keep = (block_present.T[:, :, None] > 0) & (which[None, None, :] < proj_count[None, :, None])
    blocks = coupling.transpose(1, 0, 2)
    blocks = jnp.where(keep, blocks, jnp.zeros_like(blocks))
    band, starts = call(
        band_kernel,
        [
            jax.ShapeDtypeStruct((groups, 256, WIDE), bf16),
            jax.ShapeDtypeStruct((groups,), jnp.int32),
        ],
        [smem, vmem],
        [vmem, smem],
        groups * 2 * 256 * WIDE * WIDE,
        4 << 20,
        16,
        scratch_shapes=[pltpu.SMEM((atoms + 2 * RIM,), jnp.int32), pltpu.VMEM((256, WIDE), bf16)],
    )(counts, blocks)

    weights = (occ_mask.astype(f32) * occ_weight / (cols * n_col))[None, :]
    vectors, own_part, other_part = call(
        main_kernel,
        [
            jax.ShapeDtypeStruct((rows, cols), bf16),
            jax.ShapeDtypeStruct((atoms // 2, 256), f32),
            jax.ShapeDtypeStruct((atoms // 2, 256), f32),
        ],
        [smem, smem] + [vmem] * 6 + [hbm] * 2,
        [hbm, vmem, vmem],
        10 << 30,
        14 << 20,
        50,
        scratch_shapes=[
            pltpu.VMEM((rows, cols), bf16),
            pltpu.VMEM((groups, 256, WIDE), bf16),
            pltpu.VMEM((rows + 2 * EDGE, cols), bf16),
            pltpu.SemaphoreType.DMA((rows // 256,)),
            pltpu.SemaphoreType.DMA,
            pltpu.SemaphoreType.DMA((rows // 256,)),
        ],
    )(col[None], starts, mixing, before, after, weights, panel, other, vectors_in, band)
    density = own_part + lax.ppermute(other_part, "col", [(0, 1), (1, 0)])
    return vectors, density


def solution(mesh):
    placed = (
        P("row", "col"),
        P("row", "col"),
        P(),
        P("row", None),
        P("row"),
        P("row", None, None),
        P("row", None),
        P("col"),
        P("col"),
    )
    return jax.shard_map(
        local,
        mesh=mesh,
        in_specs=placed,
        out_specs=(P("row", "col"), P(("row", "col"), None)),
        check_vma=False,
    )
```

time: 323 us -> 93.6 us (0.29)
  waiting for transfers between devices: 154 us -> 16.5 us
  matrix products: 94 us -> 0 us
  Pallas kernels: 0 us -> 37.7 us
  local copies, waits for them, and re-layouts: 44.5 us -> 7.6 us
  starting transfers between devices: 7.08 us -> 26.8 us
  between operations: 14.1 us -> 0.81 us
  other arithmetic: 8.7 us -> 3.66 us
    psum x2 -> x0, waiting for transfers between devices: 151 us -> none  [the longest x1 131 us: local(): inner_products = lax.psum(inner_products, 'row')]
    dot_general x12 -> x0, matrix products: 94 us -> none  [the longest x1 46.4 us: local(): jnp.einsum('ain,ajn->aij', weighted, rounded, preferred_element_type=jnp....]
    pallas_call x0 -> x5, Pallas kernels: none -> 37.7 us  [the longest x1 20 us: local(): call(band_kernel, [jax.ShapeDtypeStruct((groups, 256, WIDE), bf16), jax.S...]
    gather x1 -> x0, local copies, waits for them, and re-layouts: 18.7 us -> none  [local(): jnp.take(vectors, row_index.reshape(-1), axis=0, mode='fill', fill_value=0)]
    all_to_all x0 -> x2, starting transfers between devices: none -> 16.3 us  [the longest x1 11.2 us: local(): slices = lax.all_to_all(partial, 'row', 0, 0, tiled=True)]
    all_to_all x0 -> x2, waiting for transfers between devices: none -> 15.6 us  [the longest x1 15.6 us: local(): slices = lax.all_to_all(partial, 'row', 0, 0, tiled=True)]
    unnamed x40 -> x20, local copies, waits for them, and re-layouts: 14.7 us -> 4.75 us
    select_n x11 -> x0, local copies, waits for them, and re-layouts: 7.88 us -> none  [the longest x9 7.69 us: local(): jnp.where(block_present[:, relative, None, None] > 0, blocks, jnp.zeros_l...]
  transfers between devices with their start and end apart: 5 -> 6, of which waited for: 3 -> 2; matrix products, arithmetic and copies ran while one was open for 12% -> 6% of each run, Pallas kernels for 0% -> 22%
where the time goes in v1:
time: 93.6 us; the launch traced here: 93.1 us
  Pallas kernels  37.7 us (40%)
  starting transfers between devices  26.8 us (29%)
  waiting for transfers between devices  16.5 us (18%)
  local copies, waits for them, and re-layouts  7.6 us (8%)
  other arithmetic  3.66 us (4%)
    pallas_call x1, Pallas kernels, local(): call(band_kernel, [jax.ShapeDtypeStruct((groups, 256, WIDE), bf16), jax.S...  20 us
    all_to_all x1, waiting for transfers between devices, local(): slices = lax.all_to_all(partial, 'row', 0, 0, tiled=True)  15.6 us
    pallas_call x1, Pallas kernels, local(): call(main_kernel, [jax.ShapeDtypeStruct((rows, cols), bf16), jax.ShapeDty...  12 us
    all_to_all x1, starting transfers between devices, local(): slices = lax.all_to_all(partial, 'row', 0, 0, tiled=True)  11.2 us
    ppermute x1, starting transfers between devices, local(): after = lax.ppermute(to_last, 'row', [(j, i) for i, j in up])  5.89 us
    all_to_all x1, starting transfers between devices, local(): mixing = lax.all_to_all(copies.reshape(cols, npan), 'row', 0, 0, tiled=True)  5.04 us
    unnamed x20, local copies, waits for them, and re-layouts  4.75 us
    pallas_call x1, Pallas kernels, local(): pl.pallas_call(inner_kernel, out_shape=jax.ShapeDtypeStruct((cols, npan),...  3.7 us
  transfers between devices with their start and end apart: 6, of which 2 were waited for; matrix products, arithmetic and copies ran while one was open for 6% of the time, Pallas kernels for 22%

profile of v1, /device:TPU:1, one launch (start us, length us, event | category | flops | bytes accessed | tf_op | source)
XLA Modules:
  0.0 93.1 jit_solution(9206645439001710122)
XLA Ops:
  0.6 1.5 %collective-permute-start = (bf16[2048,128]{1,0:T(8,128)(2,1)}, bf16[2048,128]{1,0:T(8,128)(2,1)S(1)}, u32[]{:S(2)}, u32[]{:S(2)}) collective-permute-start(bf16[2048,128]{1,0:T(8,128)(2,1)} %own_ref.3), channel_id=1, source_target_pairs={{0,1},{1,0},{2,3},{3,2},{4,5},{5,4},{6,7},{7,6},{8,9},{9,8},{10,11... | collective-permute-start | bytes 1572872 | tf_op jit(solution)/shard_map/ppermute | solution.py:246
  2.1 0.7 compare_bitcast_fusion
  2.8 0.7 broadcast_compare_fusion
  3.6 1.0 %fusion.9 = (f32[128,256]{1,0:T(8,128)S(1)}, f32[128,256]{1,0:T(8,128)S(1)}) fusion(f32[256,256]{1,0:T(8,128)} %param.11), kind=kLoop, calls=%fused_computation.20 | loop fusion | bytes 524288 | tf_op jit(solution)/shard_map/jit(_roll_static)/slice | solution.py:267
  4.6 0.0 collective-permute-done.other_ref
  4.6 0.0 copy-start
  4.6 2.2 %copy-done = bf16[2048,1024]{1,0:T(8,128)(2,1)S(1)} copy-done((bf16[2048,1024]{1,0:T(8,128)(2,1)S(1)}, bf16[2048,1024]{1,0:T(8,128)(2,1)}, u32[]{:S(2)}) %copy-start) | copy-done | bytes 4194328
  6.8 1.0 %copy-done.1 = bf16[2048,128]{1,0:T(8,128)(2,1)S(1)} copy-done((bf16[2048,128]{1,0:T(8,128)(2,1)S(1)}, bf16[2048,128]{1,0:T(8,128)(2,1)}, u32[]{:S(2)}) %copy-start.1) | copy-done | bytes 524312
  7.8 3.7 %shard_map.105 = f32[1024,256]{1,0:T(8,128)} custom-call(bf16[2048,128]{1,0:T(8,128)(2,1)S(1)} %copy-done.1, bf16[2048,128]{1,0:T(8,128)(2,1)S(1)} %collective-permute-done.other_ref, bf16[2048,1024]{1,0:T(8,128)(2,1)S(1)} %copy-done), custom_call_target="tpu_custom_call" | custom-call | flops 1073741824 | bytes 6291456 | tf_op jit(solution)/shard_map/pallas_call | solution.py:249
  11.5 0.0 copy-done.3
  11.5 11.2 %all-to-all-start = ((f32[64,16,256]{2,1,0:T(8,128)}), f32[64,16,256]{2,1,0:T(8,128)S(1)}, u32[]{:S(2)}, u32[]{:S(2)}) async-start(f32[64,16,256]{2,1,0:T(8,128)} %bitcast.4), calls=%async_computation | async-start | bytes 2097152 | tf_op jit(solution)/shard_map/all_to_all | solution.py:265
  22.8 0.0 copy-start.5
  22.8 0.0 copy-done.2
  22.8 0.0 copy-done.7
  22.9 1.1 %fusion.6 = (bf16[128,1024]{1,0:T(8,128)(2,1)S(1)}, bf16[128,1024]{1,0:T(8,128)(2,1)S(1)}) fusion(bf16[2048,1024]{1,0:T(8,128)(2,1)} %v_hbm.1), kind=kLoop, calls=%fused_computation.17 | loop fusion | bytes 1048576 | tf_op jit(solution)/shard_map/slice | solution.py:292
  24.0 1.5 %and_select_fusion.cm_ref = bf16[9,128,384]{2,1,0:T(8,128)(2,1)S(1)} fusion(bf16[128,9,384]{2,0,1:T(8,128)(2,1)} %param.14, pred[128,384]{1,0:T(8,128)(4,1)S(1)} %broadcast_compare_fusion, pred[9,128]{1,0:T(8,128)(4,1)S(1)} %compare_bitcast_fusion), kind=kLoop, calls=%fused_computation | loop fusion | flops 884736 | bytes 1819776 | tf_op jit(solution)/shard_map/jit(_where)/select_n | solution.py:305
  25.5 15.6 %all-to-all-done.parts_ref = f32[64,16,256]{2,1,0:T(8,128)S(1)} async-done(((f32[64,16,256]{2,1,0:T(8,128)}), f32[64,16,256]{2,1,0:T(8,128)S(1)}, u32[]{:S(2)}, u32[]{:S(2)}) %all-to-all-start) | async-done | bytes 1048608 | tf_op jit(solution)/shard_map/all_to_all | solution.py:265
  41.1 1.1 %shard_map.106 = bf16[64,16,256]{2,1,0:T(8,128)(2,1)} custom-call(f32[64,16,256]{2,1,0:T(8,128)S(1)} %all-to-all-done.parts_ref, f32[256,256]{1,0:T(8,128)S(1)} %fusion.1.factor_ref), custom_call_target="tpu_custom_call" | custom-call | flops 16777216 | bytes 2097152 | tf_op jit(solution)/shard_map/pallas_call | solution.py:269
  42.2 5.0 %all-to-all-start.1 = ((bf16[64,16,256]{2,1,0:T(8,128)(2,1)}), bf16[64,16,256]{2,1,0:T(8,128)(2,1)S(1)}, u32[]{:S(2)}, u32[]{:S(2)}) async-start(bf16[64,16,256]{2,1,0:T(8,128)(2,1)} %shard_map.106), calls=%async_computation.1 | async-start | bytes 1048576 | tf_op jit(solution)/shard_map/all_to_all | solution.py:278
  47.2 0.8 fusion.7
  48.0 0.8 shard_map.107
  48.9 1.1 %collective-permute-start.1 = (bf16[96,1280]{1,0:T(8,128)(2,1)S(1)}, bf16[96,1280]{1,0:T(8,128)(2,1)S(1)}, u32[]{:S(2)}, u32[]{:S(2)}) collective-permute-start(bf16[96,1280]{1,0:T(8,128)(2,1)S(1)} %get-tuple-element.10), channel_id=1, source_target_pairs={{0,2},{2,4},{4,6},{6,8},{8,10},{10,12},{12,14},{14,16},{16,18},{18... | collective-permute-start | bytes 737288 | tf_op jit(solution)/shard_map/ppermute | solution.py:299
  49.9 5.9 %collective-permute-start.2 = (bf16[96,1280]{1,0:T(8,128)(2,1)S(1)}, bf16[96,1280]{1,0:T(8,128)(2,1)S(1)}, u32[]{:S(2)}, u32[]{:S(2)}) collective-permute-start(bf16[96,1280]{1,0:T(8,128)(2,1)S(1)} %get-tuple-element.11), channel_id=1, source_target_pairs={{2,0},{4,2},{6,4},{8,6},{10,8},{12,10},{14,12},{16,14},{18,16},{20... | collective-permute-start | bytes 737288 | tf_op jit(solution)/shard_map/ppermute | solution.py:300
  55.8 20.0 %shard_map.104 = (bf16[8,256,640]{2,1,0:T(8,128)(2,1)S(1)}, s32[8]{0:T(128)S(1)}) custom-call(s32[128]{0:T(128)S(1)} %bitcast.12, bf16[9,128,384]{2,1,0:T(8,128)(2,1)S(1)} %and_select_fusion.cm_ref), custom_call_target="tpu_custom_call" | custom-call | flops 1677721600 | bytes 4194304 | tf_op jit(solution)/shard_map/pallas_call | solution.py:306
  75.8 1.5 %copy-done.6 = bf16[8,256,640]{2,1,0:T(8,128)(2,1)} copy-done((bf16[8,256,640]{2,1,0:T(8,128)(2,1)}, bf16[8,256,640]{2,1,0:T(8,128)(2,1)S(1)}, u32[]{:S(2)}) %copy-start.6) | copy-done | bytes 2621464
  77.3 0.0 collective-permute-done.1.before_ref
  77.3 0.0 collective-permute-done.2.after_ref
  77.3 0.0 all-to-all-done.1
  77.4 12.0 %shard_map.108 = (bf16[2048,1024]{1,0:T(8,128)(2,1)}, f32[64,256]{1,0:T(8,128)S(1)}, f32[64,256]{1,0:T(8,128)S(1)}) custom-call(s32[1]{0:T(128)} %bitcast.col_ref, s32[8]{0:T(128)S(1)} %get-tuple-element.9.start_ref, bf16[1024,256]{1,0:T(8,128)(2,1)S(1)} %bitcast.9, bf16[96,1280]{1,0:T(8,128)(2,1)S(1)} %collective-permute-done.1.before_ref, ...), custom_call_target="tpu_custom_call" | custom-call | flops 10737418240 | bytes 14680064 | tf_op jit(solution)/shard_map/pallas_call | solution.py:321
  89.4 2.1 %collective-permute-start.3 = (f32[64,256]{1,0:T(8,128)S(1)}, f32[64,256]{1,0:T(8,128)S(1)}, u32[]{:S(2)}, u32[]{:S(2)}) collective-permute-start(f32[64,256]{1,0:T(8,128)S(1)} %get-tuple-element.15), channel_id=1, source_target_pairs={{0,1},{1,0},{2,3},{3,2},{4,5},{5,4},{6,7},{7,6},{8,9},{9,8},{10,11... | collective-permute-start | bytes 196616 | tf_op jit(solution)/shard_map/ppermute | solution.py:342
  91.5 0.9 collective-permute-done.3
  92.4 0.6 add.8
  (17 shorter events, 0.1 us)
Async XLA Ops:
  0.6 4.0 %collective-permute-start = (bf16[2048,128]{1,0:T(8,128)(2,1)}, bf16[2048,128]{1,0:T(8,128)(2,1)S(1)}, u32[]{:S(2)}, u32[]{:S(2)}) collective-permute-start(bf16[2048,128]{1,0:T(8,128)(2,1)} %own_ref.3), channel_id=1, source_target_pairs={{0,1},{1,0},{2,3},{3,2},{4,5},{5,4},{6,7},{7,6},{8,9},{9,8},{10,11... | collective-permute-start | bytes 1572872 | tf_op jit(solution)/shard_map/ppermute | solution.py:246
  4.6 2.2 %copy-start = (bf16[2048,1024]{1,0:T(8,128)(2,1)S(1)}, bf16[2048,1024]{1,0:T(8,128)(2,1)}, u32[]{:S(2)}) copy-start(bf16[2048,1024]{1,0:T(8,128)(2,1)} %v_hbm.1) | copy-start | bytes 12582916
  6.8 1.0 %copy-start.1 = (bf16[2048,128]{1,0:T(8,128)(2,1)S(1)}, bf16[2048,128]{1,0:T(8,128)(2,1)}, u32[]{:S(2)}) copy-start(bf16[2048,128]{1,0:T(8,128)(2,1)} %own_ref.3) | copy-start | bytes 1572868
  7.8 3.7 %copy-start.3 = (bf16[2048,128]{1,0:T(8,128)(2,1)}, bf16[2048,128]{1,0:T(8,128)(2,1)S(1)}, u32[]{:S(2)}) copy-start(bf16[2048,128]{1,0:T(8,128)(2,1)S(1)} %collective-permute-done.other_ref) | copy-start | bytes 1572868
  7.8 15.0 %copy-start.2 = (bf16[2048,128]{1,0:T(8,128)(2,1)S(1)}, bf16[2048,128]{1,0:T(8,128)(2,1)}, u32[]{:S(2)}) copy-start(bf16[2048,128]{1,0:T(8,128)(2,1)} %own_ref.3) | copy-start | bytes 1572868
  7.8 15.0 %copy-start.7 = (f32[256,256]{1,0:T(8,128)S(1)}, f32[256,256]{1,0:T(8,128)}, u32[]{:S(2)}) copy-start(f32[256,256]{1,0:T(8,128)} %param.11) | copy-start | bytes 786436
  11.5 29.5 %all-to-all-start = ((f32[64,16,256]{2,1,0:T(8,128)}), f32[64,16,256]{2,1,0:T(8,128)S(1)}, u32[]{:S(2)}, u32[]{:S(2)}) async-start(f32[64,16,256]{2,1,0:T(8,128)} %bitcast.4), calls=%async_computation | async-start | bytes 2097152 | tf_op jit(solution)/shard_map/all_to_all | solution.py:265
  22.8 25.3 %copy-start.5 = (s32[1,128]{1,0:T(1,128)S(1)}, s32[1,128]{1,0:T(1,128)}, u32[]{:S(2)}) copy-start(s32[1,128]{1,0:T(1,128)} %param.12) | copy-start | bytes 1540
  42.2 35.1 %copy-start.8 = (f32[1024]{0:T(1024)S(1)}, f32[1024]{0:T(1024)}, u32[]{:S(2)}) copy-start(f32[1024]{0:T(1024)} %param.17) | copy-start | bytes 12292
  42.2 35.1 %copy-start.9 = (s32[1024]{0:T(1024)S(1)}, s32[1024]{0:T(1024)}, u32[]{:S(2)}) copy-start(s32[1024]{0:T(1024)} %param.16) | copy-start | bytes 12292
  42.2 35.2 %copy-start.4 = (bf16[2048,128]{1,0:T(8,128)(2,1)S(1)}, bf16[2048,128]{1,0:T(8,128)(2,1)}, u32[]{:S(2)}) copy-start(bf16[2048,128]{1,0:T(8,128)(2,1)} %copy-done.3) | copy-start | bytes 1572868
  42.2 35.2 %all-to-all-start.1 = ((bf16[64,16,256]{2,1,0:T(8,128)(2,1)}), bf16[64,16,256]{2,1,0:T(8,128)(2,1)S(1)}, u32[]{:S(2)}, u32[]{:S(2)}) async-start(bf16[64,16,256]{2,1,0:T(8,128)(2,1)} %shard_map.106), calls=%async_computation.1 | async-start | bytes 1048576 | tf_op jit(solution)/shard_map/all_to_all | solution.py:278
  48.9 28.5 %collective-permute-start.1 = (bf16[96,1280]{1,0:T(8,128)(2,1)S(1)}, bf16[96,1280]{1,0:T(8,128)(2,1)S(1)}, u32[]{:S(2)}, u32[]{:S(2)}) collective-permute-start(bf16[96,1280]{1,0:T(8,128)(2,1)S(1)} %get-tuple-element.10), channel_id=1, source_target_pairs={{0,2},{2,4},{4,6},{6,8},{8,10},{10,12},{12,14},{14,16},{16,18},{18... | collective-permute-start | bytes 737288 | tf_op jit(solution)/shard_map/ppermute | solution.py:299
  49.9 27.4 %collective-permute-start.2 = (bf16[96,1280]{1,0:T(8,128)(2,1)S(1)}, bf16[96,1280]{1,0:T(8,128)(2,1)S(1)}, u32[]{:S(2)}, u32[]{:S(2)}) collective-permute-start(bf16[96,1280]{1,0:T(8,128)(2,1)S(1)} %get-tuple-element.11), channel_id=1, source_target_pairs={{2,0},{4,2},{6,4},{8,6},{10,8},{12,10},{14,12},{16,14},{18,16},{20... | collective-permute-start | bytes 737288 | tf_op jit(solution)/shard_map/ppermute | solution.py:300
  75.8 1.5 %copy-start.6 = (bf16[8,256,640]{2,1,0:T(8,128)(2,1)}, bf16[8,256,640]{2,1,0:T(8,128)(2,1)S(1)}, u32[]{:S(2)}) copy-start(bf16[8,256,640]{2,1,0:T(8,128)(2,1)S(1)} %get-tuple-element.12.band_hbm) | copy-start | bytes 7864324
  89.4 3.0 %collective-permute-start.3 = (f32[64,256]{1,0:T(8,128)S(1)}, f32[64,256]{1,0:T(8,128)S(1)}, u32[]{:S(2)}, u32[]{:S(2)}) collective-permute-start(f32[64,256]{1,0:T(8,128)S(1)} %get-tuple-element.15), channel_id=1, source_target_pairs={{0,1},{1,0},{2,3},{3,2},{4,5},{5,4},{6,7},{7,6},{8,9},{9,8},{10,11... | collective-permute-start | bytes 196616 | tf_op jit(solution)/shard_map/ppermute | solution.py:342

commit v2 on v1

v2 whole, which is shorter than its diff:
```python
import functools

import jax
import jax.numpy as jnp
from jax import lax
from jax.experimental import pallas as pl
from jax.experimental.pallas import tpu as pltpu
from jax.sharding import PartitionSpec as P

NPMAX = 16
BMAX = 24
K = 9
RIM = 4
EDGE = RIM * BMAX
TAIL = 128
GROUP = 16
SPAN = GROUP + 2 * RIM
WIDE = 640
ALIGN = 64
MIB = 1024 * 1024

VM = pltpu.MemorySpace.VMEM
SM = pltpu.MemorySpace.SMEM
NT = (((1,), (1,)), ((), ()))
NN = (((1,), (0,)), ((), ()))


def dot(a, b, dims=NN, **kw):
    return lax.dot_general(a, b, dims, preferred_element_type=jnp.float32, **kw)


def iota(shape, dim):
    return lax.broadcasted_iota(jnp.int32, shape, dim)


def padded_rows(counts_ref, first_atom, first_row, source):
    slot = iota((EDGE, 1), 0)
    target = jnp.full((EDGE, 1), -1, jnp.int32)
    row = first_row
    for t in range(RIM):
        count = counts_ref[first_atom + t]
        u = slot - t * BMAX
        target = jnp.where((u >= 0) & (u < count), row + u, target)
        row = row + count
    pick = (iota((EDGE, TAIL), 1) == target).astype(jnp.float32).astype(jnp.bfloat16)
    return dot(pick, source).astype(jnp.bfloat16)


def halo_kernel(
    counts_ref, v_hbm, own_hbm, other_hbm, partial_hbm, to_next, to_last, rows_ref, sem
):
    atoms = counts_ref.shape[0]
    rows, cols = v_hbm.shape
    half = own_hbm.shape[1]
    spans = ((0, cols), (cols, half), (cols + half, half))
    copies = []
    for n, first in enumerate((0, rows - TAIL)):
        for m, (src, (at, width)) in enumerate(zip((v_hbm, own_hbm, other_hbm), spans)):
            copies.append(
                pltpu.make_async_copy(
                    src.at[pl.ds(first, TAIL)],
                    rows_ref.at[n, :, pl.ds(at, width)],
                    sem.at[n, m],
                )
            )
            copies[-1].start()
    tail = counts_ref[atoms - 1]
    for t in range(1, RIM):
        tail = tail + counts_ref[atoms - 1 - t]
    for c in copies:
        c.wait()
    to_next[...] = padded_rows(counts_ref, atoms - RIM, TAIL - tail, rows_ref[1])
    to_last[...] = padded_rows(counts_ref, 0, 0, rows_ref[0])


def pre_kernel(
    first_group,
    counts_ref,
    present_ref,
    proj_ref,
    cm_ref,
    halo_ref,
    v_hbm,
    own_hbm,
    other_hbm,
    u_hbm,
    t_hbm,
    mark_ref,
    pos_ref,
    cp_ref,
    mask_ref,
    column_ref,
    e_ref,
    p_ref,
    u_ref,
    t_ref,
    sem,
    out_sem,
):
    atoms = counts_ref.shape[0]
    rows, cols = v_hbm.shape
    half = own_hbm.shape[1]
    inner = pl.ds(EDGE, rows)
    copies = [
        pltpu.make_async_copy(v_hbm, e_ref.at[inner], sem.at[0]),
        pltpu.make_async_copy(own_hbm, p_ref.at[inner, pl.ds(0, half)], sem.at[1]),
        pltpu.make_async_copy(other_hbm, p_ref.at[inner, pl.ds(half, half)], sem.at[2]),
    ]
    for c in copies:
        c.start()
    out_copies = []
    mine, unread = (0, EDGE + rows) if first_group == 0 else (EDGE + rows, 0)
    e_ref[mine : mine + EDGE, :] = halo_ref[:, :cols]
    p_ref[mine : mine + EDGE, :] = halo_ref[:, cols:]
    e_ref[unread : unread + EDGE, :] = jnp.zeros((EDGE, cols), jnp.bfloat16)
    p_ref[unread : unread + EDGE, :] = jnp.zeros((EDGE, 2 * half), jnp.bfloat16)
    mark_ref[0] = counts_ref[0]

    for t in range(RIM):
        pos_ref[t] = t * BMAX
        pos_ref[RIM + atoms + t] = EDGE + rows + t * BMAX

    def add(t, at):
        pos_ref[RIM + t] = at
        return at + counts_ref[t]

    lax.fori_loop(0, atoms, add, jnp.int32(EDGE), unroll=8)
    mask_ref[...] = jnp.zeros(mask_ref.shape, jnp.float32)
    mask_ref[:K, :] = present_ref[...].astype(jnp.float32)
    mask_ref[K : K + 1, :] = proj_ref[...].astype(jnp.float32)
    column_ref[...] = mask_ref[...].T
    lanes = NPMAX * BMAX
    lane = iota((8, WIDE), 1)
    which = lane // BMAX
    slot = lane - which * BMAX
    sub = iota((GROUP, lanes), 1) // BMAX
    for n in range(u_ref.shape[0]):
        g = first_group + n
        mine = slice(g * GROUP, (g + 1) * GROUP)
        first = pos_ref[g * GROUP]
        start = jnp.minimum((first // ALIGN) * ALIGN, rows + 2 * EDGE - WIDE)
        target = jnp.full((8, WIDE), -1, jnp.int32)
        for t in range(SPAN):
            atom = g * GROUP + t - RIM
            count = counts_ref[atom] if 0 <= atom < atoms else BMAX
            at = pos_ref[atom + RIM] - start
            target = jnp.where((which == t) & (slot < count), at + slot, target)
        pick = (iota((WIDE, WIDE), 0) == target[:1]).astype(jnp.float32).astype(jnp.bfloat16)
        kept = column_ref[mine, K : K + 1] > sub.astype(jnp.float32)
        x = []
        for k in range(K):
            block = cm_ref[k, mine, :].astype(jnp.float32)
            x.append(jnp.where((column_ref[mine, k : k + 1] > 0.0) & kept, block, 0.0))
        x += [None] * (NPMAX - K)
        for bit in (1, 2, 4, 8):
            low = (sub // bit) % 2 == 0
            new = list(x)
            for p in range(NPMAX):
                q = p + bit
                if p & bit or (x[p] is None and x[q] is None):
                    continue
                a, b = x[p], x[q]
                zero = jnp.zeros((GROUP, lanes), jnp.float32)
                b_up = zero if b is None else pltpu.roll(b, bit * BMAX, 1)
                a_down = zero if a is None else pltpu.roll(a, lanes - bit * BMAX, 1)
                new[p] = jnp.where(low, zero if a is None else a, b_up)
                new[q] = jnp.where(low, a_down, zero if b is None else b)
            x = new
        pad = jnp.zeros((GROUP, WIDE - lanes), jnp.float32)
        for i in range(NPMAX):
            wide = jnp.concatenate([x[i], pad], axis=1)
            halves = [wide[:8], pltpu.roll(wide[8:], 8 * BMAX, 1)]
            for _ in range(2):
                halves = [pltpu.roll(h, 0, 1, stride=BMAX // 2, stride_axis=0) for h in halves]
            skew = jnp.concatenate(halves, axis=0)
            cp_ref[n, i * GROUP : (i + 1) * GROUP, :] = skew.astype(jnp.bfloat16)
        band = dot(cp_ref[n], pick, NT).astype(jnp.bfloat16)
        if n == 0:
            for c in copies:
                c.wait()
        window = pl.ds(pl.multiple_of(start, ALIGN), WIDE)
        u_ref[n] = dot(band, e_ref[window, :]).astype(jnp.bfloat16)
        t_ref[n] = dot(band, p_ref[window, :]).astype(jnp.bfloat16)
        out_copies.append(pltpu.make_async_copy(u_ref.at[n], u_hbm.at[n], out_sem.at[0, n]))
        out_copies.append(pltpu.make_async_copy(t_ref.at[n], t_hbm.at[n], out_sem.at[1, n]))
        for c in out_copies[-2:]:
            c.start()
    for c in out_copies:
        c.wait()


def inner_kernel(own_ref, other_ref, v_ref, out_ref, pt_ref):
    half = own_ref.shape[1]

    @pl.when(pl.program_id(0) == 0)
    def _():
        pt_ref[:half, :] = own_ref[...].T
        pt_ref[half:, :] = other_ref[...].T

    out_ref[...] = dot(pt_ref[...], v_ref[...]).T.astype(jnp.bfloat16)


def mix_kernel(mark_ref, parts_ref, factor_ref, out_ref):
    total = jnp.sum(parts_ref[...].astype(jnp.float32), axis=0)
    mixed = dot(total, factor_ref[...], precision=lax.Precision.HIGHEST).astype(jnp.bfloat16)
    out_ref[...] = jnp.broadcast_to(mixed[None], out_ref.shape)


def main_kernel(
    col_ref,
    mix_ref,
    weight_ref,
    own_ref,
    other_ref,
    u_low,
    t_low,
    u_high,
    t_high,
    v_hbm,
    vectors_hbm,
    own_out,
    other_out,
    v_ref,
    u_ref,
    t_ref,
    r_ref,
    d_ref,
    v_sem,
    u_sem,
    out_sem,
):
    rows, cols = v_hbm.shape
    blocks = rows // 256
    per = u_low.shape[0]
    u_copies = []
    for n in range(2 * per):
        u, t = (u_low, t_low) if n < per else (u_high, t_high)
        at = n % per
        u_copies.append(
            [
                pltpu.make_async_copy(u.at[at], u_ref.at[n], u_sem.at[0, n]),
                pltpu.make_async_copy(t.at[at], t_ref.at[n], u_sem.at[1, n]),
            ]
        )
    for c in u_copies[0]:
        c.start()
    v_copies, out_copies = [], []
    for b in range(blocks):
        at = pl.ds(b * 256, 256)
        v_copies.append(pltpu.make_async_copy(v_hbm.at[at], v_ref.at[at], v_sem.at[b]))
        out_copies.append(pltpu.make_async_copy(r_ref.at[at], vectors_hbm.at[at], out_sem.at[b]))
    for step in range(2 * per):
        for b in (2 * step, 2 * step + 1):
            if b < blocks:
                v_copies[b].start()
        if step:
            for c in u_copies[step]:
                c.start()
    mix = mix_ref[...]
    weight = weight_ref[...]
    down, along = iota((256, 256), 0), iota((256, 256), 1)
    same_atom = (down % GROUP) == (along % GROUP)
    spread = ((down // GROUP) == (along % NPMAX)).astype(jnp.float32).astype(jnp.bfloat16)
    same_i = (down // GROUP) == (along // NPMAX)

    def rotate(b):
        v_copies[b].wait()
        at = slice(b * 256, (b + 1) * 256)
        panel = jnp.concatenate([own_ref[at, :], other_ref[at, :]], axis=1)
        turned = v_ref[at, :].astype(jnp.float32) - dot(panel, mix, NT)
        r_ref[at, :] = turned.astype(jnp.bfloat16)
        out_copies[b].start()

    def pairs_of(step):
        for c in u_copies[step]:
            c.wait()
        turned = u_ref[step].astype(jnp.float32) - dot(t_ref[step], mix, NT)
        rounded = turned.astype(jnp.bfloat16)
        weighted = (rounded.astype(jnp.float32) * weight).astype(jnp.bfloat16)
        pairs = jnp.where(same_atom, dot(weighted, rounded, NT), 0.0)
        high = pairs.astype(jnp.bfloat16)
        low = (pairs - high.astype(jnp.float32)).astype(jnp.bfloat16)
        spreaded = jnp.where(same_i, dot(high, spread) + dot(low, spread), 0.0)
        total = spreaded[:GROUP]
        for i in range(1, NPMAX):
            total = total + spreaded[i * GROUP : (i + 1) * GROUP]
        return total

    for step in range(2 * per):
        d_ref[step * GROUP : (step + 1) * GROUP, :] = pairs_of(step)
        for b in (2 * step, 2 * step + 1):
            if b < blocks:
                rotate(b)
    mine = pl.multiple_of(col_ref[0] * (per * GROUP), per * GROUP)
    own_out[...] = d_ref[pl.ds(mine, per * GROUP), :]
    other_out[...] = d_ref[pl.ds(per * GROUP - mine, per * GROUP), :]
    for c in out_copies:
        c.wait()


def call(kernel, out_shape, in_specs, out_specs, flops, nbytes, mib, **kw):
    return pl.pallas_call(
        kernel,
        out_shape=out_shape,
        in_specs=in_specs,
        out_specs=out_specs,
        compiler_params=pltpu.CompilerParams(vmem_limit_bytes=mib * MIB),
        cost_estimate=pl.CostEstimate(flops=flops, bytes_accessed=nbytes, transcendentals=0),
        **kw,
    )


def local(
    vectors_in, panel, factor, atom_basis, proj_count, coupling, block_present, occ_mask, occ_weight
):
    rows, cols = vectors_in.shape
    half = panel.shape[1]
    npan = 2 * half
    counts = atom_basis[0]
    atoms = counts.shape[0]
    groups = atoms // GROUP
    n_row = lax.axis_size("row")
    n_col = lax.axis_size("col")
    col = lax.axis_index("col")
    vmem = pl.BlockSpec(memory_space=VM)
    smem = pl.BlockSpec(memory_space=SM)
    hbm = pl.BlockSpec(memory_space=pltpu.MemorySpace.HBM)
    bf16, f32 = jnp.bfloat16, jnp.float32

    other = lax.ppermute(panel, "col", [(0, 1), (1, 0)])
    v_in_hbm = pltpu.with_memory_space_constraint(vectors_in, pltpu.MemorySpace.HBM)

    tile = 256
    partial = pl.pallas_call(
        inner_kernel,
        out_shape=jax.ShapeDtypeStruct((cols, npan), bf16),
        grid=(cols // tile,),
        in_specs=[
            pl.BlockSpec((rows, half), lambda c: (0, 0)),
            pl.BlockSpec((rows, half), lambda c: (0, 0)),
            pl.BlockSpec((rows, tile), lambda c: (0, c)),
        ],
        out_specs=pl.BlockSpec((tile, npan), lambda c: (c, 0)),
        scratch_shapes=[pltpu.VMEM((npan, rows), bf16)],
        compiler_params=pltpu.CompilerParams(vmem_limit_bytes=24 * MIB),
        cost_estimate=pl.CostEstimate(
            flops=2 * rows * cols * npan, bytes_accessed=6 << 20, transcendentals=0
        ),
    )(panel, other, v_in_hbm)
    slices = lax.all_to_all(partial, "row", 0, 0, tiled=True)
    slices = slices.reshape(n_row, cols // n_row, npan)

    to_next, to_last = call(
        halo_kernel,
        [jax.ShapeDtypeStruct((EDGE, cols + npan), bf16)] * 2,
        [smem] + [hbm] * 4,
        [vmem, vmem],
        1 << 26,
        2 << 20,
        16,
        scratch_shapes=[
            pltpu.VMEM((2, TAIL, cols + npan), bf16),
            pltpu.SemaphoreType.DMA((2, 3)),
        ],
    )(counts, v_in_hbm, panel, other, partial)
    up = [(i, (i + 1) % n_row) for i in range(n_row)]
    before = lax.ppermute(to_next, "row", up)
    after = lax.ppermute(to_last, "row", [(j, i) for i, j in up])

    per = groups // 2
    blocks = coupling.transpose(1, 0, 2)
    present = block_present.T
    halves = []
    for n, halo in enumerate((before, after)):
        halves.append(
            call(
                functools.partial(pre_kernel, n * per),
                [
                    pltpu.HBM((per, 256, cols), bf16),
                    pltpu.HBM((per, 256, npan), bf16),
                    jax.ShapeDtypeStruct((1,), jnp.int32),
                ],
                [smem] + [vmem] * 4 + [hbm] * 3,
                [hbm, hbm, smem],
                per * 2 * 256 * WIDE * (WIDE + cols + npan),
                10 << 20,
                28,
                scratch_shapes=[
                    pltpu.SMEM((atoms + 2 * RIM,), jnp.int32),
                    pltpu.VMEM((per, 256, WIDE), bf16),
                    pltpu.VMEM((16, atoms), f32),
                    pltpu.VMEM((atoms, 16), f32),
                    pltpu.VMEM((rows + 2 * EDGE, cols), bf16),
                    pltpu.VMEM((rows + 2 * EDGE, npan), bf16),
                    pltpu.VMEM((per, 256, cols), bf16),
                    pltpu.VMEM((per, 256, npan), bf16),
                    pltpu.SemaphoreType.DMA((3,)),
                    pltpu.SemaphoreType.DMA((2, per)),
                ],
            )(counts, present, proj_count[None, :], blocks, halo, v_in_hbm, panel, other)
        )
    mark = halves[0][2]
    ready = [
        pltpu.with_memory_space_constraint(x, pltpu.MemorySpace.HBM)
        for x in halves[0][:2] + halves[1][:2]
    ]

    flipped = jnp.roll(jnp.roll(factor, half, axis=0), half, axis=1)
    ordered = jnp.where(col == 0, factor, flipped)
    copies = call(
        mix_kernel,
        jax.ShapeDtypeStruct((n_row, cols // n_row, npan), bf16),
        [smem, vmem, vmem],
        vmem,
        1 << 24,
        1 << 20,
        8,
    )(mark, slices, ordered)
    mixing = lax.all_to_all(copies.reshape(cols, npan), "row", 0, 0, tiled=True)

    weights = (occ_mask.astype(f32) * occ_weight / (cols * n_col))[None, :]
    vectors, own_part, other_part = call(
        main_kernel,
        [
            jax.ShapeDtypeStruct((rows, cols), bf16),
            jax.ShapeDtypeStruct((atoms // 2, 256), f32),
            jax.ShapeDtypeStruct((atoms // 2, 256), f32),
        ],
        [smem] + [vmem] * 4 + [hbm] * 5,
        [hbm, vmem, vmem],
        10 << 30,
        14 << 20,
        28,
        scratch_shapes=[
            pltpu.VMEM((rows, cols), bf16),
            pltpu.VMEM((groups, 256, cols), bf16),
            pltpu.VMEM((groups, 256, npan), bf16),
            pltpu.VMEM((rows, cols), bf16),
            pltpu.VMEM((atoms, 256), f32),
            pltpu.SemaphoreType.DMA((rows // 256,)),
            pltpu.SemaphoreType.DMA((2, groups)),
            pltpu.SemaphoreType.DMA((rows // 256,)),
        ],
    )(col[None], mixing, weights, panel, other, *ready, v_in_hbm)
    density = own_part + lax.ppermute(other_part, "col", [(0, 1), (1, 0)])
    return vectors, density


def solution(mesh):
    placed = (
        P("row", "col"),
        P("row", "col"),
        P(),
        P("row", None),
        P("row"),
        P("row", None, None),
        P("row", None),
        P("col"),
        P("col"),
    )
    return jax.shard_map(
        local,
        mesh=mesh,
        in_specs=placed,
        out_specs=(P("row", "col"), P(("row", "col"), None)),
        check_vma=False,
    )
```

time: 93.6 us -> 88.3 us (0.943)
  local copies, waits for them, and re-layouts: 7.6 us -> 2.07 us
  waiting for transfers between devices: 16.5 us -> 19.2 us
  Pallas kernels: 37.7 us -> 35.7 us
  other arithmetic: 3.66 us -> 2.31 us
  starting transfers between devices: 26.8 us -> 27.8 us
    all_to_all x1, waiting for transfers between devices: 15.6 us -> 0.01 us  [local(): slices = lax.all_to_all(partial, 'row', 0, 0, tiled=True)]
    ppermute x1, waiting for transfers between devices: 0.01 us -> 13.4 us  [local(): before = lax.ppermute(to_next, 'row', up)]
    pallas_call x1 -> x2, Pallas kernels: 20 us -> 15.6 us  [local(): call(functools.partial(pre_kernel, n * per), [pltpu.HBM((per, 256, cols),...]
    ppermute x1, waiting for transfers between devices: 0.01 us -> 4.18 us  [local(): after = lax.ppermute(to_last, 'row', [(j, i) for i, j in up])]
    unnamed x20, local copies, waits for them, and re-layouts: 4.75 us -> 1.08 us
    slice x3 -> x0, local copies, waits for them, and re-layouts: 1.86 us -> none  [the longest x1 1.07 us: local(): vectors_in[rows - edge:]]
    select_n x2 -> x0, other arithmetic: 1.52 us -> none  [the longest x1 1.51 us: local(): blocks = jnp.where(keep, blocks, jnp.zeros_like(blocks))]
    pallas_call x1, Pallas kernels: 3.7 us -> 5.19 us  [local(): pl.pallas_call(inner_kernel, out_shape=jax.ShapeDtypeStruct((cols, npan),...]
  transfers between devices with their start and end apart: 6 -> 6, of which waited for: 2 -> 4; matrix products, arithmetic and copies ran while one was open for 6% -> 3% of each run, Pallas kernels for 22% -> 20%
where the time goes in v2:
time: 88.3 us; the launch traced here: 87.8 us
  Pallas kernels  35.7 us (40%)
  starting transfers between devices  27.8 us (31%)
  waiting for transfers between devices  19.2 us (22%)
  other arithmetic  2.31 us (3%)
  local copies, waits for them, and re-layouts  2.07 us (2%)
    pallas_call x2, Pallas kernels, local(): call(functools.partial(pre_kernel, n * per), [pltpu.HBM((per, 256, cols),...  15.6 us
    ppermute x1, waiting for transfers between devices, local(): before = lax.ppermute(to_next, 'row', up)  13.4 us
    all_to_all x1, starting transfers between devices, local(): slices = lax.all_to_all(partial, 'row', 0, 0, tiled=True)  11.4 us
    pallas_call x1, Pallas kernels, local(): call(main_kernel, [jax.ShapeDtypeStruct((rows, cols), bf16), jax.ShapeDty...  11.1 us
    ppermute x1, starting transfers between devices, local(): after = lax.ppermute(to_last, 'row', [(j, i) for i, j in up])  7 us
    pallas_call x1, Pallas kernels, local(): pl.pallas_call(inner_kernel, out_shape=jax.ShapeDtypeStruct((cols, npan),...  5.19 us
    all_to_all x1, starting transfers between devices, local(): mixing = lax.all_to_all(copies.reshape(cols, npan), 'row', 0, 0, tiled=True)  4.63 us
    ppermute x1, waiting for transfers between devices, local(): after = lax.ppermute(to_last, 'row', [(j, i) for i, j in up])  4.18 us
  transfers between devices with their start and end apart: 6, of which 4 were waited for; matrix products, arithmetic and copies ran while one was open for 3% of the time, Pallas kernels for 20%

profile of v2, /device:TPU:1, one launch (start us, length us, event | category | flops | bytes accessed | tf_op | source)
XLA Modules:
  0.0 87.8 jit_solution(5274961478491814211)
XLA Ops:
  0.6 0.0 copy-start.1
  0.6 1.5 %collective-permute-start = (bf16[2048,128]{1,0:T(8,128)(2,1)}, bf16[2048,128]{1,0:T(8,128)(2,1)S(1)}, u32[]{:S(2)}, u32[]{:S(2)}) collective-permute-start(bf16[2048,128]{1,0:T(8,128)(2,1)} %own_ref.3), channel_id=1, source_target_pairs={{0,1},{1,0},{2,3},{3,2},{4,5},{5,4},{6,7},{7,6},{8,9},{9,8},{10,11... | collective-permute-start | bytes 1572872 | tf_op jit(solution)/shard_map/ppermute | solution.py:330
  2.1 1.0 %fusion.3 = (f32[128,256]{1,0:T(8,128)S(1)}, f32[128,256]{1,0:T(8,128)S(1)}) fusion(f32[256,256]{1,0:T(8,128)} %param.11), kind=kLoop, calls=%fused_computation.7 | loop fusion | bytes 524288 | tf_op jit(solution)/shard_map/jit(_roll_static)/slice | solution.py:408
  3.1 0.0 copy-start.6
  3.1 0.0 copy-start.7
  3.2 0.7 collective-permute-done.other_ref.other_hbm
  3.9 1.0 %copy-done = bf16[2048,128]{1,0:T(8,128)(2,1)S(1)} copy-done((bf16[2048,128]{1,0:T(8,128)(2,1)S(1)}, bf16[2048,128]{1,0:T(8,128)(2,1)}, u32[]{:S(2)}) %copy-start) | copy-done | bytes 524312
  4.9 5.2 %shard_map.104.partial_hbm = bf16[1024,256]{1,0:T(8,128)(2,1)} custom-call(bf16[2048,128]{1,0:T(8,128)(2,1)S(1)} %copy-done, bf16[2048,128]{1,0:T(8,128)(2,1)S(1)} %collective-permute-done.other_ref.other_hbm, bf16[2048,1024]{1,0:T(8,128)(2,1)} %v_hbm.7), custom_call_target="tpu_custom_call" | custom-call | flops 1073741824 | bytes 6291456 | tf_op jit(solution)/shard_map/pallas_call | solution.py:334
  10.1 11.4 %all-to-all-start = ((bf16[64,16,256]{2,1,0:T(8,128)(2,1)}), bf16[64,16,256]{2,1,0:T(8,128)(2,1)S(1)}, u32[]{:S(2)}, u32[]{:S(2)}) async-start(bf16[64,16,256]{2,1,0:T(8,128)(2,1)} %bitcast.5), calls=%async_computation | async-start | bytes 1048576 | tf_op jit(solution)/shard_map/all_to_all | solution.py:350
  21.5 0.0 copy-done.1
  21.5 0.0 copy-done.2
  21.5 1.9 %shard_map.105 = (bf16[96,1280]{1,0:T(8,128)(2,1)S(1)}, bf16[96,1280]{1,0:T(8,128)(2,1)S(1)}) custom-call(s32[128]{0:T(128)S(1)} %bitcast.10, bf16[2048,1024]{1,0:T(8,128)(2,1)} %v_hbm.7, bf16[2048,128]{1,0:T(8,128)(2,1)S(1)} %copy-done.1, bf16[2048,128]{1,0:T(8,128)(2,1)S(1)} %collective-permute-done.other_ref.other_hbm, ...), custom_call_target="tpu_custom_call" | custom-call | flops 67108864 | bytes 2097152 | tf_op jit(solution)/shard_map/pallas_call | solution.py:353
  23.4 1.1 %collective-permute-start.1 = (bf16[96,1280]{1,0:T(8,128)(2,1)S(1)}, bf16[96,1280]{1,0:T(8,128)(2,1)S(1)}, u32[]{:S(2)}, u32[]{:S(2)}) collective-permute-start(bf16[96,1280]{1,0:T(8,128)(2,1)S(1)} %get-tuple-element.12), channel_id=1, source_target_pairs={{0,2},{2,4},{4,6},{6,8},{8,10},{10,12},{12,14},{14,16},{16,18},{18... | collective-permute-start | bytes 737288 | tf_op jit(solution)/shard_map/ppermute | solution.py:367
  24.5 0.0 copy-done.6
  24.5 0.7 fusion.2
  25.2 1.0 %fusion.1.factor_ref = f32[256,256]{1,0:T(8,128)S(1)} fusion(f32[256,256]{1,0:T(8,128)} %param.11, f32[128,256]{1,0:T(8,128)} %copy-done.7, f32[128,256]{1,0:T(8,128)} %copy-done.6, f32[256,128]{1,0:T(8,128)} %fusion.2, pred[]{:T(512)S(6)} %eq.3), kind=kLoop, calls=%fused_computation.2 | loop fusion | flops 196608 | bytes 917505 | tf_op jit(solution)/shard_map/jit(_where)/select_n | solution.py:409
  26.2 13.4 %collective-permute-done.1.halo_ref = bf16[96,1280]{1,0:T(8,128)(2,1)S(1)} collective-permute-done((bf16[96,1280]{1,0:T(8,128)(2,1)S(1)}, bf16[96,1280]{1,0:T(8,128)(2,1)S(1)}, u32[]{:S(2)}, u32[]{:S(2)}) %collective-permute-start.1) | collective-permute-done | bytes 245792 | tf_op jit(solution)/shard_map/ppermute | solution.py:367
  39.6 0.0 copy-done.5
  39.6 0.0 copy-start.8
  39.6 0.0 copy-start.9
  39.6 7.8 %shard_map.106 = (bf16[4,256,1024]{2,1,0:T(8,128)(2,1)}, bf16[4,256,256]{2,1,0:T(8,128)(2,1)}, s32[1]{0:T(128)}) custom-call(s32[128]{0:T(128)S(1)} %bitcast.11, s32[9,128]{1,0:T(8,128)S(1)} %bitcast.15, s32[1,128]{1,0:T(1,128)S(1)} %bitcast.17, bf16[9,128,384]{2,1,0:T(8,128)(2,1)S(1)} %bitcast.13, bf16[96,1280]{1,0:T(8,128)(2,1)S(1)} %collective-permute-done.1.halo_ref, ...), custom_call_target="tpu_custom_call" | custom-call | flops 2516582400 | bytes 10485760 | tf_op jit(solution)/shard_map/pallas_call | solution.py:376
  47.4 0.0 all-to-all-done.parts_ref
  47.4 1.8 %shard_map.107 = bf16[64,16,256]{2,1,0:T(8,128)(2,1)} custom-call(s32[1]{0:T(128)} %get-tuple-element.13.mark_ref, bf16[64,16,256]{2,1,0:T(8,128)(2,1)S(1)} %all-to-all-done.parts_ref, f32[256,256]{1,0:T(8,128)S(1)} %fusion.1.factor_ref), custom_call_target="tpu_custom_call" | custom-call | flops 16777216 | bytes 1048576 | tf_op jit(solution)/shard_map/pallas_call | solution.py:410
  49.2 4.6 %all-to-all-start.1 = ((bf16[64,16,256]{2,1,0:T(8,128)(2,1)}), bf16[64,16,256]{2,1,0:T(8,128)(2,1)S(1)}, u32[]{:S(2)}, u32[]{:S(2)}) async-start(bf16[64,16,256]{2,1,0:T(8,128)(2,1)} %shard_map.107), calls=%async_computation.1 | async-start | bytes 1048576 | tf_op jit(solution)/shard_map/all_to_all | solution.py:419
  53.9 7.0 %collective-permute-start.2 = (bf16[96,1280]{1,0:T(8,128)(2,1)S(1)}, bf16[96,1280]{1,0:T(8,128)(2,1)S(1)}, u32[]{:S(2)}, u32[]{:S(2)}) collective-permute-start(bf16[96,1280]{1,0:T(8,128)(2,1)S(1)} %get-tuple-element.16), channel_id=1, source_target_pairs={{2,0},{4,2},{6,4},{8,6},{10,8},{12,10},{14,12},{16,14},{18,16},{20... | collective-permute-start | bytes 737288 | tf_op jit(solution)/shard_map/ppermute | solution.py:368
  60.9 4.2 %collective-permute-done.2.halo_ref = bf16[96,1280]{1,0:T(8,128)(2,1)S(1)} collective-permute-done((bf16[96,1280]{1,0:T(8,128)(2,1)S(1)}, bf16[96,1280]{1,0:T(8,128)(2,1)S(1)}, u32[]{:S(2)}, u32[]{:S(2)}) %collective-permute-start.2) | collective-permute-done | bytes 245792 | tf_op jit(solution)/shard_map/ppermute | solution.py:368
  65.0 7.8 %shard_map.108 = (bf16[4,256,1024]{2,1,0:T(8,128)(2,1)}, bf16[4,256,256]{2,1,0:T(8,128)(2,1)}, s32[1]{0:T(128)}) custom-call(s32[128]{0:T(128)S(1)} %bitcast.12, s32[9,128]{1,0:T(8,128)S(1)} %bitcast.16, s32[1,128]{1,0:T(1,128)S(1)} %bitcast.18, bf16[9,128,384]{2,1,0:T(8,128)(2,1)S(1)} %bitcast.14, bf16[96,1280]{1,0:T(8,128)(2,1)S(1)} %collective-permute-done.2.halo_ref, ...), custom_call_target="tpu_custom_call" | custom-call | flops 2516582400 | bytes 10485760 | tf_op jit(solution)/shard_map/pallas_call | solution.py:376
  72.9 0.0 all-to-all-done.1
  72.9 11.1 %shard_map.109 = (bf16[2048,1024]{1,0:T(8,128)(2,1)}, f32[64,256]{1,0:T(8,128)S(1)}, f32[64,256]{1,0:T(8,128)S(1)}) custom-call(s32[1]{0:T(128)} %bitcast.col_ref, bf16[1024,256]{1,0:T(8,128)(2,1)S(1)} %bitcast.8, f32[1,1024]{1,0:T(1,128)S(1)} %bitcast.9, bf16[2048,128]{1,0:T(8,128)(2,1)S(1)} %copy-done.1, ...), custom_call_target="tpu_custom_call" | custom-call | flops 10737418240 | bytes 14680064 | tf_op jit(solution)/shard_map/pallas_call | solution.py:422
  84.0 2.3 %collective-permute-start.3 = (f32[64,256]{1,0:T(8,128)S(1)}, f32[64,256]{1,0:T(8,128)S(1)}, u32[]{:S(2)}, u32[]{:S(2)}) collective-permute-start(f32[64,256]{1,0:T(8,128)S(1)} %get-tuple-element.21), channel_id=1, source_target_pairs={{0,1},{1,0},{2,3},{3,2},{4,5},{5,4},{6,7},{7,6},{8,9},{9,8},{10,11... | collective-permute-start | bytes 196616 | tf_op jit(solution)/shard_map/ppermute | solution.py:445
  86.3 0.9 %collective-permute-done.3 = f32[64,256]{1,0:T(8,128)S(1)} collective-permute-done((f32[64,256]{1,0:T(8,128)S(1)}, f32[64,256]{1,0:T(8,128)S(1)}, u32[]{:S(2)}, u32[]{:S(2)}) %collective-permute-start.3) | collective-permute-done | bytes 65568 | tf_op jit(solution)/shard_map/ppermute | solution.py:445
  87.2 0.6 add.3
  (11 shorter events, 0.0 us)
Async XLA Ops:
  0.6 20.9 %copy-start.1 = (bf16[2048,128]{1,0:T(8,128)(2,1)S(1)}, bf16[2048,128]{1,0:T(8,128)(2,1)}, u32[]{:S(2)}) copy-start(bf16[2048,128]{1,0:T(8,128)(2,1)} %own_ref.3) | copy-start | bytes 1572868
  0.6 3.2 %collective-permute-start = (bf16[2048,128]{1,0:T(8,128)(2,1)}, bf16[2048,128]{1,0:T(8,128)(2,1)S(1)}, u32[]{:S(2)}, u32[]{:S(2)}) collective-permute-start(bf16[2048,128]{1,0:T(8,128)(2,1)} %own_ref.3), channel_id=1, source_target_pairs={{0,1},{1,0},{2,3},{3,2},{4,5},{5,4},{6,7},{7,6},{8,9},{9,8},{10,11... | collective-permute-start | bytes 1572872 | tf_op jit(solution)/shard_map/ppermute | solution.py:330
  3.1 21.4 %copy-start.6 = (f32[128,256]{1,0:T(8,128)}, f32[128,256]{1,0:T(8,128)S(1)}, u32[]{:S(2)}) copy-start(f32[128,256]{1,0:T(8,128)S(1)} %get-tuple-element.22) | copy-start | bytes 393220
  3.1 22.0 %copy-start.7 = (f32[128,256]{1,0:T(8,128)}, f32[128,256]{1,0:T(8,128)S(1)}, u32[]{:S(2)}) copy-start(f32[128,256]{1,0:T(8,128)S(1)} %get-tuple-element.23) | copy-start | bytes 393220
  3.9 1.0 %copy-start = (bf16[2048,128]{1,0:T(8,128)(2,1)S(1)}, bf16[2048,128]{1,0:T(8,128)(2,1)}, u32[]{:S(2)}) copy-start(bf16[2048,128]{1,0:T(8,128)(2,1)} %own_ref.3) | copy-start | bytes 1572868
  4.9 16.6 %copy-start.2 = (s32[1,128]{1,0:T(1,128)S(1)}, s32[1,128]{1,0:T(1,128)}, u32[]{:S(2)}) copy-start(s32[1,128]{1,0:T(1,128)} %param.12) | copy-start | bytes 1540
  10.1 29.4 %copy-start.3 = (bf16[128,9,384]{2,0,1:T(8,128)(2,1)S(1)}, bf16[128,9,384]{2,0,1:T(8,128)(2,1)}, u32[]{:S(2)}) copy-start(bf16[128,9,384]{2,0,1:T(8,128)(2,1)} %param.14) | copy-start | bytes 2654212
  10.1 29.4 %copy-start.4 = (s32[128,9]{0,1:T(8,128)S(1)}, s32[128,9]{0,1:T(8,128)}, u32[]{:S(2)}) copy-start(s32[128,9]{0,1:T(8,128)} %param.15) | copy-start | bytes 13828
  10.1 29.4 %copy-start.5 = (s32[128]{0:T(128)S(1)}, s32[128]{0:T(128)}, u32[]{:S(2)}) copy-start(s32[128]{0:T(128)} %param.13) | copy-start | bytes 1540
  10.1 37.3 %all-to-all-start = ((bf16[64,16,256]{2,1,0:T(8,128)(2,1)}), bf16[64,16,256]{2,1,0:T(8,128)(2,1)S(1)}, u32[]{:S(2)}, u32[]{:S(2)}) async-start(bf16[64,16,256]{2,1,0:T(8,128)(2,1)} %bitcast.5), calls=%async_computation | async-start | bytes 1048576 | tf_op jit(solution)/shard_map/all_to_all | solution.py:350
  23.4 16.1 %collective-permute-start.1 = (bf16[96,1280]{1,0:T(8,128)(2,1)S(1)}, bf16[96,1280]{1,0:T(8,128)(2,1)S(1)}, u32[]{:S(2)}, u32[]{:S(2)}) collective-permute-start(bf16[96,1280]{1,0:T(8,128)(2,1)S(1)} %get-tuple-element.12), channel_id=1, source_target_pairs={{0,2},{2,4},{4,6},{6,8},{8,10},{10,12},{12,14},{14,16},{16,18},{18... | collective-permute-start | bytes 737288 | tf_op jit(solution)/shard_map/ppermute | solution.py:367
  39.6 21.3 %copy-start.8 = (f32[1024]{0:T(1024)S(1)}, f32[1024]{0:T(1024)}, u32[]{:S(2)}) copy-start(f32[1024]{0:T(1024)} %param.17) | copy-start | bytes 12292
  39.6 21.3 %copy-start.9 = (s32[1024]{0:T(1024)S(1)}, s32[1024]{0:T(1024)}, u32[]{:S(2)}) copy-start(s32[1024]{0:T(1024)} %param.16) | copy-start | bytes 12292
  49.2 23.7 %all-to-all-start.1 = ((bf16[64,16,256]{2,1,0:T(8,128)(2,1)}), bf16[64,16,256]{2,1,0:T(8,128)(2,1)S(1)}, u32[]{:S(2)}, u32[]{:S(2)}) async-start(bf16[64,16,256]{2,1,0:T(8,128)(2,1)} %shard_map.107), calls=%async_computation.1 | async-start | bytes 1048576 | tf_op jit(solution)/shard_map/all_to_all | solution.py:419
  53.9 11.2 %collective-permute-start.2 = (bf16[96,1280]{1,0:T(8,128)(2,1)S(1)}, bf16[96,1280]{1,0:T(8,128)(2,1)S(1)}, u32[]{:S(2)}, u32[]{:S(2)}) collective-permute-start(bf16[96,1280]{1,0:T(8,128)(2,1)S(1)} %get-tuple-element.16), channel_id=1, source_target_pairs={{2,0},{4,2},{6,4},{8,6},{10,8},{12,10},{14,12},{16,14},{18,16},{20... | collective-permute-start | bytes 737288 | tf_op jit(solution)/shard_map/ppermute | solution.py:368
  84.0 3.2 %collective-permute-start.3 = (f32[64,256]{1,0:T(8,128)S(1)}, f32[64,256]{1,0:T(8,128)S(1)}, u32[]{:S(2)}, u32[]{:S(2)}) collective-permute-start(f32[64,256]{1,0:T(8,128)S(1)} %get-tuple-element.21), channel_id=1, source_target_pairs={{0,1},{1,0},{2,3},{3,2},{4,5},{5,4},{6,7},{7,6},{8,9},{9,8},{10,11... | collective-permute-start | bytes 196616 | tf_op jit(solution)/shard_map/ppermute | solution.py:445

commit v3 on v2

v3 whole, which is shorter than its diff:
```python
import functools

import jax
import jax.numpy as jnp
from jax import lax
from jax.experimental import pallas as pl
from jax.experimental.pallas import tpu as pltpu
from jax.sharding import PartitionSpec as P

NPMAX = 16
BMAX = 24
K = 9
RIM = 4
EDGE = RIM * BMAX
TAIL = 128
GROUP = 16
SPAN = GROUP + 2 * RIM
WIDE = 640
ALIGN = 64
MIB = 1024 * 1024

VM = pltpu.MemorySpace.VMEM
SM = pltpu.MemorySpace.SMEM
NT = (((1,), (1,)), ((), ()))
NN = (((1,), (0,)), ((), ()))


def dot(a, b, dims=NN, **kw):
    return lax.dot_general(a, b, dims, preferred_element_type=jnp.float32, **kw)


def iota(shape, dim):
    return lax.broadcasted_iota(jnp.int32, shape, dim)


def padded_rows(counts_ref, first_atom, first_row, source):
    slot = iota((EDGE, 1), 0)
    target = jnp.full((EDGE, 1), -1, jnp.int32)
    row = first_row
    for t in range(RIM):
        count = counts_ref[first_atom + t]
        u = slot - t * BMAX
        target = jnp.where((u >= 0) & (u < count), row + u, target)
        row = row + count
    pick = (iota((EDGE, TAIL), 1) == target).astype(jnp.float32).astype(jnp.bfloat16)
    return dot(pick, source).astype(jnp.bfloat16)


def halo_kernel(
    counts_ref, v_hbm, own_hbm, other_hbm, partial_hbm, to_next, to_last, rows_ref, sem
):
    atoms = counts_ref.shape[0]
    rows, cols = v_hbm.shape
    half = own_hbm.shape[1]
    spans = ((0, cols), (cols, half), (cols + half, half))
    copies = []
    for n, first in enumerate((0, rows - TAIL)):
        for m, (src, (at, width)) in enumerate(zip((v_hbm, own_hbm, other_hbm), spans)):
            copies.append(
                pltpu.make_async_copy(
                    src.at[pl.ds(first, TAIL)],
                    rows_ref.at[n, :, pl.ds(at, width)],
                    sem.at[n, m],
                )
            )
            copies[-1].start()
    tail = counts_ref[atoms - 1]
    for t in range(1, RIM):
        tail = tail + counts_ref[atoms - 1 - t]
    for c in copies:
        c.wait()
    to_next[...] = padded_rows(counts_ref, atoms - RIM, TAIL - tail, rows_ref[1])
    to_last[...] = padded_rows(counts_ref, 0, 0, rows_ref[0])


def pre_kernel(
    which_groups,
    counts_ref,
    present_ref,
    proj_ref,
    cm_ref,
    before_ref,
    after_ref,
    v_hbm,
    own_hbm,
    other_hbm,
    u_hbm,
    t_hbm,
    mark_ref,
    pos_ref,
    cp_ref,
    mask_ref,
    column_ref,
    e_ref,
    p_ref,
    u_ref,
    t_ref,
    sem,
    out_sem,
):
    atoms = counts_ref.shape[0]
    rows, cols = v_hbm.shape
    half = own_hbm.shape[1]
    inner = pl.ds(EDGE, rows)
    copies = [
        pltpu.make_async_copy(v_hbm, e_ref.at[inner], sem.at[0]),
        pltpu.make_async_copy(own_hbm, p_ref.at[inner, pl.ds(0, half)], sem.at[1]),
        pltpu.make_async_copy(other_hbm, p_ref.at[inner, pl.ds(half, half)], sem.at[2]),
    ]
    for c in copies:
        c.start()
    out_copies = []
    for halo_ref, at in ((before_ref, 0), (after_ref, EDGE + rows)):
        mine = slice(at, at + EDGE)
        if halo_ref is None:
            e_ref[mine, :] = jnp.zeros((EDGE, cols), jnp.bfloat16)
            p_ref[mine, :] = jnp.zeros((EDGE, 2 * half), jnp.bfloat16)
        else:
            e_ref[mine, :] = halo_ref[:, :cols]
            p_ref[mine, :] = halo_ref[:, cols:]
    mark_ref[0] = counts_ref[0]

    for t in range(RIM):
        pos_ref[t] = t * BMAX
        pos_ref[RIM + atoms + t] = EDGE + rows + t * BMAX

    def add(t, at):
        pos_ref[RIM + t] = at
        return at + counts_ref[t]

    lax.fori_loop(0, atoms, add, jnp.int32(EDGE), unroll=8)
    mask_ref[...] = jnp.zeros(mask_ref.shape, jnp.float32)
    mask_ref[:K, :] = present_ref[...].astype(jnp.float32)
    mask_ref[K : K + 1, :] = proj_ref[...].astype(jnp.float32)
    column_ref[...] = mask_ref[...].T
    lanes = NPMAX * BMAX
    lane = iota((8, WIDE), 1)
    which = lane // BMAX
    slot = lane - which * BMAX
    sub = iota((GROUP, lanes), 1) // BMAX
    for n, g in enumerate(which_groups):
        mine = slice(g * GROUP, (g + 1) * GROUP)
        first = pos_ref[g * GROUP]
        start = jnp.minimum((first // ALIGN) * ALIGN, rows + 2 * EDGE - WIDE)
        target = jnp.full((8, WIDE), -1, jnp.int32)
        for t in range(SPAN):
            atom = g * GROUP + t - RIM
            count = counts_ref[atom] if 0 <= atom < atoms else BMAX
            at = pos_ref[atom + RIM] - start
            target = jnp.where((which == t) & (slot < count), at + slot, target)
        pick = (iota((WIDE, WIDE), 0) == target[:1]).astype(jnp.float32).astype(jnp.bfloat16)
        kept = column_ref[mine, K : K + 1] > sub.astype(jnp.float32)
        x = []
        for k in range(K):
            block = cm_ref[k, mine, :].astype(jnp.float32)
            x.append(jnp.where((column_ref[mine, k : k + 1] > 0.0) & kept, block, 0.0))
        x += [None] * (NPMAX - K)
        for bit in (1, 2, 4, 8):
            low = (sub & bit) == 0
            new = list(x)
            for p in range(NPMAX):
                q = p + bit
                if p & bit or (x[p] is None and x[q] is None):
                    continue
                a, b = x[p], x[q]
                zero = jnp.zeros((GROUP, lanes), jnp.float32)
                b_up = zero if b is None else pltpu.roll(b, bit * BMAX, 1)
                a_down = zero if a is None else pltpu.roll(a, lanes - bit * BMAX, 1)
                new[p] = jnp.where(low, zero if a is None else a, b_up)
                new[q] = jnp.where(low, a_down, zero if b is None else b)
            x = new
        pad = jnp.zeros((GROUP, WIDE - lanes), jnp.float32)
        for i in range(NPMAX):
            wide = jnp.concatenate([x[i], pad], axis=1)
            halves = [wide[:8], pltpu.roll(wide[8:], 8 * BMAX, 1)]
            for _ in range(2):
                halves = [pltpu.roll(h, 0, 1, stride=BMAX // 2, stride_axis=0) for h in halves]
            skew = jnp.concatenate(halves, axis=0)
            cp_ref[n, i * GROUP : (i + 1) * GROUP, :] = skew.astype(jnp.bfloat16)
        band = dot(cp_ref[n], pick, NT).astype(jnp.bfloat16)
        if n == 0:
            for c in copies:
                c.wait()
        window = pl.ds(pl.multiple_of(start, ALIGN), WIDE)
        u_ref[n] = dot(band, e_ref[window, :]).astype(jnp.bfloat16)
        t_ref[n] = dot(band, p_ref[window, :]).astype(jnp.bfloat16)
        out_copies.append(pltpu.make_async_copy(u_ref.at[n], u_hbm.at[n], out_sem.at[0, n]))
        out_copies.append(pltpu.make_async_copy(t_ref.at[n], t_hbm.at[n], out_sem.at[1, n]))
        for c in out_copies[-2:]:
            c.start()
    for c in out_copies:
        c.wait()


def own_kernel(own_hbm, v_hbm, done_ref, v_ref, own_ref, acc_ref, sem):
    rows = v_hbm.shape[0]
    blocks = rows // 256
    at = [pl.ds(b * 256, 256) for b in range(blocks)]
    copies = [pltpu.make_async_copy(own_hbm, own_ref, sem.at[blocks])]
    copies += [pltpu.make_async_copy(v_hbm.at[s], v_ref.at[s], sem.at[b]) for b, s in enumerate(at)]
    for c in copies:
        c.start()
    copies[0].wait()
    turned = own_ref[...].T
    for b in range(blocks):
        copies[1 + b].wait()
        mine = slice(b * 256, (b + 1) * 256)
        product = dot(turned[:, mine], v_ref[mine, :])
        acc_ref[...] = product if b == 0 else acc_ref[...] + product
    done_ref[...] = acc_ref[...].T.astype(jnp.bfloat16)


def other_kernel(done_ref, other_ref, v_ref, out_ref):
    half = other_ref.shape[1]
    cols = v_ref.shape[1]
    turned = other_ref[...].T
    out_ref[:, :half] = done_ref[...]
    for at in range(0, cols, 256):
        mine = slice(at, at + 256)
        out_ref[mine, half:] = dot(turned, v_ref[:, mine]).T.astype(jnp.bfloat16)


def mix_kernel(col_ref, mark_ref, parts_ref, factor_ref, out_ref):
    total = jnp.sum(parts_ref[...].astype(jnp.float32), axis=0)
    half = total.shape[1] // 2
    swap = col_ref[0] == 1
    total = jnp.where(swap, pltpu.roll(total, half, 1), total)
    mixed = dot(total, factor_ref[...], precision=lax.Precision.HIGHEST)
    mixed = jnp.where(swap, pltpu.roll(mixed, half, 1), mixed).astype(jnp.bfloat16)
    out_ref[...] = jnp.broadcast_to(mixed[None], out_ref.shape)


def main_kernel(parts, col_ref, mix_ref, weight_ref, own_ref, other_ref, *refs):
    n_parts = len(parts)
    u_hbms, t_hbms = refs[:n_parts], refs[n_parts : 2 * n_parts]
    v_hbm, vectors_hbm, own_out, other_out = refs[2 * n_parts : 2 * n_parts + 4]
    mt_ref, v_ref, u_ref, t_ref, r_ref, d_ref, v_sem, u_sem, out_sem = refs[2 * n_parts + 4 :]
    rows, cols = v_hbm.shape
    blocks = rows // 256
    order = [(g, p, at) for p, part in enumerate(parts) for at, g in enumerate(part)]
    v_copies, out_copies, u_copies = [], [], []
    for b in range(blocks):
        at = pl.ds(b * 256, 256)
        v_copies.append(pltpu.make_async_copy(v_hbm.at[at], v_ref.at[at], v_sem.at[b]))
        out_copies.append(pltpu.make_async_copy(r_ref.at[at], vectors_hbm.at[at], out_sem.at[b]))
    for n, (_, p, at) in enumerate(order):
        u_copies.append(
            [
                pltpu.make_async_copy(u_hbms[p].at[at], u_ref.at[n], u_sem.at[0, n]),
                pltpu.make_async_copy(t_hbms[p].at[at], t_ref.at[n], u_sem.at[1, n]),
            ]
        )
    steps = [(n, [b for b in (2 * n, 2 * n + 1) if b < blocks]) for n in range(len(order))]
    for n, bs in steps:
        for c in u_copies[n] + [v_copies[b] for b in bs]:
            c.start()
    mt_ref[...] = mix_ref[...].T
    mix = mt_ref[...]
    weight = weight_ref[...]
    down, along = iota((256, 256), 0), iota((256, 256), 1)
    same_atom = (down & (GROUP - 1)) == (along & (GROUP - 1))
    spread = ((down >> 4) == (along & (NPMAX - 1))).astype(jnp.float32).astype(jnp.bfloat16)
    same_i = (down >> 4) == (along >> 4)

    def rotate(b):
        v_copies[b].wait()
        at = slice(b * 256, (b + 1) * 256)
        panel = jnp.concatenate([own_ref[at, :], other_ref[at, :]], axis=1)
        turned = v_ref[at, :].astype(jnp.float32) - dot(panel, mix)
        r_ref[at, :] = turned.astype(jnp.bfloat16)
        out_copies[b].start()

    def density_of(n):
        for c in u_copies[n]:
            c.wait()
        turned = u_ref[n].astype(jnp.float32) - dot(t_ref[n], mix)
        rounded = turned.astype(jnp.bfloat16)
        weighted = (rounded.astype(jnp.float32) * weight).astype(jnp.bfloat16)
        pairs = jnp.where(same_atom, dot(weighted, rounded, NT), 0.0)
        high = pairs.astype(jnp.bfloat16)
        low = (pairs - high.astype(jnp.float32)).astype(jnp.bfloat16)
        spreaded = jnp.where(same_i, dot(high, spread) + dot(low, spread), 0.0)
        total = spreaded[:GROUP]
        for i in range(1, NPMAX):
            total = total + spreaded[i * GROUP : (i + 1) * GROUP]
        return total

    for n, bs in steps:
        at = order[n][0] * GROUP
        d_ref[at : at + GROUP, :] = density_of(n)
        for b in bs:
            rotate(b)
    per = own_out.shape[0]
    mine = pl.multiple_of(col_ref[0] * per, per)
    own_out[...] = d_ref[pl.ds(mine, per), :]
    other_out[...] = d_ref[pl.ds(per - mine, per), :]
    for c in out_copies:
        c.wait()


VMEM_SPEC = pl.BlockSpec(memory_space=VM)
SMEM_SPEC = pl.BlockSpec(memory_space=SM)
HBM_SPEC = pl.BlockSpec(memory_space=pltpu.MemorySpace.HBM)
BF16, F32 = jnp.bfloat16, jnp.float32


def in_hbm(x):
    return pltpu.with_memory_space_constraint(x, pltpu.MemorySpace.HBM)


def call(kernel, out_shape, in_specs, out_specs, flops, nbytes, mib, **kw):
    return pl.pallas_call(
        kernel,
        out_shape=out_shape,
        in_specs=in_specs,
        out_specs=out_specs,
        compiler_params=pltpu.CompilerParams(vmem_limit_bytes=mib * MIB),
        cost_estimate=pl.CostEstimate(flops=flops, bytes_accessed=nbytes, transcendentals=0),
        **kw,
    )


def partial_sums(panel, other, v_hbm):
    rows, cols = v_hbm.shape
    half = panel.shape[1]
    work = 2 * rows * cols * half
    done, v_vmem = call(
        own_kernel,
        [pltpu.VMEM((cols, half), BF16), pltpu.VMEM((rows, cols), BF16)],
        [HBM_SPEC, HBM_SPEC],
        [VMEM_SPEC, VMEM_SPEC],
        work,
        5 << 20,
        24,
        scratch_shapes=[
            pltpu.VMEM((rows, half), BF16),
            pltpu.VMEM((half, cols), F32),
            pltpu.SemaphoreType.DMA((rows // 256 + 1,)),
        ],
    )(in_hbm(panel), v_hbm)
    return call(
        other_kernel,
        jax.ShapeDtypeStruct((cols, 2 * half), BF16),
        [VMEM_SPEC] * 3,
        VMEM_SPEC,
        work,
        5 << 20,
        24,
    )(done, other, v_vmem)


def rims(counts, v_hbm, panel, other, partial):
    cols, width = v_hbm.shape[1], v_hbm.shape[1] + 2 * panel.shape[1]
    return call(
        halo_kernel,
        [jax.ShapeDtypeStruct((EDGE, width), BF16)] * 2,
        [SMEM_SPEC] + [HBM_SPEC] * 4,
        [VMEM_SPEC, VMEM_SPEC],
        1 << 26,
        2 << 20,
        16,
        scratch_shapes=[pltpu.VMEM((2, TAIL, width), BF16), pltpu.SemaphoreType.DMA((2, 3))],
    )(counts, v_hbm, panel, other, partial)


def couple(which, counts, present, proj_count, blocks, halos, v_hbm, panel, other):
    rows, cols = v_hbm.shape
    npan = 2 * panel.shape[1]
    atoms = counts.shape[0]
    n = len(which)

    def kernel(counts_ref, present_ref, proj_ref, cm_ref, *rest):
        ends = rest[: len(halos)] if halos else (None, None)
        pre_kernel(which, counts_ref, present_ref, proj_ref, cm_ref, *ends, *rest[len(halos) :])

    return call(
        kernel,
        [
            pltpu.HBM((n, 256, cols), BF16),
            pltpu.HBM((n, 256, npan), BF16),
            jax.ShapeDtypeStruct((1,), jnp.int32),
        ],
        [SMEM_SPEC] + [VMEM_SPEC] * (3 + len(halos)) + [HBM_SPEC] * 3,
        [HBM_SPEC, HBM_SPEC, SMEM_SPEC],
        n * 2 * 256 * WIDE * (WIDE + cols + npan),
        10 << 20,
        28,
        scratch_shapes=[
            pltpu.SMEM((atoms + 2 * RIM,), jnp.int32),
            pltpu.VMEM((n, 256, WIDE), BF16),
            pltpu.VMEM((16, atoms), F32),
            pltpu.VMEM((atoms, 16), F32),
            pltpu.VMEM((rows + 2 * EDGE, cols), BF16),
            pltpu.VMEM((rows + 2 * EDGE, npan), BF16),
            pltpu.VMEM((n, 256, cols), BF16),
            pltpu.VMEM((n, 256, npan), BF16),
            pltpu.SemaphoreType.DMA((3,)),
            pltpu.SemaphoreType.DMA((2, n)),
        ],
    )(counts, present, proj_count, blocks, *halos, v_hbm, panel, other)


def mix(col, mark, slices, factor):
    return call(
        mix_kernel,
        jax.ShapeDtypeStruct(slices.shape, BF16),
        [SMEM_SPEC, SMEM_SPEC, VMEM_SPEC, VMEM_SPEC],
        VMEM_SPEC,
        1 << 24,
        1 << 20,
        8,
    )(col, mark, slices, factor)


def finish(parts, col, mixing, weights, panel, other, us, ts, v_hbm):
    rows, cols = v_hbm.shape
    npan = 2 * panel.shape[1]
    groups = sum(len(p) for p in parts)
    atoms = groups * GROUP
    return call(
        functools.partial(main_kernel, parts),
        [
            jax.ShapeDtypeStruct((rows, cols), BF16),
            jax.ShapeDtypeStruct((atoms // 2, 256), F32),
            jax.ShapeDtypeStruct((atoms // 2, 256), F32),
        ],
        [SMEM_SPEC] + [VMEM_SPEC] * 4 + [HBM_SPEC] * (2 * len(parts) + 1),
        [HBM_SPEC, VMEM_SPEC, VMEM_SPEC],
        6 << 30,
        14 << 20,
        28,
        scratch_shapes=[
            pltpu.VMEM((npan, cols), BF16),
            pltpu.VMEM((rows, cols), BF16),
            pltpu.VMEM((groups, 256, cols), BF16),
            pltpu.VMEM((groups, 256, npan), BF16),
            pltpu.VMEM((rows, cols), BF16),
            pltpu.VMEM((atoms, 256), F32),
            pltpu.SemaphoreType.DMA((rows // 256,)),
            pltpu.SemaphoreType.DMA((2, groups)),
            pltpu.SemaphoreType.DMA((rows // 256,)),
        ],
    )(col, mixing, weights, panel, other, *us, *ts, v_hbm)


def local(
    vectors_in, panel, factor, atom_basis, proj_count, coupling, block_present, occ_mask, occ_weight
):
    cols = vectors_in.shape[1]
    npan = 2 * panel.shape[1]
    counts = atom_basis[0]
    groups = counts.shape[0] // GROUP
    n_row = lax.axis_size("row")
    n_col = lax.axis_size("col")
    col = lax.axis_index("col")[None]
    v_hbm = in_hbm(vectors_in)

    other = lax.ppermute(panel, "col", [(0, 1), (1, 0)])
    partial = partial_sums(panel, other, v_hbm)
    slices = lax.all_to_all(partial, "row", 0, 0, tiled=True)
    slices = slices.reshape(n_row, cols // n_row, npan)

    to_next, to_last = rims(counts, v_hbm, panel, other, partial)
    up = [(i, (i + 1) % n_row) for i in range(n_row)]
    before = lax.ppermute(to_next, "row", up)
    after = lax.ppermute(to_last, "row", [(j, i) for i, j in up])

    early = list(range(1, groups // 2))
    late = list(range(groups // 2, groups)) + [0]
    shared = (counts, block_present.T, proj_count[None, :], coupling.transpose(1, 0, 2))
    u_early, t_early, mark = couple(early, *shared, (), v_hbm, panel, other)
    copies = mix(col, mark, slices, factor)
    mixing = lax.all_to_all(copies.reshape(cols, npan), "row", 0, 0, tiled=True)
    u_late, t_late, _ = couple(late, *shared, (before, after), v_hbm, panel, other)

    weights = (occ_mask.astype(F32) * occ_weight / (cols * n_col))[None, :]
    us, ts = [in_hbm(u_early), in_hbm(u_late)], [in_hbm(t_early), in_hbm(t_late)]
    vectors, own_part, other_part = finish(
        (early, late), col, mixing, weights, panel, other, us, ts, v_hbm
    )
    density = own_part + lax.ppermute(other_part, "col", [(0, 1), (1, 0)])
    return vectors, density


def solution(mesh):
    placed = (
        P("row", "col"),
        P("row", "col"),
        P(),
        P("row", None),
        P("row"),
        P("row", None, None),
        P("row", None),
        P("col"),
        P("col"),
    )
    return jax.shard_map(
        local,
        mesh=mesh,
        in_specs=placed,
        out_specs=(P("row", "col"), P(("row", "col"), None)),
        check_vma=False,
    )
```

time: 88.3 us -> 67.8 us (0.77)
  waiting for transfers between devices: 19.2 us -> 3.93 us
  local copies, waits for them, and re-layouts: 2.07 us -> 0.04 us
  other arithmetic: 2.31 us -> 0.64 us
  starting transfers between devices: 27.8 us -> 26.8 us
    ppermute x1, waiting for transfers between devices: 13.4 us -> 0.01 us  [local(): before = lax.ppermute(to_next, 'row', up)]
    ppermute x1, waiting for transfers between devices: 4.18 us -> 0.01 us  [local(): after = lax.ppermute(to_last, 'row', [(j, i) for i, j in up])]
    all_to_all x1, waiting for transfers between devices: 0.01 us -> 3.02 us  [local(): mixing = lax.all_to_all(copies.reshape(cols, npan), 'row', 0, 0, tiled=True)]
    ppermute x1, starting transfers between devices: 7 us -> 5.88 us  [local(): after = lax.ppermute(to_last, 'row', [(j, i) for i, j in up])]
    unnamed x20 -> x16, local copies, waits for them, and re-layouts: 1.08 us -> 0.04 us
    select_n x1 -> x0, other arithmetic: 1.01 us -> none  [local(): ordered = jnp.where(col == 0, factor, flipped)]
    slice x1 -> x0, local copies, waits for them, and re-layouts: 0.99 us -> none  [local(): flipped = jnp.roll(jnp.roll(factor, half, axis=0), half, axis=1)]
    pallas_call x6 -> x7, Pallas kernels: 35.7 us -> 35.2 us  [the longest x2 15.9 us: couple(): call(kernel, [pltpu.HBM((n, 256, cols), BF16), pltpu.HBM((n, 256, npan),...]
  transfers between devices with their start and end apart: 6 -> 6, of which waited for: 4 -> 2; matrix products, arithmetic and copies ran while one was open for 3% -> 0% of each run, Pallas kernels for 20% -> 34%
where the time goes in v3:
time: 67.8 us; the launch traced here: 67.4 us
  Pallas kernels  35.2 us (52%)
  starting transfers between devices  26.8 us (40%)
  waiting for transfers between devices  3.93 us (6%)
  between operations  0.81 us (1%)
    pallas_call x2, Pallas kernels, couple(): call(kernel, [pltpu.HBM((n, 256, cols), BF16), pltpu.HBM((n, 256, npan),...  15.9 us
    all_to_all x1, starting transfers between devices, local(): slices = lax.all_to_all(partial, 'row', 0, 0, tiled=True)  11.3 us
    pallas_call x1, Pallas kernels, finish(): call(functools.partial(main_kernel, parts), [jax.ShapeDtypeStruct((rows,...  10.7 us
    ppermute x1, starting transfers between devices, local(): after = lax.ppermute(to_last, 'row', [(j, i) for i, j in up])  5.88 us
    all_to_all x1, starting transfers between devices, local(): mixing = lax.all_to_all(copies.reshape(cols, npan), 'row', 0, 0, tiled=True)  4.63 us
    all_to_all x1, waiting for transfers between devices, local(): mixing = lax.all_to_all(copies.reshape(cols, npan), 'row', 0, 0, tiled=True)  3.02 us
    pallas_call x1, Pallas kernels, partial_sums(): call(own_kernel, [pltpu.VMEM((cols, half), BF16), pltpu.VMEM((rows, cols)...  2.69 us
    pallas_call x1, Pallas kernels, rims(): call(halo_kernel, [jax.ShapeDtypeStruct((EDGE, width), BF16)] * 2, [SMEM_...  2.57 us
  transfers between devices with their start and end apart: 6, of which 2 were waited for; matrix products, arithmetic and copies ran while one was open for 0% of the time, Pallas kernels for 34%

profile of v3, /device:TPU:1, one launch (start us, length us, event | category | flops | bytes accessed | tf_op | source)
XLA Modules:
  0.0 67.4 jit_solution(13971736614972004016)
XLA Ops:
  0.6 1.5 %collective-permute-start = (bf16[2048,128]{1,0:T(8,128)(2,1)}, bf16[2048,128]{1,0:T(8,128)(2,1)S(1)}, u32[]{:S(2)}, u32[]{:S(2)}) collective-permute-start(bf16[2048,128]{1,0:T(8,128)(2,1)} %own_ref.1), channel_id=1, source_target_pairs={{0,1},{1,0},{2,3},{3,2},{4,5},{5,4},{6,7},{7,6},{8,9},{9,8},{10,11... | collective-permute-start | bytes 1572872 | tf_op jit(solution)/shard_map/ppermute | solution.py:458
  2.1 2.7 %shard_map.105 = (bf16[1024,128]{1,0:T(8,128)(2,1)S(1)}, bf16[2048,1024]{1,0:T(8,128)(2,1)S(1)}) custom-call(bf16[2048,128]{1,0:T(8,128)(2,1)} %own_ref.1, bf16[2048,1024]{1,0:T(8,128)(2,1)} %refs_4_.1), custom_call_target="tpu_custom_call" | custom-call | flops 536870912 | bytes 5242880 | tf_op jit(solution)/shard_map/pallas_call | solution.py:327
  4.8 0.0 copy-start
  4.8 0.0 copy-start.2
  4.8 0.0 collective-permute-done.rest_2_.other_ref.other_hbm.rest_4_
  4.9 1.6 %shard_map.106.partial_hbm = bf16[1024,256]{1,0:T(8,128)(2,1)} custom-call(bf16[1024,128]{1,0:T(8,128)(2,1)S(1)} %get-tuple-element.15.done_ref, bf16[2048,128]{1,0:T(8,128)(2,1)S(1)} %collective-permute-done.rest_2_.other_ref.other_hbm.rest_4_, bf16[2048,1024]{1,0:T(8,128)(2,1)S(1)} %get-tuple-element.16.v_ref), custom_call_target="tpu_custom_call" | custom-call | flops 536870912 | bytes 5242880 | tf_op jit(solution)/shard_map/pallas_call | solution.py:341
  6.5 11.3 %all-to-all-start = ((bf16[64,16,256]{2,1,0:T(8,128)(2,1)}), bf16[64,16,256]{2,1,0:T(8,128)(2,1)S(1)}, u32[]{:S(2)}, u32[]{:S(2)}) async-start(bf16[64,16,256]{2,1,0:T(8,128)(2,1)} %bitcast.5), calls=%async_computation | async-start | bytes 1048576 | tf_op jit(solution)/shard_map/all_to_all | solution.py:460
  17.8 0.0 copy-done
  17.8 0.0 copy-done.2
  17.9 2.6 %shard_map.108 = (bf16[96,1280]{1,0:T(8,128)(2,1)}, bf16[96,1280]{1,0:T(8,128)(2,1)S(1)}) custom-call(s32[128]{0:T(128)S(1)} %bitcast.10, bf16[2048,1024]{1,0:T(8,128)(2,1)} %refs_4_.1, bf16[2048,128]{1,0:T(8,128)(2,1)S(1)} %copy-done, bf16[2048,128]{1,0:T(8,128)(2,1)S(1)} %collective-permute-done.rest_2_.other_ref.other_hbm.rest_4_, ...), custom_call_target="tpu_custom_call" | custom-call | flops 67108864 | bytes 2097152 | tf_op jit(solution)/shard_map/pallas_call | solution.py:354
  20.4 0.0 copy-start.1
  20.4 1.1 %collective-permute-start.1 = (bf16[96,1280]{1,0:T(8,128)(2,1)}, bf16[96,1280]{1,0:T(8,128)(2,1)S(1)}, u32[]{:S(2)}, u32[]{:S(2)}) collective-permute-start(bf16[96,1280]{1,0:T(8,128)(2,1)} %get-tuple-element.18), channel_id=1, source_target_pairs={{0,2},{2,4},{4,6},{6,8},{8,10},{10,12},{12,14},{14,16},{16,18},{18... | collective-permute-start | bytes 737288 | tf_op jit(solution)/shard_map/ppermute | solution.py:465
  21.5 5.9 %collective-permute-start.2 = (bf16[96,1280]{1,0:T(8,128)(2,1)S(1)}, bf16[96,1280]{1,0:T(8,128)(2,1)S(1)}, u32[]{:S(2)}, u32[]{:S(2)}) collective-permute-start(bf16[96,1280]{1,0:T(8,128)(2,1)S(1)} %get-tuple-element.19), channel_id=1, source_target_pairs={{2,0},{4,2},{6,4},{8,6},{10,8},{12,10},{14,12},{16,14},{18,16},{20... | collective-permute-start | bytes 737288 | tf_op jit(solution)/shard_map/ppermute | solution.py:466
  27.4 0.0 copy-done.3
  27.4 0.0 copy-done.4
  27.4 0.0 copy-done.5
  27.4 0.0 copy-start.7
  27.4 6.9 %shard_map.104 = (bf16[3,256,1024]{2,1,0:T(8,128)(2,1)}, bf16[3,256,256]{2,1,0:T(8,128)(2,1)}, s32[1]{0:T(128)}) custom-call(s32[128]{0:T(128)S(1)} %bitcast.11, s32[9,128]{1,0:T(8,128)S(1)} %bitcast.15, s32[1,128]{1,0:T(1,128)S(1)} %bitcast.17, bf16[9,128,384]{2,1,0:T(8,128)(2,1)S(1)} %bitcast.13, bf16[2048,1024]{1,0:T(8,128)(2,1)} %refs_4_.1, ...), custom_call_target="tpu_custom_call" | custom-call | flops 1887436800 | bytes 10485760 | tf_op jit(solution)/shard_map/pallas_call | solution.py:376
  34.4 0.0 all-to-all-done.parts_ref
  34.4 0.0 copy-done.1
  34.4 1.8 %shard_map.107 = bf16[64,16,256]{2,1,0:T(8,128)(2,1)} custom-call(s32[1]{0:T(128)} %bitcast.col_ref, s32[1]{0:T(128)} %get-tuple-element.14.mark_ref, bf16[64,16,256]{2,1,0:T(8,128)(2,1)S(1)} %all-to-all-done.parts_ref, f32[256,256]{1,0:T(8,128)S(1)} %copy-done.1), custom_call_target="tpu_custom_call" | custom-call | flops 16777216 | bytes 1048576 | tf_op jit(solution)/shard_map/pallas_call | solution.py:404
  36.2 4.6 %all-to-all-start.1 = ((bf16[64,16,256]{2,1,0:T(8,128)(2,1)}), bf16[64,16,256]{2,1,0:T(8,128)(2,1)S(1)}, u32[]{:S(2)}, u32[]{:S(2)}) async-start(bf16[64,16,256]{2,1,0:T(8,128)(2,1)} %shard_map.107), calls=%async_computation.1 | async-start | bytes 1048576 | tf_op jit(solution)/shard_map/all_to_all | solution.py:473
  40.8 0.0 copy-done.6
  40.9 0.0 copy-done.7
  40.9 0.0 collective-permute-done.1.rest_0_
  40.9 0.0 collective-permute-done.2.rest_1_
  40.9 8.9 %shard_map.109 = (bf16[5,256,1024]{2,1,0:T(8,128)(2,1)}, bf16[5,256,256]{2,1,0:T(8,128)(2,1)}, s32[1]{0:T(128)}) custom-call(s32[128]{0:T(128)S(1)} %bitcast.12, s32[9,128]{1,0:T(8,128)S(1)} %bitcast.16, s32[1,128]{1,0:T(1,128)S(1)} %bitcast.18, bf16[9,128,384]{2,1,0:T(8,128)(2,1)S(1)} %bitcast.14, bf16[96,1280]{1,0:T(8,128)(2,1)S(1)} %collective-permute-done.1.rest_0_, ...), custom_call_target="tpu_custom_call" | custom-call | flops 3145728000 | bytes 10485760 | tf_op jit(solution)/shard_map/pallas_call | solution.py:376
  49.8 3.0 %all-to-all-done.1 = bf16[64,16,256]{2,1,0:T(8,128)(2,1)S(1)} async-done(((bf16[64,16,256]{2,1,0:T(8,128)(2,1)}), bf16[64,16,256]{2,1,0:T(8,128)(2,1)S(1)}, u32[]{:S(2)}, u32[]{:S(2)}) %all-to-all-start.1) | async-done | bytes 524320 | tf_op jit(solution)/shard_map/all_to_all | solution.py:473
  52.8 10.7 %shard_map.110 = (bf16[2048,1024]{1,0:T(8,128)(2,1)}, f32[64,256]{1,0:T(8,128)S(1)}, f32[64,256]{1,0:T(8,128)S(1)}) custom-call(s32[1]{0:T(128)} %bitcast.col_ref, bf16[1024,256]{1,0:T(8,128)(2,1)S(1)} %bitcast.8, f32[1,1024]{1,0:T(1,128)S(1)} %bitcast.9, bf16[2048,128]{1,0:T(8,128)(2,1)S(1)} %copy-done, ...), custom_call_target="tpu_custom_call" | custom-call | flops 6442450944 | bytes 14680064 | tf_op jit(solution)/shard_map/pallas_call | solution.py:420
  63.5 2.4 %collective-permute-start.3 = (f32[64,256]{1,0:T(8,128)S(1)}, f32[64,256]{1,0:T(8,128)S(1)}, u32[]{:S(2)}, u32[]{:S(2)}) collective-permute-start(f32[64,256]{1,0:T(8,128)S(1)} %get-tuple-element.25), channel_id=1, source_target_pairs={{0,1},{1,0},{2,3},{3,2},{4,5},{5,4},{6,7},{7,6},{8,9},{9,8},{10,11... | collective-permute-start | bytes 196616 | tf_op jit(solution)/shard_map/ppermute | solution.py:481
  65.9 0.9 %collective-permute-done.3 = f32[64,256]{1,0:T(8,128)S(1)} collective-permute-done((f32[64,256]{1,0:T(8,128)S(1)}, f32[64,256]{1,0:T(8,128)S(1)}, u32[]{:S(2)}, u32[]{:S(2)}) %collective-permute-start.3) | collective-permute-done | bytes 65568 | tf_op jit(solution)/shard_map/ppermute | solution.py:481
  66.8 0.6 add.3
  (5 shorter events, 0.0 us)
Async XLA Ops:
  0.6 4.2 %collective-permute-start = (bf16[2048,128]{1,0:T(8,128)(2,1)}, bf16[2048,128]{1,0:T(8,128)(2,1)S(1)}, u32[]{:S(2)}, u32[]{:S(2)}) collective-permute-start(bf16[2048,128]{1,0:T(8,128)(2,1)} %own_ref.1), channel_id=1, source_target_pairs={{0,1},{1,0},{2,3},{3,2},{4,5},{5,4},{6,7},{7,6},{8,9},{9,8},{10,11... | collective-permute-start | bytes 1572872 | tf_op jit(solution)/shard_map/ppermute | solution.py:458
  4.8 13.0 %copy-start = (bf16[2048,128]{1,0:T(8,128)(2,1)S(1)}, bf16[2048,128]{1,0:T(8,128)(2,1)}, u32[]{:S(2)}) copy-start(bf16[2048,128]{1,0:T(8,128)(2,1)} %own_ref.1) | copy-start | bytes 1572868
  4.8 13.0 %copy-start.2 = (s32[1,128]{1,0:T(1,128)S(1)}, s32[1,128]{1,0:T(1,128)}, u32[]{:S(2)}) copy-start(s32[1,128]{1,0:T(1,128)} %param.12) | copy-start | bytes 1540
  6.5 20.9 %copy-start.3 = (bf16[128,9,384]{2,0,1:T(8,128)(2,1)S(1)}, bf16[128,9,384]{2,0,1:T(8,128)(2,1)}, u32[]{:S(2)}) copy-start(bf16[128,9,384]{2,0,1:T(8,128)(2,1)} %param.14) | copy-start | bytes 2654212
  6.5 20.9 %copy-start.4 = (s32[128,9]{0,1:T(8,128)S(1)}, s32[128,9]{0,1:T(8,128)}, u32[]{:S(2)}) copy-start(s32[128,9]{0,1:T(8,128)} %param.15) | copy-start | bytes 13828
  6.5 20.9 %copy-start.5 = (s32[128]{0:T(128)S(1)}, s32[128]{0:T(128)}, u32[]{:S(2)}) copy-start(s32[128]{0:T(128)} %param.13) | copy-start | bytes 1540
  6.5 27.9 %all-to-all-start = ((bf16[64,16,256]{2,1,0:T(8,128)(2,1)}), bf16[64,16,256]{2,1,0:T(8,128)(2,1)S(1)}, u32[]{:S(2)}, u32[]{:S(2)}) async-start(bf16[64,16,256]{2,1,0:T(8,128)(2,1)} %bitcast.5), calls=%async_computation | async-start | bytes 1048576 | tf_op jit(solution)/shard_map/all_to_all | solution.py:460
  20.4 14.0 %copy-start.1 = (f32[256,256]{1,0:T(8,128)S(1)}, f32[256,256]{1,0:T(8,128)}, u32[]{:S(2)}) copy-start(f32[256,256]{1,0:T(8,128)} %factor_ref.1) | copy-start | bytes 786436
  20.4 20.4 %collective-permute-start.1 = (bf16[96,1280]{1,0:T(8,128)(2,1)}, bf16[96,1280]{1,0:T(8,128)(2,1)S(1)}, u32[]{:S(2)}, u32[]{:S(2)}) collective-permute-start(bf16[96,1280]{1,0:T(8,128)(2,1)} %get-tuple-element.18), channel_id=1, source_target_pairs={{0,2},{2,4},{4,6},{6,8},{8,10},{10,12},{12,14},{14,16},{16,18},{18... | collective-permute-start | bytes 737288 | tf_op jit(solution)/shard_map/ppermute | solution.py:465
  21.5 19.4 %collective-permute-start.2 = (bf16[96,1280]{1,0:T(8,128)(2,1)S(1)}, bf16[96,1280]{1,0:T(8,128)(2,1)S(1)}, u32[]{:S(2)}, u32[]{:S(2)}) collective-permute-start(bf16[96,1280]{1,0:T(8,128)(2,1)S(1)} %get-tuple-element.19), channel_id=1, source_target_pairs={{2,0},{4,2},{6,4},{8,6},{10,8},{12,10},{14,12},{16,14},{18,16},{20... | collective-permute-start | bytes 737288 | tf_op jit(solution)/shard_map/ppermute | solution.py:466
  27.4 13.4 %copy-start.6 = (f32[1024]{0:T(1024)S(1)}, f32[1024]{0:T(1024)}, u32[]{:S(2)}) copy-start(f32[1024]{0:T(1024)} %param.17) | copy-start | bytes 12292
  27.4 13.4 %copy-start.7 = (s32[1024]{0:T(1024)S(1)}, s32[1024]{0:T(1024)}, u32[]{:S(2)}) copy-start(s32[1024]{0:T(1024)} %param.16) | copy-start | bytes 12292
  36.2 16.6 %all-to-all-start.1 = ((bf16[64,16,256]{2,1,0:T(8,128)(2,1)}), bf16[64,16,256]{2,1,0:T(8,128)(2,1)S(1)}, u32[]{:S(2)}, u32[]{:S(2)}) async-start(bf16[64,16,256]{2,1,0:T(8,128)(2,1)} %shard_map.107), calls=%async_computation.1 | async-start | bytes 1048576 | tf_op jit(solution)/shard_map/all_to_all | solution.py:473
  63.5 3.3 %collective-permute-start.3 = (f32[64,256]{1,0:T(8,128)S(1)}, f32[64,256]{1,0:T(8,128)S(1)}, u32[]{:S(2)}, u32[]{:S(2)}) collective-permute-start(f32[64,256]{1,0:T(8,128)S(1)} %get-tuple-element.25), channel_id=1, source_target_pairs={{0,1},{1,0},{2,3},{3,2},{4,5},{5,4},{6,7},{7,6},{8,9},{9,8},{10,11... | collective-permute-start | bytes 196616 | tf_op jit(solution)/shard_map/ppermute | solution.py:481

commit v4 on v3

--- a/solution.py
+++ b/solution.py
@@ -33,7 +33,7 @@
     return lax.broadcasted_iota(jnp.int32, shape, dim)
 
 
-def padded_rows(counts_ref, first_atom, first_row, source):
+def padded_rows(counts_ref, first_atom, first_row, sources):
     slot = iota((EDGE, 1), 0)
     target = jnp.full((EDGE, 1), -1, jnp.int32)
     row = first_row
@@ -43,38 +43,28 @@
         target = jnp.where((u >= 0) & (u < count), row + u, target)
         row = row + count
     pick = (iota((EDGE, TAIL), 1) == target).astype(jnp.float32).astype(jnp.bfloat16)
-    return dot(pick, source).astype(jnp.bfloat16)
-
-
-def halo_kernel(
-    counts_ref, v_hbm, own_hbm, other_hbm, partial_hbm, to_next, to_last, rows_ref, sem
-):
+    return [dot(pick, source).astype(jnp.bfloat16) for source in sources]
+
+
+def fill_rims(counts_ref, e_ref, p_ref, to_next, to_last):
     atoms = counts_ref.shape[0]
-    rows, cols = v_hbm.shape
-    half = own_hbm.shape[1]
-    spans = ((0, cols), (cols, half), (cols + half, half))
-    copies = []
-    for n, first in enumerate((0, rows - TAIL)):
-        for m, (src, (at, width)) in enumerate(zip((v_hbm, own_hbm, other_hbm), spans)):
-            copies.append(
-                pltpu.make_async_copy(
-                    src.at[pl.ds(first, TAIL)],
-                    rows_ref.at[n, :, pl.ds(at, width)],
-                    sem.at[n, m],
-                )
-            )
-            copies[-1].start()
+    cols = e_ref.shape[1]
+    end = e_ref.shape[0] - EDGE
     tail = counts_ref[atoms - 1]
     for t in range(1, RIM):
         tail = tail + counts_ref[atoms - 1 - t]
-    for c in copies:
-        c.wait()
-    to_next[...] = padded_rows(counts_ref, atoms - RIM, TAIL - tail, rows_ref[1])
-    to_last[...] = padded_rows(counts_ref, 0, 0, rows_ref[0])
+    for out, atom, row, at in (
+        (to_next, atoms - RIM, TAIL - tail, slice(end - TAIL, end)),
+        (to_last, 0, 0, slice(EDGE, EDGE + TAIL)),
+    ):
+        pieces = padded_rows(counts_ref, atom, row, [e_ref[at, :], p_ref[at, :]])
+        out[:, :cols] = pieces[0]
+        out[:, cols:] = pieces[1]
 
 
 def pre_kernel(
     which_groups,
+    rim_refs,
     counts_ref,
     present_ref,
     proj_ref,
@@ -138,6 +128,22 @@
     which = lane // BMAX
     slot = lane - which * BMAX
     sub = iota((GROUP, lanes), 1) // BMAX
+    starts, bands = [], []
+
+    def multiply(n):
+        if n == 0:
+            for c in copies:
+                c.wait()
+            if rim_refs is not None:
+                fill_rims(counts_ref, e_ref, p_ref, *rim_refs)
+        window = pl.ds(pl.multiple_of(starts[n], ALIGN), WIDE)
+        u_ref[n] = dot(bands[n], e_ref[window, :]).astype(jnp.bfloat16)
+        t_ref[n] = dot(bands[n], p_ref[window, :]).astype(jnp.bfloat16)
+        out_copies.append(pltpu.make_async_copy(u_ref.at[n], u_hbm.at[n], out_sem.at[0, n]))
+        out_copies.append(pltpu.make_async_copy(t_ref.at[n], t_hbm.at[n], out_sem.at[1, n]))
+        for c in out_copies[-2:]:
+            c.start()
+
     for n, g in enumerate(which_groups):
         mine = slice(g * GROUP, (g + 1) * GROUP)
         first = pos_ref[g * GROUP]
@@ -177,17 +183,9 @@
                 halves = [pltpu.roll(h, 0, 1, stride=BMAX // 2, stride_axis=0) for h in halves]
             skew = jnp.concatenate(halves, axis=0)
             cp_ref[n, i * GROUP : (i + 1) * GROUP, :] = skew.astype(jnp.bfloat16)
-        band = dot(cp_ref[n], pick, NT).astype(jnp.bfloat16)
-        if n == 0:
-            for c in copies:
-                c.wait()
-        window = pl.ds(pl.multiple_of(start, ALIGN), WIDE)
-        u_ref[n] = dot(band, e_ref[window, :]).astype(jnp.bfloat16)
-        t_ref[n] = dot(band, p_ref[window, :]).astype(jnp.bfloat16)
-        out_copies.append(pltpu.make_async_copy(u_ref.at[n], u_hbm.at[n], out_sem.at[0, n]))
-        out_copies.append(pltpu.make_async_copy(t_ref.at[n], t_hbm.at[n], out_sem.at[1, n]))
-        for c in out_copies[-2:]:
-            c.start()
+        bands.append(dot(cp_ref[n], pick, NT).astype(jnp.bfloat16))
+        starts.append(start)
+        multiply(n)
     for c in out_copies:
         c.wait()
 
@@ -220,7 +218,9 @@
         out_ref[mine, half:] = dot(turned, v_ref[:, mine]).T.astype(jnp.bfloat16)
 
 
-def mix_kernel(col_ref, mark_ref, parts_ref, factor_ref, out_ref):
+def mix_kernel(col_ref, mark_ref, parts_ref, factor_ref, rim_ref, out_ref, rim_out, sem):
+    passing = pltpu.make_async_copy(rim_ref, rim_out, sem)
+    passing.start()
     total = jnp.sum(parts_ref[...].astype(jnp.float32), axis=0)
     half = total.shape[1] // 2
     swap = col_ref[0] == 1
@@ -228,6 +228,7 @@
     mixed = dot(total, factor_ref[...], precision=lax.Precision.HIGHEST)
     mixed = jnp.where(swap, pltpu.roll(mixed, half, 1), mixed).astype(jnp.bfloat16)
     out_ref[...] = jnp.broadcast_to(mixed[None], out_ref.shape)
+    passing.wait()
 
 
 def main_kernel(parts, col_ref, mix_ref, weight_ref, own_ref, other_ref, *refs):
@@ -340,7 +341,7 @@
     )(in_hbm(panel), v_hbm)
     return call(
         other_kernel,
-        jax.ShapeDtypeStruct((cols, 2 * half), BF16),
+        pltpu.VMEM((cols, 2 * half), BF16),
         [VMEM_SPEC] * 3,
         VMEM_SPEC,
         work,
@@ -349,29 +350,20 @@
     )(done, other, v_vmem)
 
 
-def rims(counts, v_hbm, panel, other, partial):
-    cols, width = v_hbm.shape[1], v_hbm.shape[1] + 2 * panel.shape[1]
-    return call(
-        halo_kernel,
-        [jax.ShapeDtypeStruct((EDGE, width), BF16)] * 2,
-        [SMEM_SPEC] + [HBM_SPEC] * 4,
-        [VMEM_SPEC, VMEM_SPEC],
-        1 << 26,
-        2 << 20,
-        16,
-        scratch_shapes=[pltpu.VMEM((2, TAIL, width), BF16), pltpu.SemaphoreType.DMA((2, 3))],
-    )(counts, v_hbm, panel, other, partial)
-
-
 def couple(which, counts, present, proj_count, blocks, halos, v_hbm, panel, other):
     rows, cols = v_hbm.shape
     npan = 2 * panel.shape[1]
     atoms = counts.shape[0]
     n = len(which)
 
+    first = not halos
+
     def kernel(counts_ref, present_ref, proj_ref, cm_ref, *rest):
-        ends = rest[: len(halos)] if halos else (None, None)
-        pre_kernel(which, counts_ref, present_ref, proj_ref, cm_ref, *ends, *rest[len(halos) :])
+        ends = (None, None) if first else rest[:2]
+        rest = rest[len(halos) :]
+        rim_refs = rest[6:8] if first else None
+        rest = rest[:6] + rest[8:] if first else rest
+        pre_kernel(which, rim_refs, counts_ref, present_ref, proj_ref, cm_ref, *ends, *rest)
 
     return call(
         kernel,
@@ -379,9 +371,10 @@
             pltpu.HBM((n, 256, cols), BF16),
             pltpu.HBM((n, 256, npan), BF16),
             jax.ShapeDtypeStruct((1,), jnp.int32),
-        ],
+        ]
+        + [jax.ShapeDtypeStruct((EDGE, cols + npan), BF16)] * (2 if first else 0),
         [SMEM_SPEC] + [VMEM_SPEC] * (3 + len(halos)) + [HBM_SPEC] * 3,
-        [HBM_SPEC, HBM_SPEC, SMEM_SPEC],
+        [HBM_SPEC, HBM_SPEC, SMEM_SPEC] + [VMEM_SPEC] * (2 if first else 0),
         n * 2 * 256 * WIDE * (WIDE + cols + npan),
         10 << 20,
         28,
@@ -400,16 +393,17 @@
     )(counts, present, proj_count, blocks, *halos, v_hbm, panel, other)
 
 
-def mix(col, mark, slices, factor):
+def mix(col, mark, slices, factor, rim):
     return call(
         mix_kernel,
-        jax.ShapeDtypeStruct(slices.shape, BF16),
-        [SMEM_SPEC, SMEM_SPEC, VMEM_SPEC, VMEM_SPEC],
-        VMEM_SPEC,
+        [pltpu.VMEM(slices.shape, BF16), pltpu.VMEM(rim.shape, BF16)],
+        [SMEM_SPEC, SMEM_SPEC, VMEM_SPEC, VMEM_SPEC, VMEM_SPEC],
+        [VMEM_SPEC, VMEM_SPEC],
         1 << 24,
         1 << 20,
         8,
-    )(col, mark, slices, factor)
+        scratch_shapes=[pltpu.SemaphoreType.DMA],
+    )(col, mark, slices, factor, rim)
 
 
 def finish(parts, col, mixing, weights, panel, other, us, ts, v_hbm):
@@ -460,16 +454,14 @@
     slices = lax.all_to_all(partial, "row", 0, 0, tiled=True)
     slices = slices.reshape(n_row, cols // n_row, npan)
 
-    to_next, to_last = rims(counts, v_hbm, panel, other, partial)
-    up = [(i, (i + 1) % n_row) for i in range(n_row)]
-    before = lax.ppermute(to_next, "row", up)
-    after = lax.ppermute(to_last, "row", [(j, i) for i, j in up])
-
     early = list(range(1, groups // 2))
     late = list(range(groups // 2, groups)) + [0]
     shared = (counts, block_present.T, proj_count[None, :], coupling.transpose(1, 0, 2))
-    u_early, t_early, mark = couple(early, *shared, (), v_hbm, panel, other)
-    copies = mix(col, mark, slices, factor)
+    u_early, t_early, mark, to_next, to_last = couple(early, *shared, (), v_hbm, panel, other)
+    up = [(i, (i + 1) % n_row) for i in range(n_row)]
+    before = lax.ppermute(to_next, "row", up)
+    copies, to_last = mix(col, mark, slices, factor, to_last)
+    after = lax.ppermute(to_last, "row", [(j, i) for i, j in up])
     mixing = lax.all_to_all(copies.reshape(cols, npan), "row", 0, 0, tiled=True)
     u_late, t_late, _ = couple(late, *shared, (before, after), v_hbm, panel, other)
 

time: 67.8 us -> 65.7 us (0.969)
  waiting for transfers between devices: 3.93 us -> 7.78 us
  starting transfers between devices: 26.8 us -> 23.1 us
  Pallas kernels: 35.2 us -> 33 us
    all_to_all x1, waiting for transfers between devices: 0.01 us -> 4.72 us  [local(): slices = lax.all_to_all(partial, 'row', 0, 0, tiled=True)]
    ppermute x1, starting transfers between devices: 5.88 us -> 1.24 us  [local(): after = lax.ppermute(to_last, 'row', [(j, i) for i, j in up])]
    pallas_call x3 -> x2, Pallas kernels: 5.97 us -> 3.81 us  [the longest x1 2.2 us: mix(): call(mix_kernel, [pltpu.VMEM(slices.shape, BF16), pltpu.VMEM(rim.shape, B...]
    all_to_all x1, waiting for transfers between devices: 3.02 us -> 1.86 us  [local(): mixing = lax.all_to_all(copies.reshape(cols, npan), 'row', 0, 0, tiled=True)]
    ppermute x1, starting transfers between devices: 2.4 us -> 3.28 us  [local(): density = own_part + lax.ppermute(other_part, 'col', [(0, 1), (1, 0)])]
  transfers between devices with their start and end apart: 6 -> 6, of which waited for: 2 -> 4; matrix products, arithmetic and copies ran while one was open for 0% -> 0% of each run, Pallas kernels for 34% -> 32%
where the time goes in v4:
time: 65.7 us; the launch traced here: 65.4 us
  Pallas kernels  33 us (50%)
  starting transfers between devices  23.1 us (35%)
  waiting for transfers between devices  7.78 us (12%)
  between operations  0.83 us (1%)
    pallas_call x2, Pallas kernels, couple(): call(kernel, [pltpu.HBM((n, 256, cols), BF16), pltpu.HBM((n, 256, npan),...  15.8 us
    all_to_all x1, starting transfers between devices, local(): slices = lax.all_to_all(partial, 'row', 0, 0, tiled=True)  11.3 us
    pallas_call x1, Pallas kernels, finish(): call(functools.partial(main_kernel, parts), [jax.ShapeDtypeStruct((rows,...  10.7 us
    all_to_all x1, waiting for transfers between devices, local(): slices = lax.all_to_all(partial, 'row', 0, 0, tiled=True)  4.72 us
    all_to_all x1, starting transfers between devices, local(): mixing = lax.all_to_all(copies.reshape(cols, npan), 'row', 0, 0, tiled=True)  4.63 us
    ppermute x1, starting transfers between devices, local(): density = own_part + lax.ppermute(other_part, 'col', [(0, 1), (1, 0)])  3.28 us
    pallas_call x1, Pallas kernels, partial_sums(): call(own_kernel, [pltpu.VMEM((cols, half), BF16), pltpu.VMEM((rows, cols)...  2.69 us
    pallas_call x1, Pallas kernels, mix(): call(mix_kernel, [pltpu.VMEM(slices.shape, BF16), pltpu.VMEM(rim.shape, B...  2.2 us
  transfers between devices with their start and end apart: 6, of which 4 were waited for; matrix products, arithmetic and copies ran while one was open for 0% of the time, Pallas kernels for 32%

profile of v4, /device:TPU:1, one launch (start us, length us, event | category | flops | bytes accessed | tf_op | source)
XLA Modules:
  0.0 65.4 jit_solution(14718048449600020348)
XLA Ops:
  0.6 1.5 %collective-permute-start = (bf16[2048,128]{1,0:T(8,128)(2,1)}, bf16[2048,128]{1,0:T(8,128)(2,1)S(1)}, u32[]{:S(2)}, u32[]{:S(2)}) collective-permute-start(bf16[2048,128]{1,0:T(8,128)(2,1)} %own_ref.1), channel_id=1, source_target_pairs={{0,1},{1,0},{2,3},{3,2},{4,5},{5,4},{6,7},{7,6},{8,9},{9,8},{10,11... | collective-permute-start | bytes 1572872 | tf_op jit(solution)/shard_map/ppermute | solution.py:452
  2.1 2.7 %shard_map.105 = (bf16[1024,128]{1,0:T(8,128)(2,1)S(1)}, bf16[2048,1024]{1,0:T(8,128)(2,1)S(1)}) custom-call(bf16[2048,128]{1,0:T(8,128)(2,1)} %own_ref.1, bf16[2048,1024]{1,0:T(8,128)(2,1)} %refs_4_.1), custom_call_target="tpu_custom_call" | custom-call | flops 536870912 | bytes 5242880 | tf_op jit(solution)/shard_map/pallas_call | solution.py:328
  4.8 0.0 copy-start
  4.8 0.0 copy-start.2
  4.8 0.0 copy-start.3
  4.9 0.0 copy-start.4
  4.9 0.0 copy-start.5
  4.9 0.0 collective-permute-done.rest_2_.other_ref.rest_4_
  4.9 1.6 %shard_map.106 = bf16[1024,256]{1,0:T(8,128)(2,1)} custom-call(bf16[1024,128]{1,0:T(8,128)(2,1)S(1)} %get-tuple-element.17.done_ref, bf16[2048,128]{1,0:T(8,128)(2,1)S(1)} %collective-permute-done.rest_2_.other_ref.rest_4_, bf16[2048,1024]{1,0:T(8,128)(2,1)S(1)} %get-tuple-element.18.v_ref), custom_call_target="tpu_custom_call" | custom-call | flops 536870912 | bytes 5242880 | tf_op jit(solution)/shard_map/pallas_call | solution.py:342
  6.5 11.3 %all-to-all-start = ((bf16[64,16,256]{2,1,0:T(8,128)(2,1)}), bf16[64,16,256]{2,1,0:T(8,128)(2,1)S(1)}, u32[]{:S(2)}, u32[]{:S(2)}) async-start(bf16[64,16,256]{2,1,0:T(8,128)(2,1)} %bitcast.5), calls=%async_computation | async-start | bytes 1048576 | tf_op jit(solution)/shard_map/all_to_all | solution.py:454
  17.9 0.0 copy-done
  17.9 0.0 copy-done.2
  17.9 0.0 copy-done.3
  17.9 0.0 copy-done.4
  17.9 0.0 copy-done.5
  17.9 0.0 copy-start.6
  17.9 0.0 copy-start.7
  17.9 6.9 %shard_map.104 = (bf16[3,256,1024]{2,1,0:T(8,128)(2,1)}, bf16[3,256,256]{2,1,0:T(8,128)(2,1)}, s32[1]{0:T(128)}, bf16[96,1280]{1,0:T(8,128)(2,1)S(1)}, bf16[96,1280]{1,0:T(8,128)(2,1)S(1)}) custom-call(s32[128]{0:T(128)S(1)} %bitcast.14, s32[9,128]{1,0:T(8,128)S(1)} %bitcast.12, s32[1,128]{1,0:T(1,128)S(1)} %bitcast.16, bf16[9,128,384]{2,1,0:T(8,128)(2,1)S(1)} %bitcast.10, ...), custom_call_target="tpu_custom_call" | custom-call | flops 1887436800 | bytes 10485760 | tf_op jit(solution)/shard_map/pallas_call | solution.py:368
  24.9 1.1 %collective-permute-start.1 = (bf16[96,1280]{1,0:T(8,128)(2,1)S(1)}, bf16[96,1280]{1,0:T(8,128)(2,1)S(1)}, u32[]{:S(2)}, u32[]{:S(2)}) collective-permute-start(bf16[96,1280]{1,0:T(8,128)(2,1)S(1)} %get-tuple-element.22), channel_id=1, source_target_pairs={{0,2},{2,4},{4,6},{6,8},{8,10},{10,12},{12,14},{14,16},{16,18},{18... | collective-permute-start | bytes 737288 | tf_op jit(solution)/shard_map/ppermute | solution.py:462
  25.9 4.7 %all-to-all-done.parts_ref = bf16[64,16,256]{2,1,0:T(8,128)(2,1)S(1)} async-done(((bf16[64,16,256]{2,1,0:T(8,128)(2,1)}), bf16[64,16,256]{2,1,0:T(8,128)(2,1)S(1)}, u32[]{:S(2)}, u32[]{:S(2)}) %all-to-all-start) | async-done | bytes 524320 | tf_op jit(solution)/shard_map/all_to_all | solution.py:454
  30.7 0.0 copy-done.1
  30.7 2.2 %shard_map.107 = (bf16[64,16,256]{2,1,0:T(8,128)(2,1)}, bf16[96,1280]{1,0:T(8,128)(2,1)}) custom-call(s32[1]{0:T(128)} %bitcast.col_ref, s32[1]{0:T(128)} %get-tuple-element.16.mark_ref, bf16[64,16,256]{2,1,0:T(8,128)(2,1)S(1)} %all-to-all-done.parts_ref, f32[256,256]{1,0:T(8,128)S(1)} %copy-done.1, bf16[96,1280]{1,0:T(8,128)(2,1)S(1)} %get-tuple-element.19.rim_ref), custom_call_target="tpu_custom_call" | custom-call | flops 16777216 | bytes 1048576 | tf_op jit(solution)/shard_map/pallas_call | solution.py:397
  32.9 1.2 %collective-permute-start.2 = (bf16[96,1280]{1,0:T(8,128)(2,1)}, bf16[96,1280]{1,0:T(8,128)(2,1)S(1)}, u32[]{:S(2)}, u32[]{:S(2)}) collective-permute-start(bf16[96,1280]{1,0:T(8,128)(2,1)} %get-tuple-element.23), channel_id=1, source_target_pairs={{2,0},{4,2},{6,4},{8,6},{10,8},{12,10},{14,12},{16,14},{18,16},{20... | collective-permute-start | bytes 737288 | tf_op jit(solution)/shard_map/ppermute | solution.py:464
  34.1 4.6 %all-to-all-start.1 = ((bf16[64,16,256]{2,1,0:T(8,128)(2,1)}), bf16[64,16,256]{2,1,0:T(8,128)(2,1)S(1)}, u32[]{:S(2)}, u32[]{:S(2)}) async-start(bf16[64,16,256]{2,1,0:T(8,128)(2,1)} %get-tuple-element.20), calls=%async_computation.1 | async-start | bytes 1048576 | tf_op jit(solution)/shard_map/all_to_all | solution.py:465
  38.8 0.0 collective-permute-done.1.rest_0_
  38.8 0.3 collective-permute-done.2.rest_1_
  39.1 8.9 %shard_map.108 = (bf16[5,256,1024]{2,1,0:T(8,128)(2,1)}, bf16[5,256,256]{2,1,0:T(8,128)(2,1)}, s32[1]{0:T(128)}) custom-call(s32[128]{0:T(128)S(1)} %bitcast.15, s32[9,128]{1,0:T(8,128)S(1)} %bitcast.13, s32[1,128]{1,0:T(1,128)S(1)} %bitcast.17, bf16[9,128,384]{2,1,0:T(8,128)(2,1)S(1)} %bitcast.11, bf16[96,1280]{1,0:T(8,128)(2,1)S(1)} %collective-permute-done.1.rest_0_, ...), custom_call_target="tpu_custom_call" | custom-call | flops 3145728000 | bytes 10485760 | tf_op jit(solution)/shard_map/pallas_call | solution.py:368
  48.0 1.9 %all-to-all-done.1 = bf16[64,16,256]{2,1,0:T(8,128)(2,1)S(1)} async-done(((bf16[64,16,256]{2,1,0:T(8,128)(2,1)}), bf16[64,16,256]{2,1,0:T(8,128)(2,1)S(1)}, u32[]{:S(2)}, u32[]{:S(2)}) %all-to-all-start.1) | async-done | bytes 524320 | tf_op jit(solution)/shard_map/all_to_all | solution.py:465
  49.9 10.7 %shard_map.109 = (bf16[2048,1024]{1,0:T(8,128)(2,1)}, f32[64,256]{1,0:T(8,128)S(1)}, f32[64,256]{1,0:T(8,128)S(1)}) custom-call(s32[1]{0:T(128)} %bitcast.col_ref, bf16[1024,256]{1,0:T(8,128)(2,1)S(1)} %bitcast.8, f32[1,1024]{1,0:T(1,128)S(1)} %bitcast.9, bf16[2048,128]{1,0:T(8,128)(2,1)S(1)} %copy-done, ...), custom_call_target="tpu_custom_call" | custom-call | flops 6442450944 | bytes 14680064 | tf_op jit(solution)/shard_map/pallas_call | solution.py:414
  60.5 3.3 %collective-permute-start.3 = (f32[64,256]{1,0:T(8,128)S(1)}, f32[64,256]{1,0:T(8,128)S(1)}, u32[]{:S(2)}, u32[]{:S(2)}) collective-permute-start(f32[64,256]{1,0:T(8,128)S(1)} %get-tuple-element.29), channel_id=1, source_target_pairs={{0,1},{1,0},{2,3},{3,2},{4,5},{5,4},{6,7},{7,6},{8,9},{9,8},{10,11... | collective-permute-start | bytes 196616 | tf_op jit(solution)/shard_map/ppermute | solution.py:473
  63.8 0.9 %collective-permute-done.3 = f32[64,256]{1,0:T(8,128)S(1)} collective-permute-done((f32[64,256]{1,0:T(8,128)S(1)}, f32[64,256]{1,0:T(8,128)S(1)}, u32[]{:S(2)}, u32[]{:S(2)}) %collective-permute-start.3) | collective-permute-done | bytes 65568 | tf_op jit(solution)/shard_map/ppermute | solution.py:473
  64.7 0.6 add.3
  (4 shorter events, 0.0 us)
Async XLA Ops:
  0.6 4.3 %collective-permute-start = (bf16[2048,128]{1,0:T(8,128)(2,1)}, bf16[2048,128]{1,0:T(8,128)(2,1)S(1)}, u32[]{:S(2)}, u32[]{:S(2)}) collective-permute-start(bf16[2048,128]{1,0:T(8,128)(2,1)} %own_ref.1), channel_id=1, source_target_pairs={{0,1},{1,0},{2,3},{3,2},{4,5},{5,4},{6,7},{7,6},{8,9},{9,8},{10,11... | collective-permute-start | bytes 1572872 | tf_op jit(solution)/shard_map/ppermute | solution.py:452
  4.8 13.0 %copy-start = (bf16[2048,128]{1,0:T(8,128)(2,1)S(1)}, bf16[2048,128]{1,0:T(8,128)(2,1)}, u32[]{:S(2)}) copy-start(bf16[2048,128]{1,0:T(8,128)(2,1)} %own_ref.1) | copy-start | bytes 1572868
  4.8 13.0 %copy-start.2 = (bf16[128,9,384]{2,0,1:T(8,128)(2,1)S(1)}, bf16[128,9,384]{2,0,1:T(8,128)(2,1)}, u32[]{:S(2)}) copy-start(bf16[128,9,384]{2,0,1:T(8,128)(2,1)} %param.14) | copy-start | bytes 2654212
  4.8 13.0 %copy-start.3 = (s32[128,9]{0,1:T(8,128)S(1)}, s32[128,9]{0,1:T(8,128)}, u32[]{:S(2)}) copy-start(s32[128,9]{0,1:T(8,128)} %param.15) | copy-start | bytes 13828
  4.9 13.0 %copy-start.4 = (s32[1,128]{1,0:T(1,128)S(1)}, s32[1,128]{1,0:T(1,128)}, u32[]{:S(2)}) copy-start(s32[1,128]{1,0:T(1,128)} %param.12) | copy-start | bytes 1540
  4.9 13.0 %copy-start.5 = (s32[128]{0:T(128)S(1)}, s32[128]{0:T(128)}, u32[]{:S(2)}) copy-start(s32[128]{0:T(128)} %param.13) | copy-start | bytes 1540
  6.5 24.2 %copy-start.1 = (f32[256,256]{1,0:T(8,128)S(1)}, f32[256,256]{1,0:T(8,128)}, u32[]{:S(2)}) copy-start(f32[256,256]{1,0:T(8,128)} %factor_ref.1) | copy-start | bytes 786436
  6.5 24.2 %all-to-all-start = ((bf16[64,16,256]{2,1,0:T(8,128)(2,1)}), bf16[64,16,256]{2,1,0:T(8,128)(2,1)S(1)}, u32[]{:S(2)}, u32[]{:S(2)}) async-start(bf16[64,16,256]{2,1,0:T(8,128)(2,1)} %bitcast.5), calls=%async_computation | async-start | bytes 1048576 | tf_op jit(solution)/shard_map/all_to_all | solution.py:454
  17.9 20.8 %copy-start.6 = (f32[1024]{0:T(1024)S(1)}, f32[1024]{0:T(1024)}, u32[]{:S(2)}) copy-start(f32[1024]{0:T(1024)} %param.17) | copy-start | bytes 12292
  17.9 20.8 %copy-start.7 = (s32[1024]{0:T(1024)S(1)}, s32[1024]{0:T(1024)}, u32[]{:S(2)}) copy-start(s32[1024]{0:T(1024)} %param.16) | copy-start | bytes 12292
  24.9 13.9 %collective-permute-start.1 = (bf16[96,1280]{1,0:T(8,128)(2,1)S(1)}, bf16[96,1280]{1,0:T(8,128)(2,1)S(1)}, u32[]{:S(2)}, u32[]{:S(2)}) collective-permute-start(bf16[96,1280]{1,0:T(8,128)(2,1)S(1)} %get-tuple-element.22), channel_id=1, source_target_pairs={{0,2},{2,4},{4,6},{6,8},{8,10},{10,12},{12,14},{14,16},{16,18},{18... | collective-permute-start | bytes 737288 | tf_op jit(solution)/shard_map/ppermute | solution.py:462
  32.9 6.2 %collective-permute-start.2 = (bf16[96,1280]{1,0:T(8,128)(2,1)}, bf16[96,1280]{1,0:T(8,128)(2,1)S(1)}, u32[]{:S(2)}, u32[]{:S(2)}) collective-permute-start(bf16[96,1280]{1,0:T(8,128)(2,1)} %get-tuple-element.23), channel_id=1, source_target_pairs={{2,0},{4,2},{6,4},{8,6},{10,8},{12,10},{14,12},{16,14},{18,16},{20... | collective-permute-start | bytes 737288 | tf_op jit(solution)/shard_map/ppermute | solution.py:464
  34.1 15.8 %all-to-all-start.1 = ((bf16[64,16,256]{2,1,0:T(8,128)(2,1)}), bf16[64,16,256]{2,1,0:T(8,128)(2,1)S(1)}, u32[]{:S(2)}, u32[]{:S(2)}) async-start(bf16[64,16,256]{2,1,0:T(8,128)(2,1)} %get-tuple-element.20), calls=%async_computation.1 | async-start | bytes 1048576 | tf_op jit(solution)/shard_map/all_to_all | solution.py:465
  60.5 4.2 %collective-permute-start.3 = (f32[64,256]{1,0:T(8,128)S(1)}, f32[64,256]{1,0:T(8,128)S(1)}, u32[]{:S(2)}, u32[]{:S(2)}) collective-permute-start(f32[64,256]{1,0:T(8,128)S(1)} %get-tuple-element.29), channel_id=1, source_target_pairs={{0,1},{1,0},{2,3},{3,2},{4,5},{5,4},{6,7},{7,6},{8,9},{9,8},{10,11... | collective-permute-start | bytes 196616 | tf_op jit(solution)/shard_map/ppermute | solution.py:473

commit v5 on v4

--- a/solution.py
+++ b/solution.py
@@ -218,9 +218,7 @@
         out_ref[mine, half:] = dot(turned, v_ref[:, mine]).T.astype(jnp.bfloat16)
 
 
-def mix_kernel(col_ref, mark_ref, parts_ref, factor_ref, rim_ref, out_ref, rim_out, sem):
-    passing = pltpu.make_async_copy(rim_ref, rim_out, sem)
-    passing.start()
+def mix_kernel(col_ref, mark_ref, parts_ref, factor_ref, out_ref):
     total = jnp.sum(parts_ref[...].astype(jnp.float32), axis=0)
     half = total.shape[1] // 2
     swap = col_ref[0] == 1
@@ -228,7 +226,6 @@
     mixed = dot(total, factor_ref[...], precision=lax.Precision.HIGHEST)
     mixed = jnp.where(swap, pltpu.roll(mixed, half, 1), mixed).astype(jnp.bfloat16)
     out_ref[...] = jnp.broadcast_to(mixed[None], out_ref.shape)
-    passing.wait()
 
 
 def main_kernel(parts, col_ref, mix_ref, weight_ref, own_ref, other_ref, *refs):
@@ -251,9 +248,14 @@
                 pltpu.make_async_copy(t_hbms[p].at[at], t_ref.at[n], u_sem.at[1, n]),
             ]
         )
-    steps = [(n, [b for b in (2 * n, 2 * n + 1) if b < blocks]) for n in range(len(order))]
-    for n, bs in steps:
-        for c in u_copies[n] + [v_copies[b] for b in bs]:
+    early, late = range(len(order) // 2), range(len(order) // 2, len(order))
+    for n in early:
+        for c in u_copies[n]:
+            c.start()
+    for c in v_copies:
+        c.start()
+    for n in late:
+        for c in u_copies[n]:
             c.start()
     mt_ref[...] = mix_ref[...].T
     mix = mt_ref[...]
@@ -264,33 +266,50 @@
     same_i = (down >> 4) == (along >> 4)
 
     def rotate(b):
-        v_copies[b].wait()
         at = slice(b * 256, (b + 1) * 256)
         panel = jnp.concatenate([own_ref[at, :], other_ref[at, :]], axis=1)
         turned = v_ref[at, :].astype(jnp.float32) - dot(panel, mix)
         r_ref[at, :] = turned.astype(jnp.bfloat16)
-        out_copies[b].start()
-
-    def density_of(n):
-        for c in u_copies[n]:
-            c.wait()
+
+    def project(n):
         turned = u_ref[n].astype(jnp.float32) - dot(t_ref[n], mix)
-        rounded = turned.astype(jnp.bfloat16)
+        return turned.astype(jnp.bfloat16)
+
+    def pair(rounded):
         weighted = (rounded.astype(jnp.float32) * weight).astype(jnp.bfloat16)
-        pairs = jnp.where(same_atom, dot(weighted, rounded, NT), 0.0)
+        return jnp.where(same_atom, dot(weighted, rounded, NT), 0.0)
+
+    def pack(n, pairs):
         high = pairs.astype(jnp.bfloat16)
         low = (pairs - high.astype(jnp.float32)).astype(jnp.bfloat16)
         spreaded = jnp.where(same_i, dot(high, spread) + dot(low, spread), 0.0)
         total = spreaded[:GROUP]
         for i in range(1, NPMAX):
             total = total + spreaded[i * GROUP : (i + 1) * GROUP]
-        return total
-
-    for n, bs in steps:
         at = order[n][0] * GROUP
-        d_ref[at : at + GROUP, :] = density_of(n)
-        for b in bs:
-            rotate(b)
+        d_ref[at : at + GROUP, :] = total
+
+    def densities(which):
+        for n in which:
+            for c in u_copies[n]:
+                c.wait()
+        projected, paired = {}, {}
+        for n in range(which[0], which[-1] + 3):
+            if n in which:
+                projected[n] = project(n)
+            if n - 1 in which:
+                paired[n - 1] = pair(projected.pop(n - 1))
+            if n - 2 in which:
+                pack(n - 2, paired.pop(n - 2))
+
+    densities(early)
+    for c in v_copies:
+        c.wait()
+    for b in range(blocks):
+        rotate(b)
+    for c in out_copies:
+        c.start()
+    densities(late)
     per = own_out.shape[0]
     mine = pl.multiple_of(col_ref[0] * per, per)
     own_out[...] = d_ref[pl.ds(mine, per), :]
@@ -393,17 +412,16 @@
     )(counts, present, proj_count, blocks, *halos, v_hbm, panel, other)
 
 
-def mix(col, mark, slices, factor, rim):
+def mix(col, mark, slices, factor):
     return call(
         mix_kernel,
-        [pltpu.VMEM(slices.shape, BF16), pltpu.VMEM(rim.shape, BF16)],
-        [SMEM_SPEC, SMEM_SPEC, VMEM_SPEC, VMEM_SPEC, VMEM_SPEC],
-        [VMEM_SPEC, VMEM_SPEC],
+        pltpu.VMEM(slices.shape, BF16),
+        [SMEM_SPEC, SMEM_SPEC, VMEM_SPEC, VMEM_SPEC],
+        VMEM_SPEC,
         1 << 24,
         1 << 20,
         8,
-        scratch_shapes=[pltpu.SemaphoreType.DMA],
-    )(col, mark, slices, factor, rim)
+    )(col, mark, slices, factor)
 
 
 def finish(parts, col, mixing, weights, panel, other, us, ts, v_hbm):
@@ -460,7 +478,7 @@
     u_early, t_early, mark, to_next, to_last = couple(early, *shared, (), v_hbm, panel, other)
     up = [(i, (i + 1) % n_row) for i in range(n_row)]
     before = lax.ppermute(to_next, "row", up)
-    copies, to_last = mix(col, mark, slices, factor, to_last)
+    copies = mix(col, mark, slices, factor)
     after = lax.ppermute(to_last, "row", [(j, i) for i, j in up])
     mixing = lax.all_to_all(copies.reshape(cols, npan), "row", 0, 0, tiled=True)
     u_late, t_late, _ = couple(late, *shared, (before, after), v_hbm, panel, other)

time: 65.7 us -> 61.8 us (0.941)
  Pallas kernels: 33 us -> 29 us
  starting transfers between devices: 23.1 us -> 27 us
  waiting for transfers between devices: 7.78 us -> 3.92 us
    all_to_all x1, waiting for transfers between devices: 4.72 us -> 0.01 us  [local(): slices = lax.all_to_all(partial, 'row', 0, 0, tiled=True)]
    ppermute x1, starting transfers between devices: 1.24 us -> 5.89 us  [local(): after = lax.ppermute(to_last, 'row', [(j, i) for i, j in up])]
    pallas_call x1, Pallas kernels: 10.7 us -> 7.13 us  [finish(): call(functools.partial(main_kernel, parts), [jax.ShapeDtypeStruct((rows,...]
    all_to_all x1, waiting for transfers between devices: 1.86 us -> 3.01 us  [local(): mixing = lax.all_to_all(copies.reshape(cols, npan), 'row', 0, 0, tiled=True)]
    ppermute x1, starting transfers between devices: 3.28 us -> 2.41 us  [local(): density = own_part + lax.ppermute(other_part, 'col', [(0, 1), (1, 0)])]
  transfers between devices with their start and end apart: 6 -> 6, of which waited for: 4 -> 2; matrix products, arithmetic and copies ran while one was open for 0% -> 0% of each run, Pallas kernels for 32% -> 33%
where the time goes in v5:
time: 61.8 us; the launch traced here: 61.5 us
  Pallas kernels  29 us (47%)
  starting transfers between devices  27 us (44%)
  waiting for transfers between devices  3.92 us (6%)
  between operations  0.82 us (1%)
  other arithmetic  0.64 us (1%)
    pallas_call x2, Pallas kernels, couple(): call(kernel, [pltpu.HBM((n, 256, cols), BF16), pltpu.HBM((n, 256, npan),...  15.8 us
    all_to_all x1, starting transfers between devices, local(): slices = lax.all_to_all(partial, 'row', 0, 0, tiled=True)  11.3 us
    pallas_call x1, Pallas kernels, finish(): call(functools.partial(main_kernel, parts), [jax.ShapeDtypeStruct((rows,...  7.13 us
    ppermute x1, starting transfers between devices, local(): after = lax.ppermute(to_last, 'row', [(j, i) for i, j in up])  5.89 us
    all_to_all x1, starting transfers between devices, local(): mixing = lax.all_to_all(copies.reshape(cols, npan), 'row', 0, 0, tiled=True)  4.81 us
    all_to_all x1, waiting for transfers between devices, local(): mixing = lax.all_to_all(copies.reshape(cols, npan), 'row', 0, 0, tiled=True)  3.01 us
    pallas_call x1, Pallas kernels, partial_sums(): call(own_kernel, [pltpu.VMEM((cols, half), BF16), pltpu.VMEM((rows, cols)...  2.69 us
    ppermute x1, starting transfers between devices, local(): density = own_part + lax.ppermute(other_part, 'col', [(0, 1), (1, 0)])  2.41 us
  transfers between devices with their start and end apart: 6, of which 2 were waited for; matrix products, arithmetic and copies ran while one was open for 0% of the time, Pallas kernels for 33%

profile of v5, /device:TPU:1, one launch (start us, length us, event | category | flops | bytes accessed | tf_op | source)
XLA Modules:
  0.0 61.5 jit_solution(17824706761459655804)
XLA Ops:
  0.6 1.5 %collective-permute-start = (bf16[2048,128]{1,0:T(8,128)(2,1)}, bf16[2048,128]{1,0:T(8,128)(2,1)S(1)}, u32[]{:S(2)}, u32[]{:S(2)}) collective-permute-start(bf16[2048,128]{1,0:T(8,128)(2,1)} %own_ref.1), channel_id=1, source_target_pairs={{0,1},{1,0},{2,3},{3,2},{4,5},{5,4},{6,7},{7,6},{8,9},{9,8},{10,11... | collective-permute-start | bytes 1572872 | tf_op jit(solution)/shard_map/ppermute | solution.py:470
  2.1 2.7 %shard_map.105 = (bf16[1024,128]{1,0:T(8,128)(2,1)S(1)}, bf16[2048,1024]{1,0:T(8,128)(2,1)S(1)}) custom-call(bf16[2048,128]{1,0:T(8,128)(2,1)} %own_ref.1, bf16[2048,1024]{1,0:T(8,128)(2,1)} %refs_4_.1), custom_call_target="tpu_custom_call" | custom-call | flops 536870912 | bytes 5242880 | tf_op jit(solution)/shard_map/pallas_call | solution.py:347
  4.8 0.0 copy-start
  4.8 0.0 copy-start.2
  4.8 0.0 copy-start.3
  4.9 0.0 copy-start.4
  4.9 0.0 copy-start.5
  4.9 0.0 collective-permute-done.rest_2_.other_ref.rest_4_
  4.9 1.6 %shard_map.106 = bf16[1024,256]{1,0:T(8,128)(2,1)} custom-call(bf16[1024,128]{1,0:T(8,128)(2,1)S(1)} %get-tuple-element.15.done_ref, bf16[2048,128]{1,0:T(8,128)(2,1)S(1)} %collective-permute-done.rest_2_.other_ref.rest_4_, bf16[2048,1024]{1,0:T(8,128)(2,1)S(1)} %get-tuple-element.16.v_ref), custom_call_target="tpu_custom_call" | custom-call | flops 536870912 | bytes 5242880 | tf_op jit(solution)/shard_map/pallas_call | solution.py:361
  6.5 11.3 %all-to-all-start = ((bf16[64,16,256]{2,1,0:T(8,128)(2,1)}), bf16[64,16,256]{2,1,0:T(8,128)(2,1)S(1)}, u32[]{:S(2)}, u32[]{:S(2)}) async-start(bf16[64,16,256]{2,1,0:T(8,128)(2,1)} %bitcast.5), calls=%async_computation | async-start | bytes 1048576 | tf_op jit(solution)/shard_map/all_to_all | solution.py:472
  17.9 0.0 copy-done
  17.9 0.0 copy-done.2
  17.9 0.0 copy-done.3
  17.9 0.0 copy-done.4
  17.9 0.0 copy-done.5
  17.9 0.0 copy-start.6
  17.9 0.0 copy-start.7
  17.9 7.1 %shard_map.104 = (bf16[3,256,1024]{2,1,0:T(8,128)(2,1)}, bf16[3,256,256]{2,1,0:T(8,128)(2,1)}, s32[1]{0:T(128)}, bf16[96,1280]{1,0:T(8,128)(2,1)}, bf16[96,1280]{1,0:T(8,128)(2,1)S(1)}) custom-call(s32[128]{0:T(128)S(1)} %bitcast.14, s32[9,128]{1,0:T(8,128)S(1)} %bitcast.12, s32[1,128]{1,0:T(1,128)S(1)} %bitcast.16, bf16[9,128,384]{2,1,0:T(8,128)(2,1)S(1)} %bitcast.10, ...), custom_call_target="tpu_custom_call" | custom-call | flops 1887436800 | bytes 10485760 | tf_op jit(solution)/shard_map/pallas_call | solution.py:387
  25.0 1.1 %collective-permute-start.1 = (bf16[96,1280]{1,0:T(8,128)(2,1)}, bf16[96,1280]{1,0:T(8,128)(2,1)S(1)}, u32[]{:S(2)}, u32[]{:S(2)}) collective-permute-start(bf16[96,1280]{1,0:T(8,128)(2,1)} %get-tuple-element.18), channel_id=1, source_target_pairs={{0,2},{2,4},{4,6},{6,8},{8,10},{10,12},{12,14},{14,16},{16,18},{18... | collective-permute-start | bytes 737288 | tf_op jit(solution)/shard_map/ppermute | solution.py:480
  26.1 5.9 %collective-permute-start.2 = (bf16[96,1280]{1,0:T(8,128)(2,1)S(1)}, bf16[96,1280]{1,0:T(8,128)(2,1)S(1)}, u32[]{:S(2)}, u32[]{:S(2)}) collective-permute-start(bf16[96,1280]{1,0:T(8,128)(2,1)S(1)} %get-tuple-element.19), channel_id=1, source_target_pairs={{2,0},{4,2},{6,4},{8,6},{10,8},{12,10},{14,12},{16,14},{18,16},{20... | collective-permute-start | bytes 737288 | tf_op jit(solution)/shard_map/ppermute | solution.py:482
  32.0 0.0 all-to-all-done.parts_ref
  32.0 0.0 copy-done.1
  32.0 1.7 %shard_map.107 = bf16[64,16,256]{2,1,0:T(8,128)(2,1)} custom-call(s32[1]{0:T(128)} %bitcast.col_ref, s32[1]{0:T(128)} %get-tuple-element.14.mark_ref, bf16[64,16,256]{2,1,0:T(8,128)(2,1)S(1)} %all-to-all-done.parts_ref, f32[256,256]{1,0:T(8,128)S(1)} %copy-done.1), custom_call_target="tpu_custom_call" | custom-call | flops 16777216 | bytes 1048576 | tf_op jit(solution)/shard_map/pallas_call | solution.py:416
  33.7 4.8 %all-to-all-start.1 = ((bf16[64,16,256]{2,1,0:T(8,128)(2,1)}), bf16[64,16,256]{2,1,0:T(8,128)(2,1)S(1)}, u32[]{:S(2)}, u32[]{:S(2)}) async-start(bf16[64,16,256]{2,1,0:T(8,128)(2,1)} %shard_map.107), calls=%async_computation.1 | async-start | bytes 1048576 | tf_op jit(solution)/shard_map/all_to_all | solution.py:483
  38.6 0.0 collective-permute-done.1.rest_0_
  38.6 0.0 collective-permute-done.2.rest_1_
  38.6 8.7 %shard_map.108 = (bf16[5,256,1024]{2,1,0:T(8,128)(2,1)}, bf16[5,256,256]{2,1,0:T(8,128)(2,1)}, s32[1]{0:T(128)}) custom-call(s32[128]{0:T(128)S(1)} %bitcast.15, s32[9,128]{1,0:T(8,128)S(1)} %bitcast.13, s32[1,128]{1,0:T(1,128)S(1)} %bitcast.17, bf16[9,128,384]{2,1,0:T(8,128)(2,1)S(1)} %bitcast.11, bf16[96,1280]{1,0:T(8,128)(2,1)S(1)} %collective-permute-done.1.rest_0_, ...), custom_call_target="tpu_custom_call" | custom-call | flops 3145728000 | bytes 10485760 | tf_op jit(solution)/shard_map/pallas_call | solution.py:387
  47.4 3.0 %all-to-all-done.1 = bf16[64,16,256]{2,1,0:T(8,128)(2,1)S(1)} async-done(((bf16[64,16,256]{2,1,0:T(8,128)(2,1)}), bf16[64,16,256]{2,1,0:T(8,128)(2,1)S(1)}, u32[]{:S(2)}, u32[]{:S(2)}) %all-to-all-start.1) | async-done | bytes 524320 | tf_op jit(solution)/shard_map/all_to_all | solution.py:483
  50.4 7.1 %shard_map.109 = (bf16[2048,1024]{1,0:T(8,128)(2,1)}, f32[64,256]{1,0:T(8,128)S(1)}, f32[64,256]{1,0:T(8,128)S(1)}) custom-call(s32[1]{0:T(128)} %bitcast.col_ref, bf16[1024,256]{1,0:T(8,128)(2,1)S(1)} %bitcast.8, f32[1,1024]{1,0:T(1,128)S(1)} %bitcast.9, bf16[2048,128]{1,0:T(8,128)(2,1)S(1)} %copy-done, ...), custom_call_target="tpu_custom_call" | custom-call | flops 6442450944 | bytes 14680064 | tf_op jit(solution)/shard_map/pallas_call | solution.py:432
  57.5 2.4 %collective-permute-start.3 = (f32[64,256]{1,0:T(8,128)S(1)}, f32[64,256]{1,0:T(8,128)S(1)}, u32[]{:S(2)}, u32[]{:S(2)}) collective-permute-start(f32[64,256]{1,0:T(8,128)S(1)} %get-tuple-element.25), channel_id=1, source_target_pairs={{0,1},{1,0},{2,3},{3,2},{4,5},{5,4},{6,7},{7,6},{8,9},{9,8},{10,11... | collective-permute-start | bytes 196616 | tf_op jit(solution)/shard_map/ppermute | solution.py:491
  59.9 0.9 %collective-permute-done.3 = f32[64,256]{1,0:T(8,128)S(1)} collective-permute-done((f32[64,256]{1,0:T(8,128)S(1)}, f32[64,256]{1,0:T(8,128)S(1)}, u32[]{:S(2)}, u32[]{:S(2)}) %collective-permute-start.3) | collective-permute-done | bytes 65568 | tf_op jit(solution)/shard_map/ppermute | solution.py:491
  60.8 0.6 %add.3 = f32[64,256]{1,0:T(8,128)} add(f32[64,256]{1,0:T(8,128)S(1)} %get-tuple-element.24, f32[64,256]{1,0:T(8,128)S(1)} %collective-permute-done.3) | non-fusion elementwise | flops 16384 | bytes 196608 | tf_op jit(solution)/shard_map/add | solution.py:491
  (4 shorter events, 0.0 us)
Async XLA Ops:
  0.6 4.3 %collective-permute-start = (bf16[2048,128]{1,0:T(8,128)(2,1)}, bf16[2048,128]{1,0:T(8,128)(2,1)S(1)}, u32[]{:S(2)}, u32[]{:S(2)}) collective-permute-start(bf16[2048,128]{1,0:T(8,128)(2,1)} %own_ref.1), channel_id=1, source_target_pairs={{0,1},{1,0},{2,3},{3,2},{4,5},{5,4},{6,7},{7,6},{8,9},{9,8},{10,11... | collective-permute-start | bytes 1572872 | tf_op jit(solution)/shard_map/ppermute | solution.py:470
  4.8 13.0 %copy-start = (bf16[2048,128]{1,0:T(8,128)(2,1)S(1)}, bf16[2048,128]{1,0:T(8,128)(2,1)}, u32[]{:S(2)}) copy-start(bf16[2048,128]{1,0:T(8,128)(2,1)} %own_ref.1) | copy-start | bytes 1572868
  4.8 13.0 %copy-start.2 = (bf16[128,9,384]{2,0,1:T(8,128)(2,1)S(1)}, bf16[128,9,384]{2,0,1:T(8,128)(2,1)}, u32[]{:S(2)}) copy-start(bf16[128,9,384]{2,0,1:T(8,128)(2,1)} %param.14) | copy-start | bytes 2654212
  4.8 13.0 %copy-start.3 = (s32[128,9]{0,1:T(8,128)S(1)}, s32[128,9]{0,1:T(8,128)}, u32[]{:S(2)}) copy-start(s32[128,9]{0,1:T(8,128)} %param.15) | copy-start | bytes 13828
  4.9 13.0 %copy-start.4 = (s32[1,128]{1,0:T(1,128)S(1)}, s32[1,128]{1,0:T(1,128)}, u32[]{:S(2)}) copy-start(s32[1,128]{1,0:T(1,128)} %param.12) | copy-start | bytes 1540
  4.9 13.0 %copy-start.5 = (s32[128]{0:T(128)S(1)}, s32[128]{0:T(128)}, u32[]{:S(2)}) copy-start(s32[128]{0:T(128)} %param.13) | copy-start | bytes 1540
  6.5 25.5 %copy-start.1 = (f32[256,256]{1,0:T(8,128)S(1)}, f32[256,256]{1,0:T(8,128)}, u32[]{:S(2)}) copy-start(f32[256,256]{1,0:T(8,128)} %factor_ref.1) | copy-start | bytes 786436
  6.5 25.5 %all-to-all-start = ((bf16[64,16,256]{2,1,0:T(8,128)(2,1)}), bf16[64,16,256]{2,1,0:T(8,128)(2,1)S(1)}, u32[]{:S(2)}, u32[]{:S(2)}) async-start(bf16[64,16,256]{2,1,0:T(8,128)(2,1)} %bitcast.5), calls=%async_computation | async-start | bytes 1048576 | tf_op jit(solution)/shard_map/all_to_all | solution.py:472
  17.9 20.7 %copy-start.6 = (f32[1024]{0:T(1024)S(1)}, f32[1024]{0:T(1024)}, u32[]{:S(2)}) copy-start(f32[1024]{0:T(1024)} %param.17) | copy-start | bytes 12292
  17.9 20.7 %copy-start.7 = (s32[1024]{0:T(1024)S(1)}, s32[1024]{0:T(1024)}, u32[]{:S(2)}) copy-start(s32[1024]{0:T(1024)} %param.16) | copy-start | bytes 12292
  25.0 13.6 %collective-permute-start.1 = (bf16[96,1280]{1,0:T(8,128)(2,1)}, bf16[96,1280]{1,0:T(8,128)(2,1)S(1)}, u32[]{:S(2)}, u32[]{:S(2)}) collective-permute-start(bf16[96,1280]{1,0:T(8,128)(2,1)} %get-tuple-element.18), channel_id=1, source_target_pairs={{0,2},{2,4},{4,6},{6,8},{8,10},{10,12},{12,14},{14,16},{16,18},{18... | collective-permute-start | bytes 737288 | tf_op jit(solution)/shard_map/ppermute | solution.py:480
  26.1 12.5 %collective-permute-start.2 = (bf16[96,1280]{1,0:T(8,128)(2,1)S(1)}, bf16[96,1280]{1,0:T(8,128)(2,1)S(1)}, u32[]{:S(2)}, u32[]{:S(2)}) collective-permute-start(bf16[96,1280]{1,0:T(8,128)(2,1)S(1)} %get-tuple-element.19), channel_id=1, source_target_pairs={{2,0},{4,2},{6,4},{8,6},{10,8},{12,10},{14,12},{16,14},{18,16},{20... | collective-permute-start | bytes 737288 | tf_op jit(solution)/shard_map/ppermute | solution.py:482
  33.7 16.6 %all-to-all-start.1 = ((bf16[64,16,256]{2,1,0:T(8,128)(2,1)}), bf16[64,16,256]{2,1,0:T(8,128)(2,1)S(1)}, u32[]{:S(2)}, u32[]{:S(2)}) async-start(bf16[64,16,256]{2,1,0:T(8,128)(2,1)} %shard_map.107), calls=%async_computation.1 | async-start | bytes 1048576 | tf_op jit(solution)/shard_map/all_to_all | solution.py:483
  57.5 3.3 %collective-permute-start.3 = (f32[64,256]{1,0:T(8,128)S(1)}, f32[64,256]{1,0:T(8,128)S(1)}, u32[]{:S(2)}, u32[]{:S(2)}) collective-permute-start(f32[64,256]{1,0:T(8,128)S(1)} %get-tuple-element.25), channel_id=1, source_target_pairs={{0,1},{1,0},{2,3},{3,2},{4,5},{5,4},{6,7},{7,6},{8,9},{9,8},{10,11... | collective-permute-start | bytes 196616 | tf_op jit(solution)/shard_map/ppermute | solution.py:491

commit v6 on v5

--- a/solution.py
+++ b/solution.py
@@ -43,34 +43,38 @@
         target = jnp.where((u >= 0) & (u < count), row + u, target)
         row = row + count
     pick = (iota((EDGE, TAIL), 1) == target).astype(jnp.float32).astype(jnp.bfloat16)
-    return [dot(pick, source).astype(jnp.bfloat16) for source in sources]
-
-
-def fill_rims(counts_ref, e_ref, p_ref, to_next, to_last):
+    return [dot(pick, source) for source in sources]
+
+
+def fill_rims(odd_ref, counts_ref, e_ref, p_ref, to_pair, to_other):
     atoms = counts_ref.shape[0]
     cols = e_ref.shape[1]
     end = e_ref.shape[0] - EDGE
     tail = counts_ref[atoms - 1]
     for t in range(1, RIM):
         tail = tail + counts_ref[atoms - 1 - t]
-    for out, atom, row, at in (
-        (to_next, atoms - RIM, TAIL - tail, slice(end - TAIL, end)),
-        (to_last, 0, 0, slice(EDGE, EDGE + TAIL)),
+    ends = []
+    for atom, row, at in (
+        (atoms - RIM, TAIL - tail, slice(end - TAIL, end)),
+        (0, 0, slice(EDGE, EDGE + TAIL)),
     ):
-        pieces = padded_rows(counts_ref, atom, row, [e_ref[at, :], p_ref[at, :]])
-        out[:, :cols] = pieces[0]
-        out[:, cols:] = pieces[1]
+        ends.append(padded_rows(counts_ref, atom, row, [e_ref[at, :], p_ref[at, :]]))
+    odd = odd_ref[0] == 1
+    for last, first, at in zip(*ends, (slice(0, cols), slice(cols, None))):
+        to_pair[:, at] = jnp.where(odd, first, last).astype(jnp.bfloat16)
+        to_other[:, at] = jnp.where(odd, last, first).astype(jnp.bfloat16)
 
 
 def pre_kernel(
     which_groups,
     rim_refs,
+    odd_ref,
     counts_ref,
     present_ref,
     proj_ref,
     cm_ref,
-    before_ref,
-    after_ref,
+    pair_ref,
+    other_ref,
     v_hbm,
     own_hbm,
     other_hbm,
@@ -100,14 +104,20 @@
     for c in copies:
         c.start()
     out_copies = []
-    for halo_ref, at in ((before_ref, 0), (after_ref, EDGE + rows)):
-        mine = slice(at, at + EDGE)
-        if halo_ref is None:
-            e_ref[mine, :] = jnp.zeros((EDGE, cols), jnp.bfloat16)
-            p_ref[mine, :] = jnp.zeros((EDGE, 2 * half), jnp.bfloat16)
-        else:
-            e_ref[mine, :] = halo_ref[:, :cols]
-            p_ref[mine, :] = halo_ref[:, cols:]
+    below, above = slice(0, EDGE), slice(EDGE + rows, None)
+    if pair_ref is None:
+        for at in (below, above):
+            e_ref[at, :] = jnp.zeros((EDGE, cols), jnp.bfloat16)
+            p_ref[at, :] = jnp.zeros((EDGE, 2 * half), jnp.bfloat16)
+    else:
+        for parity, places in ((0, (above, below)), (1, (below, above))):
+
+            @pl.when(odd_ref[0] == parity)
+            def _():
+                for rim_ref, at in zip((pair_ref, other_ref), places):
+                    e_ref[at, :] = rim_ref[:, :cols]
+                    p_ref[at, :] = rim_ref[:, cols:]
+
     mark_ref[0] = counts_ref[0]
 
     for t in range(RIM):
@@ -135,7 +145,7 @@
             for c in copies:
                 c.wait()
             if rim_refs is not None:
-                fill_rims(counts_ref, e_ref, p_ref, *rim_refs)
+                fill_rims(odd_ref, counts_ref, e_ref, p_ref, *rim_refs)
         window = pl.ds(pl.multiple_of(starts[n], ALIGN), WIDE)
         u_ref[n] = dot(bands[n], e_ref[window, :]).astype(jnp.bfloat16)
         t_ref[n] = dot(bands[n], p_ref[window, :]).astype(jnp.bfloat16)
@@ -208,14 +218,20 @@
     done_ref[...] = acc_ref[...].T.astype(jnp.bfloat16)
 
 
-def other_kernel(done_ref, other_ref, v_ref, out_ref):
+def other_kernel(done_ref, other_ref, v_ref, out_hbm, out_ref, sem):
     half = other_ref.shape[1]
     cols = v_ref.shape[1]
     turned = other_ref[...].T
-    out_ref[:, :half] = done_ref[...]
-    for at in range(0, cols, 256):
+    copies = []
+    for n, at in enumerate(range(0, cols, 256)):
         mine = slice(at, at + 256)
+        out_ref[mine, :half] = done_ref[mine, :]
         out_ref[mine, half:] = dot(turned, v_ref[:, mine]).T.astype(jnp.bfloat16)
+        piece = pl.ds(at, 256)
+        copies.append(pltpu.make_async_copy(out_ref.at[piece], out_hbm.at[piece], sem.at[n]))
+        copies[-1].start()
+    for c in copies:
+        c.wait()
 
 
 def mix_kernel(col_ref, mark_ref, parts_ref, factor_ref, out_ref):
@@ -360,16 +376,20 @@
     )(in_hbm(panel), v_hbm)
     return call(
         other_kernel,
-        pltpu.VMEM((cols, 2 * half), BF16),
+        pltpu.HBM((cols, 2 * half), BF16),
         [VMEM_SPEC] * 3,
-        VMEM_SPEC,
+        HBM_SPEC,
         work,
         5 << 20,
         24,
+        scratch_shapes=[
+            pltpu.VMEM((cols, 2 * half), BF16),
+            pltpu.SemaphoreType.DMA((cols // 256,)),
+        ],
     )(done, other, v_vmem)
 
 
-def couple(which, counts, present, proj_count, blocks, halos, v_hbm, panel, other):
+def couple(which, odd, counts, present, proj_count, blocks, halos, v_hbm, panel, other):
     rows, cols = v_hbm.shape
     npan = 2 * panel.shape[1]
     atoms = counts.shape[0]
@@ -377,12 +397,13 @@
 
     first = not halos
 
-    def kernel(counts_ref, present_ref, proj_ref, cm_ref, *rest):
+    def kernel(odd_ref, counts_ref, present_ref, proj_ref, cm_ref, *rest):
         ends = (None, None) if first else rest[:2]
         rest = rest[len(halos) :]
         rim_refs = rest[6:8] if first else None
         rest = rest[:6] + rest[8:] if first else rest
-        pre_kernel(which, rim_refs, counts_ref, present_ref, proj_ref, cm_ref, *ends, *rest)
+        shared = (odd_ref, counts_ref, present_ref, proj_ref, cm_ref)
+        pre_kernel(which, rim_refs, *shared, *ends, *rest)
 
     return call(
         kernel,
@@ -392,7 +413,7 @@
             jax.ShapeDtypeStruct((1,), jnp.int32),
         ]
         + [jax.ShapeDtypeStruct((EDGE, cols + npan), BF16)] * (2 if first else 0),
-        [SMEM_SPEC] + [VMEM_SPEC] * (3 + len(halos)) + [HBM_SPEC] * 3,
+        [SMEM_SPEC] * 2 + [VMEM_SPEC] * (3 + len(halos)) + [HBM_SPEC] * 3,
         [HBM_SPEC, HBM_SPEC, SMEM_SPEC] + [VMEM_SPEC] * (2 if first else 0),
         n * 2 * 256 * WIDE * (WIDE + cols + npan),
         10 << 20,
@@ -409,7 +430,7 @@
             pltpu.SemaphoreType.DMA((3,)),
             pltpu.SemaphoreType.DMA((2, n)),
         ],
-    )(counts, present, proj_count, blocks, *halos, v_hbm, panel, other)
+    )(odd, counts, present, proj_count, blocks, *halos, v_hbm, panel, other)
 
 
 def mix(col, mark, slices, factor):
@@ -474,14 +495,17 @@
 
     early = list(range(1, groups // 2))
     late = list(range(groups // 2, groups)) + [0]
-    shared = (counts, block_present.T, proj_count[None, :], coupling.transpose(1, 0, 2))
-    u_early, t_early, mark, to_next, to_last = couple(early, *shared, (), v_hbm, panel, other)
-    up = [(i, (i + 1) % n_row) for i in range(n_row)]
-    before = lax.ppermute(to_next, "row", up)
+    odd = (lax.axis_index("row") & 1)[None]
+    shared = (odd, counts, block_present.T, proj_count[None, :], coupling.transpose(1, 0, 2))
+    u_early, t_early, mark, to_pair, to_other = couple(early, *shared, (), v_hbm, panel, other)
+    firsts = range(0, n_row, 2)
+    pairs = [(i, i + 1) for i in firsts]
+    others = [(i + 1, (i + 2) % n_row) for i in firsts]
+    rim_pair = lax.ppermute(to_pair, "row", pairs + [(j, i) for i, j in pairs])
+    rim_other = lax.ppermute(to_other, "row", others + [(j, i) for i, j in others])
     copies = mix(col, mark, slices, factor)
-    after = lax.ppermute(to_last, "row", [(j, i) for i, j in up])
     mixing = lax.all_to_all(copies.reshape(cols, npan), "row", 0, 0, tiled=True)
-    u_late, t_late, _ = couple(late, *shared, (before, after), v_hbm, panel, other)
+    u_late, t_late, _ = couple(late, *shared, (rim_pair, rim_other), v_hbm, panel, other)
 
     weights = (occ_mask.astype(F32) * occ_weight / (cols * n_col))[None, :]
     us, ts = [in_hbm(u_early), in_hbm(u_late)], [in_hbm(t_early), in_hbm(t_late)]

time: 61.8 us -> 62.2 us (level)
  no operation moved by 1% of the time
where the time goes in v6:
time: 62.2 us; the launch traced here: 61.9 us
  Pallas kernels  29.1 us (47%)
  starting transfers between devices  27.3 us (44%)
  waiting for transfers between devices  3.91 us (6%)
  between operations  0.84 us (1%)
  other arithmetic  0.64 us (1%)
    pallas_call x2, Pallas kernels, couple(): call(kernel, [pltpu.HBM((n, 256, cols), BF16), pltpu.HBM((n, 256, npan),...  16 us
    all_to_all x1, starting transfers between devices, local(): slices = lax.all_to_all(partial, 'row', 0, 0, tiled=True)  11.4 us
    pallas_call x1, Pallas kernels, finish(): call(functools.partial(main_kernel, parts), [jax.ShapeDtypeStruct((rows,...  7.13 us
    ppermute x1, starting transfers between devices, local(): lax.ppermute(to_other, 'row', others + [(j, i) for i, j in others])  6.32 us
    all_to_all x1, starting transfers between devices, local(): mixing = lax.all_to_all(copies.reshape(cols, npan), 'row', 0, 0, tiled=True)  4.63 us
    all_to_all x1, waiting for transfers between devices, local(): mixing = lax.all_to_all(copies.reshape(cols, npan), 'row', 0, 0, tiled=True)  3 us
    pallas_call x1, Pallas kernels, partial_sums(): call(own_kernel, [pltpu.VMEM((cols, half), BF16), pltpu.VMEM((rows, cols)...  2.69 us
    ppermute x1, starting transfers between devices, local(): density = own_part + lax.ppermute(other_part, 'col', [(0, 1), (1, 0)])  2.4 us
  transfers between devices with their start and end apart: 6, of which 2 were waited for; matrix products, arithmetic and copies ran while one was open for 0% of the time, Pallas kernels for 33%

profile of v6, /device:TPU:1, one launch (start us, length us, event | category | flops | bytes accessed | tf_op | source)
XLA Modules:
  0.0 61.9 jit_solution(3711467516237007177)
XLA Ops:
  0.6 1.5 %collective-permute-start = (bf16[2048,128]{1,0:T(8,128)(2,1)}, bf16[2048,128]{1,0:T(8,128)(2,1)S(1)}, u32[]{:S(2)}, u32[]{:S(2)}) collective-permute-start(bf16[2048,128]{1,0:T(8,128)(2,1)} %own_ref.1), channel_id=1, source_target_pairs={{0,1},{1,0},{2,3},{3,2},{4,5},{5,4},{6,7},{7,6},{8,9},{9,8},{10,11... | collective-permute-start | bytes 1572872 | tf_op jit(solution)/shard_map/ppermute | solution.py:491
  2.1 2.7 %shard_map.105 = (bf16[1024,128]{1,0:T(8,128)(2,1)S(1)}, bf16[2048,1024]{1,0:T(8,128)(2,1)S(1)}) custom-call(bf16[2048,128]{1,0:T(8,128)(2,1)} %own_ref.1, bf16[2048,1024]{1,0:T(8,128)(2,1)} %refs_4_.1), custom_call_target="tpu_custom_call" | custom-call | flops 536870912 | bytes 5242880 | tf_op jit(solution)/shard_map/pallas_call | solution.py:363
  4.8 0.0 copy-start
  4.8 0.0 copy-start.2
  4.8 0.0 copy-start.3
  4.9 0.0 copy-start.4
  4.9 0.0 copy-start.5
  4.9 0.0 collective-permute-done.rest_2_.other_ref.rest_4_
  4.9 1.5 %shard_map.106 = bf16[1024,256]{1,0:T(8,128)(2,1)} custom-call(bf16[1024,128]{1,0:T(8,128)(2,1)S(1)} %get-tuple-element.15.done_ref, bf16[2048,128]{1,0:T(8,128)(2,1)S(1)} %collective-permute-done.rest_2_.other_ref.rest_4_, bf16[2048,1024]{1,0:T(8,128)(2,1)S(1)} %get-tuple-element.16.v_ref), custom_call_target="tpu_custom_call" | custom-call | flops 536870912 | bytes 5242880 | tf_op jit(solution)/shard_map/pallas_call | solution.py:377
  6.5 0.0 copy-start.1
  6.5 11.4 %all-to-all-start = ((bf16[64,16,256]{2,1,0:T(8,128)(2,1)}), bf16[64,16,256]{2,1,0:T(8,128)(2,1)S(1)}, u32[]{:S(2)}, u32[]{:S(2)}) async-start(bf16[64,16,256]{2,1,0:T(8,128)(2,1)} %bitcast.19), calls=%async_computation | async-start | bytes 1048576 | tf_op jit(solution)/shard_map/all_to_all | solution.py:493
  17.8 0.0 copy-done
  17.9 0.0 copy-done.2
  17.9 0.0 copy-done.3
  17.9 0.0 copy-done.4
  17.9 0.0 copy-done.5
  17.9 0.0 copy-start.6
  17.9 0.0 copy-start.7
  17.9 7.1 %shard_map.104 = (bf16[3,256,1024]{2,1,0:T(8,128)(2,1)}, bf16[3,256,256]{2,1,0:T(8,128)(2,1)}, s32[1]{0:T(128)}, bf16[96,1280]{1,0:T(8,128)(2,1)}, bf16[96,1280]{1,0:T(8,128)(2,1)S(1)}) custom-call(s32[1]{0:T(128)} %bitcast.1.odd_ref, s32[128]{0:T(128)S(1)} %bitcast.15, s32[9,128]{1,0:T(8,128)S(1)} %bitcast.13, s32[1,128]{1,0:T(1,128)S(1)} %bitcast.17, ...), custom_call_target="tpu_custom_call" | custom-call | flops 1887436800 | bytes 10485760 | tf_op jit(solution)/shard_map/pallas_call | solution.py:408
  25.0 1.1 %collective-permute-start.1 = (bf16[96,1280]{1,0:T(8,128)(2,1)}, bf16[96,1280]{1,0:T(8,128)(2,1)S(1)}, u32[]{:S(2)}, u32[]{:S(2)}) collective-permute-start(bf16[96,1280]{1,0:T(8,128)(2,1)} %get-tuple-element.18), channel_id=1, source_target_pairs={{0,2},{4,6},{8,10},{12,14},{16,18},{20,22},{24,26},{28,30},{32,34}... | collective-permute-start | bytes 737288 | tf_op jit(solution)/shard_map/ppermute | solution.py:504
  26.1 6.3 %collective-permute-start.2 = (bf16[96,1280]{1,0:T(8,128)(2,1)S(1)}, bf16[96,1280]{1,0:T(8,128)(2,1)S(1)}, u32[]{:S(2)}, u32[]{:S(2)}) collective-permute-start(bf16[96,1280]{1,0:T(8,128)(2,1)S(1)} %get-tuple-element.19), channel_id=1, source_target_pairs={{2,4},{6,8},{10,12},{14,16},{18,20},{22,24},{26,28},{30,32},{34,36... | collective-permute-start | bytes 737288 | tf_op jit(solution)/shard_map/ppermute | solution.py:505
  32.4 0.0 all-to-all-done.parts_ref
  32.4 1.7 %shard_map.107 = bf16[64,16,256]{2,1,0:T(8,128)(2,1)} custom-call(s32[1]{0:T(128)} %bitcast.col_ref, s32[1]{0:T(128)} %get-tuple-element.14.mark_ref, bf16[64,16,256]{2,1,0:T(8,128)(2,1)S(1)} %all-to-all-done.parts_ref, f32[256,256]{1,0:T(8,128)S(1)} %copy-done.1), custom_call_target="tpu_custom_call" | custom-call | flops 16777216 | bytes 1048576 | tf_op jit(solution)/shard_map/pallas_call | solution.py:437
  34.2 4.6 %all-to-all-start.1 = ((bf16[64,16,256]{2,1,0:T(8,128)(2,1)}), bf16[64,16,256]{2,1,0:T(8,128)(2,1)S(1)}, u32[]{:S(2)}, u32[]{:S(2)}) async-start(bf16[64,16,256]{2,1,0:T(8,128)(2,1)} %shard_map.107), calls=%async_computation.1 | async-start | bytes 1048576 | tf_op jit(solution)/shard_map/all_to_all | solution.py:507
  38.8 0.0 collective-permute-done.1.rest_0_
  38.9 0.0 collective-permute-done.2.rest_1_
  38.9 8.9 %shard_map.108 = (bf16[5,256,1024]{2,1,0:T(8,128)(2,1)}, bf16[5,256,256]{2,1,0:T(8,128)(2,1)}, s32[1]{0:T(128)}) custom-call(s32[1]{0:T(128)} %bitcast.1.odd_ref, s32[128]{0:T(128)S(1)} %bitcast.16, s32[9,128]{1,0:T(8,128)S(1)} %bitcast.14, s32[1,128]{1,0:T(1,128)S(1)} %bitcast.18, bf16[9,128,384]{2,1,0:T(8,128)(2,1)S(1)} %bitcast.12, ...), custom_call_target="tpu_custom_call" | custom-call | flops 3145728000 | bytes 10485760 | tf_op jit(solution)/shard_map/pallas_call | solution.py:408
  47.8 3.0 %all-to-all-done.1 = bf16[64,16,256]{2,1,0:T(8,128)(2,1)S(1)} async-done(((bf16[64,16,256]{2,1,0:T(8,128)(2,1)}), bf16[64,16,256]{2,1,0:T(8,128)(2,1)S(1)}, u32[]{:S(2)}, u32[]{:S(2)}) %all-to-all-start.1) | async-done | bytes 524320 | tf_op jit(solution)/shard_map/all_to_all | solution.py:507
  50.8 7.1 %shard_map.109 = (bf16[2048,1024]{1,0:T(8,128)(2,1)}, f32[64,256]{1,0:T(8,128)S(1)}, f32[64,256]{1,0:T(8,128)S(1)}) custom-call(s32[1]{0:T(128)} %bitcast.col_ref, bf16[1024,256]{1,0:T(8,128)(2,1)S(1)} %bitcast.9, f32[1,1024]{1,0:T(1,128)S(1)} %bitcast.10, bf16[2048,128]{1,0:T(8,128)(2,1)S(1)} %copy-done, ...), custom_call_target="tpu_custom_call" | custom-call | flops 6442450944 | bytes 14680064 | tf_op jit(solution)/shard_map/pallas_call | solution.py:453
  57.9 2.4 %collective-permute-start.3 = (f32[64,256]{1,0:T(8,128)S(1)}, f32[64,256]{1,0:T(8,128)S(1)}, u32[]{:S(2)}, u32[]{:S(2)}) collective-permute-start(f32[64,256]{1,0:T(8,128)S(1)} %get-tuple-element.25), channel_id=1, source_target_pairs={{0,1},{1,0},{2,3},{3,2},{4,5},{5,4},{6,7},{7,6},{8,9},{9,8},{10,11... | collective-permute-start | bytes 196616 | tf_op jit(solution)/shard_map/ppermute | solution.py:515
  60.3 0.9 %collective-permute-done.3 = f32[64,256]{1,0:T(8,128)S(1)} collective-permute-done((f32[64,256]{1,0:T(8,128)S(1)}, f32[64,256]{1,0:T(8,128)S(1)}, u32[]{:S(2)}, u32[]{:S(2)}) %collective-permute-start.3) | collective-permute-done | bytes 65568 | tf_op jit(solution)/shard_map/ppermute | solution.py:515
  61.2 0.6 %add.3 = f32[64,256]{1,0:T(8,128)} add(f32[64,256]{1,0:T(8,128)S(1)} %get-tuple-element.24, f32[64,256]{1,0:T(8,128)S(1)} %collective-permute-done.3) | non-fusion elementwise | flops 16384 | bytes 196608 | tf_op jit(solution)/shard_map/add | solution.py:515
  (4 shorter events, 0.0 us)
Async XLA Ops:
  0.6 4.3 %collective-permute-start = (bf16[2048,128]{1,0:T(8,128)(2,1)}, bf16[2048,128]{1,0:T(8,128)(2,1)S(1)}, u32[]{:S(2)}, u32[]{:S(2)}) collective-permute-start(bf16[2048,128]{1,0:T(8,128)(2,1)} %own_ref.1), channel_id=1, source_target_pairs={{0,1},{1,0},{2,3},{3,2},{4,5},{5,4},{6,7},{7,6},{8,9},{9,8},{10,11... | collective-permute-start | bytes 1572872 | tf_op jit(solution)/shard_map/ppermute | solution.py:491
  4.8 13.0 %copy-start = (bf16[2048,128]{1,0:T(8,128)(2,1)S(1)}, bf16[2048,128]{1,0:T(8,128)(2,1)}, u32[]{:S(2)}) copy-start(bf16[2048,128]{1,0:T(8,128)(2,1)} %own_ref.1) | copy-start | bytes 1572868
  4.8 13.0 %copy-start.2 = (bf16[128,9,384]{2,0,1:T(8,128)(2,1)S(1)}, bf16[128,9,384]{2,0,1:T(8,128)(2,1)}, u32[]{:S(2)}) copy-start(bf16[128,9,384]{2,0,1:T(8,128)(2,1)} %param.14) | copy-start | bytes 2654212
  4.8 13.0 %copy-start.3 = (s32[128,9]{0,1:T(8,128)S(1)}, s32[128,9]{0,1:T(8,128)}, u32[]{:S(2)}) copy-start(s32[128,9]{0,1:T(8,128)} %param.15) | copy-start | bytes 13828
  4.9 13.0 %copy-start.4 = (s32[1,128]{1,0:T(1,128)S(1)}, s32[1,128]{1,0:T(1,128)}, u32[]{:S(2)}) copy-start(s32[1,128]{1,0:T(1,128)} %param.12) | copy-start | bytes 1540
  4.9 13.0 %copy-start.5 = (s32[128]{0:T(128)S(1)}, s32[128]{0:T(128)}, u32[]{:S(2)}) copy-start(s32[128]{0:T(128)} %param.13) | copy-start | bytes 1540
  6.5 26.0 %copy-start.1 = (f32[256,256]{1,0:T(8,128)S(1)}, f32[256,256]{1,0:T(8,128)}, u32[]{:S(2)}) copy-start(f32[256,256]{1,0:T(8,128)} %factor_ref.1) | copy-start | bytes 786436
  6.5 26.0 %all-to-all-start = ((bf16[64,16,256]{2,1,0:T(8,128)(2,1)}), bf16[64,16,256]{2,1,0:T(8,128)(2,1)S(1)}, u32[]{:S(2)}, u32[]{:S(2)}) async-start(bf16[64,16,256]{2,1,0:T(8,128)(2,1)} %bitcast.19), calls=%async_computation | async-start | bytes 1048576 | tf_op jit(solution)/shard_map/all_to_all | solution.py:493
  17.9 20.9 %copy-start.6 = (f32[1024]{0:T(1024)S(1)}, f32[1024]{0:T(1024)}, u32[]{:S(2)}) copy-start(f32[1024]{0:T(1024)} %param.17) | copy-start | bytes 12292
  17.9 20.9 %copy-start.7 = (s32[1024]{0:T(1024)S(1)}, s32[1024]{0:T(1024)}, u32[]{:S(2)}) copy-start(s32[1024]{0:T(1024)} %param.16) | copy-start | bytes 12292
  25.0 13.8 %collective-permute-start.1 = (bf16[96,1280]{1,0:T(8,128)(2,1)}, bf16[96,1280]{1,0:T(8,128)(2,1)S(1)}, u32[]{:S(2)}, u32[]{:S(2)}) collective-permute-start(bf16[96,1280]{1,0:T(8,128)(2,1)} %get-tuple-element.18), channel_id=1, source_target_pairs={{0,2},{4,6},{8,10},{12,14},{16,18},{20,22},{24,26},{28,30},{32,34}... | collective-permute-start | bytes 737288 | tf_op jit(solution)/shard_map/ppermute | solution.py:504
  26.1 12.7 %collective-permute-start.2 = (bf16[96,1280]{1,0:T(8,128)(2,1)S(1)}, bf16[96,1280]{1,0:T(8,128)(2,1)S(1)}, u32[]{:S(2)}, u32[]{:S(2)}) collective-permute-start(bf16[96,1280]{1,0:T(8,128)(2,1)S(1)} %get-tuple-element.19), channel_id=1, source_target_pairs={{2,4},{6,8},{10,12},{14,16},{18,20},{22,24},{26,28},{30,32},{34,36... | collective-permute-start | bytes 737288 | tf_op jit(solution)/shard_map/ppermute | solution.py:505
  34.2 16.6 %all-to-all-start.1 = ((bf16[64,16,256]{2,1,0:T(8,128)(2,1)}), bf16[64,16,256]{2,1,0:T(8,128)(2,1)S(1)}, u32[]{:S(2)}, u32[]{:S(2)}) async-start(bf16[64,16,256]{2,1,0:T(8,128)(2,1)} %shard_map.107), calls=%async_computation.1 | async-start | bytes 1048576 | tf_op jit(solution)/shard_map/all_to_all | solution.py:507
  57.9 3.3 %collective-permute-start.3 = (f32[64,256]{1,0:T(8,128)S(1)}, f32[64,256]{1,0:T(8,128)S(1)}, u32[]{:S(2)}, u32[]{:S(2)}) collective-permute-start(f32[64,256]{1,0:T(8,128)S(1)} %get-tuple-element.25), channel_id=1, source_target_pairs={{0,1},{1,0},{2,3},{3,2},{4,5},{5,4},{6,7},{7,6},{8,9},{9,8},{10,11... | collective-permute-start | bytes 196616 | tf_op jit(solution)/shard_map/ppermute | solution.py:515

commit v7 on v5

--- a/solution.py
+++ b/solution.py
@@ -469,7 +469,17 @@
 
     other = lax.ppermute(panel, "col", [(0, 1), (1, 0)])
     partial = partial_sums(panel, other, v_hbm)
-    slices = lax.all_to_all(partial, "row", 0, 0, tiled=True)
+    forward = [i * n_col for i in range(n_row)]
+    groups_of = [forward] + [[i + c for i in reversed(forward)] for c in range(1, n_col)]
+    exchange = functools.partial(
+        lax.all_to_all,
+        axis_name=("row", "col"),
+        split_axis=0,
+        concat_axis=0,
+        axis_index_groups=groups_of,
+        tiled=True,
+    )
+    slices = exchange(partial)
     slices = slices.reshape(n_row, cols // n_row, npan)
 
     early = list(range(1, groups // 2))
@@ -480,7 +490,7 @@
     before = lax.ppermute(to_next, "row", up)
     copies = mix(col, mark, slices, factor)
     after = lax.ppermute(to_last, "row", [(j, i) for i, j in up])
-    mixing = lax.all_to_all(copies.reshape(cols, npan), "row", 0, 0, tiled=True)
+    mixing = exchange(copies.reshape(cols, npan))
     u_late, t_late, _ = couple(late, *shared, (before, after), v_hbm, panel, other)
 
     weights = (occ_mask.astype(F32) * occ_weight / (cols * n_col))[None, :]

time: 61.8 us -> 62.8 us (1.016)
  starting transfers between devices: 27 us -> 30.7 us
  waiting for transfers between devices: 3.92 us -> 1.25 us
    all_to_all x2, starting transfers between devices: 16.2 us -> 22.2 us  [the longest x1 13.1 us: local(): slices = exchange(partial)]
    all_to_all x2, waiting for transfers between devices: 3.01 us -> 0.01 us  [the longest x1 0.01 us: local(): slices = exchange(partial)]
    ppermute x1, starting transfers between devices: 2.41 us -> 0.09 us  [local(): density = own_part + lax.ppermute(other_part, 'col', [(0, 1), (1, 0)])]
  transfers between devices with their start and end apart: 6 -> 6, of which waited for: 2 -> 1; matrix products, arithmetic and copies ran while one was open for 0% -> 0% of each run, Pallas kernels for 33% -> 32%
where the time goes in v7:
time: 62.8 us; the launch traced here: 62.5 us
  starting transfers between devices  30.7 us (49%)
  Pallas kernels  29 us (46%)
  waiting for transfers between devices  1.25 us (2%)
  between operations  0.84 us (1%)
  other arithmetic  0.65 us (1%)
    pallas_call x2, Pallas kernels, couple(): call(kernel, [pltpu.HBM((n, 256, cols), BF16), pltpu.HBM((n, 256, npan),...  15.8 us
    all_to_all x1, starting transfers between devices, local(): slices = exchange(partial)  13.1 us
    all_to_all x1, starting transfers between devices, local(): mixing = exchange(copies.reshape(cols, npan))  9.05 us
    pallas_call x1, Pallas kernels, finish(): call(functools.partial(main_kernel, parts), [jax.ShapeDtypeStruct((rows,...  7.13 us
    ppermute x1, starting transfers between devices, local(): after = lax.ppermute(to_last, 'row', [(j, i) for i, j in up])  6.33 us
    pallas_call x1, Pallas kernels, partial_sums(): call(own_kernel, [pltpu.VMEM((cols, half), BF16), pltpu.VMEM((rows, cols)...  2.69 us
    pallas_call x1, Pallas kernels, mix(): call(mix_kernel, pltpu.VMEM(slices.shape, BF16), [SMEM_SPEC, SMEM_SPEC, V...  1.72 us
    pallas_call x1, Pallas kernels, partial_sums(): call(other_kernel, pltpu.VMEM((cols, 2 * half), BF16), [VMEM_SPEC] * 3, V...  1.6 us
  transfers between devices with their start and end apart: 6, of which 1 were waited for; matrix products, arithmetic and copies ran while one was open for 0% of the time, Pallas kernels for 32%

profile of v7, /device:TPU:1, one launch (start us, length us, event | category | flops | bytes accessed | tf_op | source)
XLA Modules:
  0.0 62.5 jit_solution(17943036011653596977)
XLA Ops:
  0.6 1.5 %collective-permute-start = (bf16[2048,128]{1,0:T(8,128)(2,1)}, bf16[2048,128]{1,0:T(8,128)(2,1)S(1)}, u32[]{:S(2)}, u32[]{:S(2)}) collective-permute-start(bf16[2048,128]{1,0:T(8,128)(2,1)} %own_ref.1), channel_id=1, source_target_pairs={{0,1},{1,0},{2,3},{3,2},{4,5},{5,4},{6,7},{7,6},{8,9},{9,8},{10,11... | collective-permute-start | bytes 1572872 | tf_op jit(solution)/shard_map/ppermute | solution.py:470
  2.1 2.7 %shard_map.105 = (bf16[1024,128]{1,0:T(8,128)(2,1)S(1)}, bf16[2048,1024]{1,0:T(8,128)(2,1)S(1)}) custom-call(bf16[2048,128]{1,0:T(8,128)(2,1)} %own_ref.1, bf16[2048,1024]{1,0:T(8,128)(2,1)} %refs_4_.1), custom_call_target="tpu_custom_call" | custom-call | flops 536870912 | bytes 5242880 | tf_op jit(solution)/shard_map/pallas_call | solution.py:347
  4.8 0.0 copy-start
  4.8 0.0 copy-start.2
  4.8 0.0 copy-start.3
  4.9 0.0 copy-start.4
  4.9 0.0 copy-start.5
  4.9 0.0 collective-permute-done.rest_2_.other_ref.rest_4_
  4.9 1.6 %shard_map.106 = bf16[1024,256]{1,0:T(8,128)(2,1)} custom-call(bf16[1024,128]{1,0:T(8,128)(2,1)S(1)} %get-tuple-element.15.done_ref, bf16[2048,128]{1,0:T(8,128)(2,1)S(1)} %collective-permute-done.rest_2_.other_ref.rest_4_, bf16[2048,1024]{1,0:T(8,128)(2,1)S(1)} %get-tuple-element.16.v_ref), custom_call_target="tpu_custom_call" | custom-call | flops 536870912 | bytes 5242880 | tf_op jit(solution)/shard_map/pallas_call | solution.py:361
  6.5 13.1 %all-to-all-start = ((bf16[64,16,256]{2,1,0:T(8,128)(2,1)}), bf16[64,16,256]{2,1,0:T(8,128)(2,1)S(1)}, u32[]{:S(2)}, u32[]{:S(2)}) async-start(bf16[64,16,256]{2,1,0:T(8,128)(2,1)} %bitcast.5), calls=%async_computation | async-start | bytes 1048576 | tf_op jit(solution)/shard_map/all_to_all | solution.py:482
  19.6 0.0 copy-done
  19.6 0.0 copy-done.2
  19.6 0.0 copy-done.3
  19.7 0.0 copy-start.6
  19.7 0.0 copy-start.7
  19.7 7.1 %shard_map.104 = (bf16[3,256,1024]{2,1,0:T(8,128)(2,1)}, bf16[3,256,256]{2,1,0:T(8,128)(2,1)}, s32[1]{0:T(128)}, bf16[96,1280]{1,0:T(8,128)(2,1)}, bf16[96,1280]{1,0:T(8,128)(2,1)S(1)}) custom-call(s32[128]{0:T(128)S(1)} %bitcast.14, s32[9,128]{1,0:T(8,128)S(1)} %bitcast.12, s32[1,128]{1,0:T(1,128)S(1)} %bitcast.16, bf16[9,128,384]{2,1,0:T(8,128)(2,1)S(1)} %bitcast.10, ...), custom_call_target="tpu_custom_call" | custom-call | flops 1887436800 | bytes 10485760 | tf_op jit(solution)/shard_map/pallas_call | solution.py:387
  26.8 0.6 %collective-permute-start.1 = (bf16[96,1280]{1,0:T(8,128)(2,1)}, bf16[96,1280]{1,0:T(8,128)(2,1)S(1)}, u32[]{:S(2)}, u32[]{:S(2)}) collective-permute-start(bf16[96,1280]{1,0:T(8,128)(2,1)} %get-tuple-element.18), channel_id=1, source_target_pairs={{0,2},{2,4},{4,6},{6,8},{8,10},{10,12},{12,14},{14,16},{16,18},{18... | collective-permute-start | bytes 737288 | tf_op jit(solution)/shard_map/ppermute | solution.py:490
  27.5 6.3 %collective-permute-start.2 = (bf16[96,1280]{1,0:T(8,128)(2,1)S(1)}, bf16[96,1280]{1,0:T(8,128)(2,1)S(1)}, u32[]{:S(2)}, u32[]{:S(2)}) collective-permute-start(bf16[96,1280]{1,0:T(8,128)(2,1)S(1)} %get-tuple-element.19), channel_id=1, source_target_pairs={{2,0},{4,2},{6,4},{8,6},{10,8},{12,10},{14,12},{16,14},{18,16},{20... | collective-permute-start | bytes 737288 | tf_op jit(solution)/shard_map/ppermute | solution.py:492
  33.8 0.0 all-to-all-done.parts_ref
  33.8 0.0 copy-done.1
  33.8 1.7 %shard_map.107 = bf16[64,16,256]{2,1,0:T(8,128)(2,1)} custom-call(s32[1]{0:T(128)} %bitcast.col_ref, s32[1]{0:T(128)} %get-tuple-element.14.mark_ref, bf16[64,16,256]{2,1,0:T(8,128)(2,1)S(1)} %all-to-all-done.parts_ref, f32[256,256]{1,0:T(8,128)S(1)} %copy-done.1), custom_call_target="tpu_custom_call" | custom-call | flops 16777216 | bytes 1048576 | tf_op jit(solution)/shard_map/pallas_call | solution.py:416
  35.5 9.0 %all-to-all-start.1 = ((bf16[64,16,256]{2,1,0:T(8,128)(2,1)}), bf16[64,16,256]{2,1,0:T(8,128)(2,1)S(1)}, u32[]{:S(2)}, u32[]{:S(2)}) async-start(bf16[64,16,256]{2,1,0:T(8,128)(2,1)} %shard_map.107), calls=%async_computation.1 | async-start | bytes 1048576 | tf_op jit(solution)/shard_map/all_to_all | solution.py:493
  44.6 0.0 copy-done.6
  44.6 0.0 copy-done.7
  44.6 0.0 collective-permute-done.1.rest_0_
  44.6 0.0 collective-permute-done.2.rest_1_
  44.6 8.7 %shard_map.108 = (bf16[5,256,1024]{2,1,0:T(8,128)(2,1)}, bf16[5,256,256]{2,1,0:T(8,128)(2,1)}, s32[1]{0:T(128)}) custom-call(s32[128]{0:T(128)S(1)} %bitcast.15, s32[9,128]{1,0:T(8,128)S(1)} %bitcast.13, s32[1,128]{1,0:T(1,128)S(1)} %bitcast.17, bf16[9,128,384]{2,1,0:T(8,128)(2,1)S(1)} %bitcast.11, bf16[96,1280]{1,0:T(8,128)(2,1)S(1)} %collective-permute-done.1.rest_0_, ...), custom_call_target="tpu_custom_call" | custom-call | flops 3145728000 | bytes 10485760 | tf_op jit(solution)/shard_map/pallas_call | solution.py:387
  53.4 0.0 all-to-all-done.1
  53.4 7.1 %shard_map.109 = (bf16[2048,1024]{1,0:T(8,128)(2,1)}, f32[64,256]{1,0:T(8,128)S(1)}, f32[64,256]{1,0:T(8,128)S(1)}) custom-call(s32[1]{0:T(128)} %bitcast.col_ref, bf16[1024,256]{1,0:T(8,128)(2,1)S(1)} %bitcast.8, f32[1,1024]{1,0:T(1,128)S(1)} %bitcast.9, bf16[2048,128]{1,0:T(8,128)(2,1)S(1)} %copy-done, ...), custom_call_target="tpu_custom_call" | custom-call | flops 6442450944 | bytes 14680064 | tf_op jit(solution)/shard_map/pallas_call | solution.py:432
  60.5 0.1 collective-permute-start.3
  60.6 1.2 %collective-permute-done.3 = f32[64,256]{1,0:T(8,128)S(1)} collective-permute-done((f32[64,256]{1,0:T(8,128)S(1)}, f32[64,256]{1,0:T(8,128)S(1)}, u32[]{:S(2)}, u32[]{:S(2)}) %collective-permute-start.3) | collective-permute-done | bytes 65568 | tf_op jit(solution)/shard_map/ppermute | solution.py:501
  61.8 0.6 %add.3 = f32[64,256]{1,0:T(8,128)} add(f32[64,256]{1,0:T(8,128)S(1)} %get-tuple-element.24, f32[64,256]{1,0:T(8,128)S(1)} %collective-permute-done.3) | non-fusion elementwise | flops 16384 | bytes 196608 | tf_op jit(solution)/shard_map/add | solution.py:501
  (4 shorter events, 0.0 us)
Async XLA Ops:
  0.6 4.3 %collective-permute-start = (bf16[2048,128]{1,0:T(8,128)(2,1)}, bf16[2048,128]{1,0:T(8,128)(2,1)S(1)}, u32[]{:S(2)}, u32[]{:S(2)}) collective-permute-start(bf16[2048,128]{1,0:T(8,128)(2,1)} %own_ref.1), channel_id=1, source_target_pairs={{0,1},{1,0},{2,3},{3,2},{4,5},{5,4},{6,7},{7,6},{8,9},{9,8},{10,11... | collective-permute-start | bytes 1572872 | tf_op jit(solution)/shard_map/ppermute | solution.py:470
  4.8 14.8 %copy-start = (bf16[2048,128]{1,0:T(8,128)(2,1)S(1)}, bf16[2048,128]{1,0:T(8,128)(2,1)}, u32[]{:S(2)}) copy-start(bf16[2048,128]{1,0:T(8,128)(2,1)} %own_ref.1) | copy-start | bytes 1572868
  4.8 14.8 %copy-start.2 = (bf16[128,9,384]{2,0,1:T(8,128)(2,1)S(1)}, bf16[128,9,384]{2,0,1:T(8,128)(2,1)}, u32[]{:S(2)}) copy-start(bf16[128,9,384]{2,0,1:T(8,128)(2,1)} %param.14) | copy-start | bytes 2654212
  4.8 14.8 %copy-start.3 = (s32[128,9]{0,1:T(8,128)S(1)}, s32[128,9]{0,1:T(8,128)}, u32[]{:S(2)}) copy-start(s32[128,9]{0,1:T(8,128)} %param.15) | copy-start | bytes 13828
  4.9 14.8 %copy-start.4 = (s32[1,128]{1,0:T(1,128)S(1)}, s32[1,128]{1,0:T(1,128)}, u32[]{:S(2)}) copy-start(s32[1,128]{1,0:T(1,128)} %param.12) | copy-start | bytes 1540
  4.9 14.8 %copy-start.5 = (s32[128]{0:T(128)S(1)}, s32[128]{0:T(128)}, u32[]{:S(2)}) copy-start(s32[128]{0:T(128)} %param.13) | copy-start | bytes 1540
  6.5 27.3 %copy-start.1 = (f32[256,256]{1,0:T(8,128)S(1)}, f32[256,256]{1,0:T(8,128)}, u32[]{:S(2)}) copy-start(f32[256,256]{1,0:T(8,128)} %factor_ref.1) | copy-start | bytes 786436
  6.5 27.3 %all-to-all-start = ((bf16[64,16,256]{2,1,0:T(8,128)(2,1)}), bf16[64,16,256]{2,1,0:T(8,128)(2,1)S(1)}, u32[]{:S(2)}, u32[]{:S(2)}) async-start(bf16[64,16,256]{2,1,0:T(8,128)(2,1)} %bitcast.5), calls=%async_computation | async-start | bytes 1048576 | tf_op jit(solution)/shard_map/all_to_all | solution.py:482
  19.7 24.9 %copy-start.6 = (f32[1024]{0:T(1024)S(1)}, f32[1024]{0:T(1024)}, u32[]{:S(2)}) copy-start(f32[1024]{0:T(1024)} %param.17) | copy-start | bytes 12292
  19.7 24.9 %copy-start.7 = (s32[1024]{0:T(1024)S(1)}, s32[1024]{0:T(1024)}, u32[]{:S(2)}) copy-start(s32[1024]{0:T(1024)} %param.16) | copy-start | bytes 12292
  26.8 17.8 %collective-permute-start.1 = (bf16[96,1280]{1,0:T(8,128)(2,1)}, bf16[96,1280]{1,0:T(8,128)(2,1)S(1)}, u32[]{:S(2)}, u32[]{:S(2)}) collective-permute-start(bf16[96,1280]{1,0:T(8,128)(2,1)} %get-tuple-element.18), channel_id=1, source_target_pairs={{0,2},{2,4},{4,6},{6,8},{8,10},{10,12},{12,14},{14,16},{16,18},{18... | collective-permute-start | bytes 737288 | tf_op jit(solution)/shard_map/ppermute | solution.py:490
  27.5 17.2 %collective-permute-start.2 = (bf16[96,1280]{1,0:T(8,128)(2,1)S(1)}, bf16[96,1280]{1,0:T(8,128)(2,1)S(1)}, u32[]{:S(2)}, u32[]{:S(2)}) collective-permute-start(bf16[96,1280]{1,0:T(8,128)(2,1)S(1)} %get-tuple-element.19), channel_id=1, source_target_pairs={{2,0},{4,2},{6,4},{8,6},{10,8},{12,10},{14,12},{16,14},{18,16},{20... | collective-permute-start | bytes 737288 | tf_op jit(solution)/shard_map/ppermute | solution.py:492
  35.5 17.9 %all-to-all-start.1 = ((bf16[64,16,256]{2,1,0:T(8,128)(2,1)}), bf16[64,16,256]{2,1,0:T(8,128)(2,1)S(1)}, u32[]{:S(2)}, u32[]{:S(2)}) async-start(bf16[64,16,256]{2,1,0:T(8,128)(2,1)} %shard_map.107), calls=%async_computation.1 | async-start | bytes 1048576 | tf_op jit(solution)/shard_map/all_to_all | solution.py:493
  60.5 1.3 %collective-permute-start.3 = (f32[64,256]{1,0:T(8,128)S(1)}, f32[64,256]{1,0:T(8,128)S(1)}, u32[]{:S(2)}, u32[]{:S(2)}) collective-permute-start(f32[64,256]{1,0:T(8,128)S(1)} %get-tuple-element.25), channel_id=1, source_target_pairs={{0,1},{1,0},{2,3},{3,2},{4,5},{5,4},{6,7},{7,6},{8,9},{9,8},{10,11... | collective-permute-start | bytes 196616 | tf_op jit(solution)/shard_map/ppermute | solution.py:501

commit v8 on v5

--- a/solution.py
+++ b/solution.py
@@ -472,8 +472,8 @@
     slices = lax.all_to_all(partial, "row", 0, 0, tiled=True)
     slices = slices.reshape(n_row, cols // n_row, npan)
 
-    early = list(range(1, groups // 2))
-    late = list(range(groups // 2, groups)) + [0]
+    early = list(range(1, groups // 2 - 2))
+    late = list(range(groups // 2 - 2, groups)) + [0]
     shared = (counts, block_present.T, proj_count[None, :], coupling.transpose(1, 0, 2))
     u_early, t_early, mark, to_next, to_last = couple(early, *shared, (), v_hbm, panel, other)
     up = [(i, (i + 1) % n_row) for i in range(n_row)]

time: 61.8 us -> 60.5 us (0.979)
  waiting for transfers between devices: 3.92 us -> 2.21 us
    all_to_all x1, waiting for transfers between devices: 3.01 us -> 0.63 us  [local(): mixing = lax.all_to_all(copies.reshape(cols, npan), 'row', 0, 0, tiled=True)]
    all_to_all x1, waiting for transfers between devices: 0.01 us -> 0.68 us  [local(): slices = lax.all_to_all(partial, 'row', 0, 0, tiled=True)]
  transfers between devices with their start and end apart: 6 -> 6, of which waited for: 2 -> 3; matrix products, arithmetic and copies ran while one was open for 0% -> 0% of each run, Pallas kernels for 33% -> 34%
where the time goes in v8:
time: 60.5 us; the launch traced here: 60.1 us
  Pallas kernels  29 us (48%)
  starting transfers between devices  27.4 us (45%)
  waiting for transfers between devices  2.21 us (4%)
  between operations  0.82 us (1%)
  other arithmetic  0.64 us (1%)
    pallas_call x2, Pallas kernels, couple(): call(kernel, [pltpu.HBM((n, 256, cols), BF16), pltpu.HBM((n, 256, npan),...  15.8 us
    all_to_all x1, starting transfers between devices, local(): slices = lax.all_to_all(partial, 'row', 0, 0, tiled=True)  11.3 us
    pallas_call x1, Pallas kernels, finish(): call(functools.partial(main_kernel, parts), [jax.ShapeDtypeStruct((rows,...  7.12 us
    ppermute x1, starting transfers between devices, local(): after = lax.ppermute(to_last, 'row', [(j, i) for i, j in up])  5.88 us
    all_to_all x1, starting transfers between devices, local(): mixing = lax.all_to_all(copies.reshape(cols, npan), 'row', 0, 0, tiled=True)  4.63 us
    ppermute x1, starting transfers between devices, local(): density = own_part + lax.ppermute(other_part, 'col', [(0, 1), (1, 0)])  3 us
    pallas_call x1, Pallas kernels, partial_sums(): call(own_kernel, [pltpu.VMEM((cols, half), BF16), pltpu.VMEM((rows, cols)...  2.69 us
    pallas_call x1, Pallas kernels, mix(): call(mix_kernel, pltpu.VMEM(slices.shape, BF16), [SMEM_SPEC, SMEM_SPEC, V...  1.77 us
  transfers between devices with their start and end apart: 6, of which 3 were waited for; matrix products, arithmetic and copies ran while one was open for 0% of the time, Pallas kernels for 34%

profile of v8, /device:TPU:1, one launch (start us, length us, event | category | flops | bytes accessed | tf_op | source)
XLA Modules:
  0.0 60.1 jit_solution(13428584231895433453)
XLA Ops:
  0.6 1.5 %collective-permute-start = (bf16[2048,128]{1,0:T(8,128)(2,1)}, bf16[2048,128]{1,0:T(8,128)(2,1)S(1)}, u32[]{:S(2)}, u32[]{:S(2)}) collective-permute-start(bf16[2048,128]{1,0:T(8,128)(2,1)} %own_ref.1), channel_id=1, source_target_pairs={{0,1},{1,0},{2,3},{3,2},{4,5},{5,4},{6,7},{7,6},{8,9},{9,8},{10,11... | collective-permute-start | bytes 1572872 | tf_op jit(solution)/shard_map/ppermute | solution.py:470
  2.1 2.7 %shard_map.105 = (bf16[1024,128]{1,0:T(8,128)(2,1)S(1)}, bf16[2048,1024]{1,0:T(8,128)(2,1)S(1)}) custom-call(bf16[2048,128]{1,0:T(8,128)(2,1)} %own_ref.1, bf16[2048,1024]{1,0:T(8,128)(2,1)} %refs_4_.1), custom_call_target="tpu_custom_call" | custom-call | flops 536870912 | bytes 5242880 | tf_op jit(solution)/shard_map/pallas_call | solution.py:347
  4.8 0.0 copy-start
  4.8 0.0 copy-start.1
  4.8 0.0 copy-start.3
  4.9 0.0 copy-start.4
  4.9 0.0 copy-start.5
  4.9 0.0 collective-permute-done.rest_2_.other_ref.rest_4_
  4.9 1.6 %shard_map.106 = bf16[1024,256]{1,0:T(8,128)(2,1)} custom-call(bf16[1024,128]{1,0:T(8,128)(2,1)S(1)} %get-tuple-element.15.done_ref, bf16[2048,128]{1,0:T(8,128)(2,1)S(1)} %collective-permute-done.rest_2_.other_ref.rest_4_, bf16[2048,1024]{1,0:T(8,128)(2,1)S(1)} %get-tuple-element.16.v_ref), custom_call_target="tpu_custom_call" | custom-call | flops 536870912 | bytes 5242880 | tf_op jit(solution)/shard_map/pallas_call | solution.py:361
  6.5 11.3 %all-to-all-start = ((bf16[64,16,256]{2,1,0:T(8,128)(2,1)}), bf16[64,16,256]{2,1,0:T(8,128)(2,1)S(1)}, u32[]{:S(2)}, u32[]{:S(2)}) async-start(bf16[64,16,256]{2,1,0:T(8,128)(2,1)} %bitcast.5), calls=%async_computation | async-start | bytes 1048576 | tf_op jit(solution)/shard_map/all_to_all | solution.py:472
  17.9 0.0 copy-done
  17.9 0.0 copy-done.1
  17.9 0.0 copy-done.3
  17.9 0.0 copy-done.4
  17.9 0.0 copy-done.5
  17.9 0.0 copy-start.6
  17.9 0.0 copy-start.7
  17.9 5.1 %shard_map.104 = (bf16[1,256,1024]{2,1,0:T(8,128)(2,1)}, bf16[1,256,256]{2,1,0:T(8,128)(2,1)}, s32[1]{0:T(128)}, bf16[96,1280]{1,0:T(8,128)(2,1)}, bf16[96,1280]{1,0:T(8,128)(2,1)S(1)}) custom-call(s32[128]{0:T(128)S(1)} %bitcast.14, s32[9,128]{1,0:T(8,128)S(1)} %bitcast.11, s32[1,128]{1,0:T(1,128)S(1)} %bitcast.16, bf16[9,128,384]{2,1,0:T(8,128)(2,1)S(1)} %bitcast.8, ...), custom_call_target="tpu_custom_call" | custom-call | flops 629145600 | bytes 10485760 | tf_op jit(solution)/shard_map/pallas_call | solution.py:387
  23.0 1.1 %collective-permute-start.1 = (bf16[96,1280]{1,0:T(8,128)(2,1)}, bf16[96,1280]{1,0:T(8,128)(2,1)S(1)}, u32[]{:S(2)}, u32[]{:S(2)}) collective-permute-start(bf16[96,1280]{1,0:T(8,128)(2,1)} %get-tuple-element.18), channel_id=1, source_target_pairs={{0,2},{2,4},{4,6},{6,8},{8,10},{10,12},{12,14},{14,16},{16,18},{18... | collective-permute-start | bytes 737288 | tf_op jit(solution)/shard_map/ppermute | solution.py:480
  24.1 5.9 %collective-permute-start.2 = (bf16[96,1280]{1,0:T(8,128)(2,1)S(1)}, bf16[96,1280]{1,0:T(8,128)(2,1)S(1)}, u32[]{:S(2)}, u32[]{:S(2)}) collective-permute-start(bf16[96,1280]{1,0:T(8,128)(2,1)S(1)} %get-tuple-element.19), channel_id=1, source_target_pairs={{2,0},{4,2},{6,4},{8,6},{10,8},{12,10},{14,12},{16,14},{18,16},{20... | collective-permute-start | bytes 737288 | tf_op jit(solution)/shard_map/ppermute | solution.py:482
  30.0 0.7 %all-to-all-done.parts_ref = bf16[64,16,256]{2,1,0:T(8,128)(2,1)S(1)} async-done(((bf16[64,16,256]{2,1,0:T(8,128)(2,1)}), bf16[64,16,256]{2,1,0:T(8,128)(2,1)S(1)}, u32[]{:S(2)}, u32[]{:S(2)}) %all-to-all-start) | async-done | bytes 524320 | tf_op jit(solution)/shard_map/all_to_all | solution.py:472
  30.7 0.0 copy-done.2
  30.7 1.8 %shard_map.107 = bf16[64,16,256]{2,1,0:T(8,128)(2,1)} custom-call(s32[1]{0:T(128)} %bitcast.col_ref, s32[1]{0:T(128)} %get-tuple-element.14.mark_ref, bf16[64,16,256]{2,1,0:T(8,128)(2,1)S(1)} %all-to-all-done.parts_ref, f32[256,256]{1,0:T(8,128)S(1)} %copy-done.2), custom_call_target="tpu_custom_call" | custom-call | flops 16777216 | bytes 1048576 | tf_op jit(solution)/shard_map/pallas_call | solution.py:416
  32.4 4.6 %all-to-all-start.1 = ((bf16[64,16,256]{2,1,0:T(8,128)(2,1)}), bf16[64,16,256]{2,1,0:T(8,128)(2,1)S(1)}, u32[]{:S(2)}, u32[]{:S(2)}) async-start(bf16[64,16,256]{2,1,0:T(8,128)(2,1)} %shard_map.107), calls=%async_computation.1 | async-start | bytes 1048576 | tf_op jit(solution)/shard_map/all_to_all | solution.py:483
  37.1 0.0 collective-permute-done.1.rest_0_
  37.1 0.0 collective-permute-done.2.rest_1_
  37.1 10.7 %shard_map.108 = (bf16[7,256,1024]{2,1,0:T(8,128)(2,1)}, bf16[7,256,256]{2,1,0:T(8,128)(2,1)}, s32[1]{0:T(128)}) custom-call(s32[128]{0:T(128)S(1)} %bitcast.15, s32[9,128]{1,0:T(8,128)S(1)} %bitcast.12, s32[1,128]{1,0:T(1,128)S(1)} %bitcast.17, bf16[9,128,384]{2,1,0:T(8,128)(2,1)S(1)} %bitcast.9, bf16[96,1280]{1,0:T(8,128)(2,1)S(1)} %collective-permute-done.1.rest_0_, ...), custom_call_target="tpu_custom_call" | custom-call | flops 4404019200 | bytes 10485760 | tf_op jit(solution)/shard_map/pallas_call | solution.py:387
  47.8 0.6 %all-to-all-done.1 = bf16[64,16,256]{2,1,0:T(8,128)(2,1)S(1)} async-done(((bf16[64,16,256]{2,1,0:T(8,128)(2,1)}), bf16[64,16,256]{2,1,0:T(8,128)(2,1)S(1)}, u32[]{:S(2)}, u32[]{:S(2)}) %all-to-all-start.1) | async-done | bytes 524320 | tf_op jit(solution)/shard_map/all_to_all | solution.py:483
  48.5 7.1 %shard_map.109 = (bf16[2048,1024]{1,0:T(8,128)(2,1)}, f32[64,256]{1,0:T(8,128)S(1)}, f32[64,256]{1,0:T(8,128)S(1)}) custom-call(s32[1]{0:T(128)} %bitcast.col_ref, bf16[1024,256]{1,0:T(8,128)(2,1)S(1)} %bitcast.10, f32[1,1024]{1,0:T(1,128)S(1)} %bitcast.13, bf16[2048,128]{1,0:T(8,128)(2,1)S(1)} %copy-done, ...), custom_call_target="tpu_custom_call" | custom-call | flops 6442450944 | bytes 14680064 | tf_op jit(solution)/shard_map/pallas_call | solution.py:432
  55.6 3.0 %collective-permute-start.3 = (f32[64,256]{1,0:T(8,128)S(1)}, f32[64,256]{1,0:T(8,128)S(1)}, u32[]{:S(2)}, u32[]{:S(2)}) collective-permute-start(f32[64,256]{1,0:T(8,128)S(1)} %get-tuple-element.25), channel_id=1, source_target_pairs={{0,1},{1,0},{2,3},{3,2},{4,5},{5,4},{6,7},{7,6},{8,9},{9,8},{10,11... | collective-permute-start | bytes 196616 | tf_op jit(solution)/shard_map/ppermute | solution.py:491
  58.6 0.9 %collective-permute-done.3 = f32[64,256]{1,0:T(8,128)S(1)} collective-permute-done((f32[64,256]{1,0:T(8,128)S(1)}, f32[64,256]{1,0:T(8,128)S(1)}, u32[]{:S(2)}, u32[]{:S(2)}) %collective-permute-start.3) | collective-permute-done | bytes 65568 | tf_op jit(solution)/shard_map/ppermute | solution.py:491
  59.5 0.6 %add.3 = f32[64,256]{1,0:T(8,128)} add(f32[64,256]{1,0:T(8,128)S(1)} %get-tuple-element.24, f32[64,256]{1,0:T(8,128)S(1)} %collective-permute-done.3) | non-fusion elementwise | flops 16384 | bytes 196608 | tf_op jit(solution)/shard_map/add | solution.py:491
  (4 shorter events, 0.0 us)
Async XLA Ops:
  0.6 4.3 %collective-permute-start = (bf16[2048,128]{1,0:T(8,128)(2,1)}, bf16[2048,128]{1,0:T(8,128)(2,1)S(1)}, u32[]{:S(2)}, u32[]{:S(2)}) collective-permute-start(bf16[2048,128]{1,0:T(8,128)(2,1)} %own_ref.1), channel_id=1, source_target_pairs={{0,1},{1,0},{2,3},{3,2},{4,5},{5,4},{6,7},{7,6},{8,9},{9,8},{10,11... | collective-permute-start | bytes 1572872 | tf_op jit(solution)/shard_map/ppermute | solution.py:470
  4.8 13.0 %copy-start = (bf16[2048,128]{1,0:T(8,128)(2,1)S(1)}, bf16[2048,128]{1,0:T(8,128)(2,1)}, u32[]{:S(2)}) copy-start(bf16[2048,128]{1,0:T(8,128)(2,1)} %own_ref.1) | copy-start | bytes 1572868
  4.8 13.0 %copy-start.1 = (bf16[128,9,384]{2,0,1:T(8,128)(2,1)S(1)}, bf16[128,9,384]{2,0,1:T(8,128)(2,1)}, u32[]{:S(2)}) copy-start(bf16[128,9,384]{2,0,1:T(8,128)(2,1)} %param.14) | copy-start | bytes 2654212
  4.8 13.0 %copy-start.3 = (s32[128,9]{0,1:T(8,128)S(1)}, s32[128,9]{0,1:T(8,128)}, u32[]{:S(2)}) copy-start(s32[128,9]{0,1:T(8,128)} %param.15) | copy-start | bytes 13828
  4.9 13.0 %copy-start.4 = (s32[1,128]{1,0:T(1,128)S(1)}, s32[1,128]{1,0:T(1,128)}, u32[]{:S(2)}) copy-start(s32[1,128]{1,0:T(1,128)} %param.12) | copy-start | bytes 1540
  4.9 13.0 %copy-start.5 = (s32[128]{0:T(128)S(1)}, s32[128]{0:T(128)}, u32[]{:S(2)}) copy-start(s32[128]{0:T(128)} %param.13) | copy-start | bytes 1540
  6.5 24.2 %copy-start.2 = (f32[256,256]{1,0:T(8,128)S(1)}, f32[256,256]{1,0:T(8,128)}, u32[]{:S(2)}) copy-start(f32[256,256]{1,0:T(8,128)} %factor_ref.1) | copy-start | bytes 786436
  6.5 24.2 %all-to-all-start = ((bf16[64,16,256]{2,1,0:T(8,128)(2,1)}), bf16[64,16,256]{2,1,0:T(8,128)(2,1)S(1)}, u32[]{:S(2)}, u32[]{:S(2)}) async-start(bf16[64,16,256]{2,1,0:T(8,128)(2,1)} %bitcast.5), calls=%async_computation | async-start | bytes 1048576 | tf_op jit(solution)/shard_map/all_to_all | solution.py:472
  17.9 19.2 %copy-start.6 = (f32[1024]{0:T(1024)S(1)}, f32[1024]{0:T(1024)}, u32[]{:S(2)}) copy-start(f32[1024]{0:T(1024)} %param.17) | copy-start | bytes 12292
  17.9 19.2 %copy-start.7 = (s32[1024]{0:T(1024)S(1)}, s32[1024]{0:T(1024)}, u32[]{:S(2)}) copy-start(s32[1024]{0:T(1024)} %param.16) | copy-start | bytes 12292
  23.0 14.1 %collective-permute-start.1 = (bf16[96,1280]{1,0:T(8,128)(2,1)}, bf16[96,1280]{1,0:T(8,128)(2,1)S(1)}, u32[]{:S(2)}, u32[]{:S(2)}) collective-permute-start(bf16[96,1280]{1,0:T(8,128)(2,1)} %get-tuple-element.18), channel_id=1, source_target_pairs={{0,2},{2,4},{4,6},{6,8},{8,10},{10,12},{12,14},{14,16},{16,18},{18... | collective-permute-start | bytes 737288 | tf_op jit(solution)/shard_map/ppermute | solution.py:480
  24.1 13.0 %collective-permute-start.2 = (bf16[96,1280]{1,0:T(8,128)(2,1)S(1)}, bf16[96,1280]{1,0:T(8,128)(2,1)S(1)}, u32[]{:S(2)}, u32[]{:S(2)}) collective-permute-start(bf16[96,1280]{1,0:T(8,128)(2,1)S(1)} %get-tuple-element.19), channel_id=1, source_target_pairs={{2,0},{4,2},{6,4},{8,6},{10,8},{12,10},{14,12},{16,14},{18,16},{20... | collective-permute-start | bytes 737288 | tf_op jit(solution)/shard_map/ppermute | solution.py:482
  32.4 16.0 %all-to-all-start.1 = ((bf16[64,16,256]{2,1,0:T(8,128)(2,1)}), bf16[64,16,256]{2,1,0:T(8,128)(2,1)S(1)}, u32[]{:S(2)}, u32[]{:S(2)}) async-start(bf16[64,16,256]{2,1,0:T(8,128)(2,1)} %shard_map.107), calls=%async_computation.1 | async-start | bytes 1048576 | tf_op jit(solution)/shard_map/all_to_all | solution.py:483
  55.6 3.9 %collective-permute-start.3 = (f32[64,256]{1,0:T(8,128)S(1)}, f32[64,256]{1,0:T(8,128)S(1)}, u32[]{:S(2)}, u32[]{:S(2)}) collective-permute-start(f32[64,256]{1,0:T(8,128)S(1)} %get-tuple-element.25), channel_id=1, source_target_pairs={{0,1},{1,0},{2,3},{3,2},{4,5},{5,4},{6,7},{7,6},{8,9},{9,8},{10,11... | collective-permute-start | bytes 196616 | tf_op jit(solution)/shard_map/ppermute | solution.py:491

commit v9 on v8

--- a/solution.py
+++ b/solution.py
@@ -218,14 +218,22 @@
         out_ref[mine, half:] = dot(turned, v_ref[:, mine]).T.astype(jnp.bfloat16)
 
 
-def mix_kernel(col_ref, mark_ref, parts_ref, factor_ref, out_ref):
+def mix_kernel(col_ref, mark_ref, parts_ref, factor_ref, out_hbm, some_ref, sem):
     total = jnp.sum(parts_ref[...].astype(jnp.float32), axis=0)
     half = total.shape[1] // 2
     swap = col_ref[0] == 1
     total = jnp.where(swap, pltpu.roll(total, half, 1), total)
     mixed = dot(total, factor_ref[...], precision=lax.Precision.HIGHEST)
     mixed = jnp.where(swap, pltpu.roll(mixed, half, 1), mixed).astype(jnp.bfloat16)
-    out_ref[...] = jnp.broadcast_to(mixed[None], out_ref.shape)
+    some_ref[...] = jnp.broadcast_to(mixed[None], some_ref.shape)
+    some = some_ref.shape[0]
+    copies = []
+    for n in range(out_hbm.shape[0] // some):
+        at = pl.ds(n * some, some)
+        copies.append(pltpu.make_async_copy(some_ref, out_hbm.at[at], sem.at[n]))
+        copies[-1].start()
+    for c in copies:
+        c.wait()
 
 
 def main_kernel(parts, col_ref, mix_ref, weight_ref, own_ref, other_ref, *refs):
@@ -415,12 +423,16 @@
 def mix(col, mark, slices, factor):
     return call(
         mix_kernel,
-        pltpu.VMEM(slices.shape, BF16),
+        pltpu.HBM(slices.shape, BF16),
         [SMEM_SPEC, SMEM_SPEC, VMEM_SPEC, VMEM_SPEC],
-        VMEM_SPEC,
+        HBM_SPEC,
         1 << 24,
         1 << 20,
         8,
+        scratch_shapes=[
+            pltpu.VMEM((8, *slices.shape[1:]), BF16),
+            pltpu.SemaphoreType.DMA((slices.shape[0] // 8,)),
+        ],
     )(col, mark, slices, factor)
 
 

time: 60.5 us -> 60.5 us (level)
  no operation moved by 1% of the time
where the time goes in v9:
time: 60.5 us; the launch traced here: 60.2 us
  Pallas kernels  29 us (48%)
  starting transfers between devices  27.5 us (45%)
  waiting for transfers between devices  2.21 us (4%)
  between operations  0.83 us (1%)
  other arithmetic  0.64 us (1%)
    pallas_call x2, Pallas kernels, couple(): call(kernel, [pltpu.HBM((n, 256, cols), BF16), pltpu.HBM((n, 256, npan),...  15.8 us
    all_to_all x1, starting transfers between devices, local(): slices = lax.all_to_all(partial, 'row', 0, 0, tiled=True)  11.3 us
    pallas_call x1, Pallas kernels, finish(): call(functools.partial(main_kernel, parts), [jax.ShapeDtypeStruct((rows,...  7.12 us
    ppermute x1, starting transfers between devices, local(): after = lax.ppermute(to_last, 'row', [(j, i) for i, j in up])  5.88 us
    all_to_all x1, starting transfers between devices, local(): mixing = lax.all_to_all(copies.reshape(cols, npan), 'row', 0, 0, tiled=True)  4.65 us
    ppermute x1, starting transfers between devices, local(): density = own_part + lax.ppermute(other_part, 'col', [(0, 1), (1, 0)])  3 us
    pallas_call x1, Pallas kernels, partial_sums(): call(own_kernel, [pltpu.VMEM((cols, half), BF16), pltpu.VMEM((rows, cols)...  2.69 us
    pallas_call x1, Pallas kernels, mix(): call(mix_kernel, pltpu.HBM(slices.shape, BF16), [SMEM_SPEC, SMEM_SPEC, VM...  1.79 us
  transfers between devices with their start and end apart: 6, of which 3 were waited for; matrix products, arithmetic and copies ran while one was open for 0% of the time, Pallas kernels for 34%

profile of v9, /device:TPU:1, one launch (start us, length us, event | category | flops | bytes accessed | tf_op | source)
XLA Modules:
  0.0 60.2 jit_solution(5375040962031428666)
XLA Ops:
  0.6 1.5 %collective-permute-start = (bf16[2048,128]{1,0:T(8,128)(2,1)}, bf16[2048,128]{1,0:T(8,128)(2,1)S(1)}, u32[]{:S(2)}, u32[]{:S(2)}) collective-permute-start(bf16[2048,128]{1,0:T(8,128)(2,1)} %own_ref.1), channel_id=1, source_target_pairs={{0,1},{1,0},{2,3},{3,2},{4,5},{5,4},{6,7},{7,6},{8,9},{9,8},{10,11... | collective-permute-start | bytes 1572872 | tf_op jit(solution)/shard_map/ppermute | solution.py:482
  2.1 2.7 %shard_map.105 = (bf16[1024,128]{1,0:T(8,128)(2,1)S(1)}, bf16[2048,1024]{1,0:T(8,128)(2,1)S(1)}) custom-call(bf16[2048,128]{1,0:T(8,128)(2,1)} %own_ref.1, bf16[2048,1024]{1,0:T(8,128)(2,1)} %refs_4_.1), custom_call_target="tpu_custom_call" | custom-call | flops 536870912 | bytes 5242880 | tf_op jit(solution)/shard_map/pallas_call | solution.py:355
  4.8 0.0 copy-start
  4.8 0.0 copy-start.1
  4.8 0.0 copy-start.3
  4.9 0.0 copy-start.4
  4.9 0.0 copy-start.5
  4.9 0.0 collective-permute-done.rest_2_.other_ref.rest_4_
  4.9 1.6 %shard_map.106 = bf16[1024,256]{1,0:T(8,128)(2,1)} custom-call(bf16[1024,128]{1,0:T(8,128)(2,1)S(1)} %get-tuple-element.15.done_ref, bf16[2048,128]{1,0:T(8,128)(2,1)S(1)} %collective-permute-done.rest_2_.other_ref.rest_4_, bf16[2048,1024]{1,0:T(8,128)(2,1)S(1)} %get-tuple-element.16.v_ref), custom_call_target="tpu_custom_call" | custom-call | flops 536870912 | bytes 5242880 | tf_op jit(solution)/shard_map/pallas_call | solution.py:369
  6.5 11.3 %all-to-all-start = ((bf16[64,16,256]{2,1,0:T(8,128)(2,1)}), bf16[64,16,256]{2,1,0:T(8,128)(2,1)S(1)}, u32[]{:S(2)}, u32[]{:S(2)}) async-start(bf16[64,16,256]{2,1,0:T(8,128)(2,1)} %bitcast.5), calls=%async_computation | async-start | bytes 1048576 | tf_op jit(solution)/shard_map/all_to_all | solution.py:484
  17.9 0.0 copy-done
  17.9 0.0 copy-done.1
  17.9 0.0 copy-done.3
  17.9 0.0 copy-done.4
  17.9 0.0 copy-start.6
  17.9 0.0 copy-start.7
  17.9 5.1 %shard_map.104 = (bf16[1,256,1024]{2,1,0:T(8,128)(2,1)}, bf16[1,256,256]{2,1,0:T(8,128)(2,1)}, s32[1]{0:T(128)}, bf16[96,1280]{1,0:T(8,128)(2,1)}, bf16[96,1280]{1,0:T(8,128)(2,1)S(1)}) custom-call(s32[128]{0:T(128)S(1)} %bitcast.14, s32[9,128]{1,0:T(8,128)S(1)} %bitcast.11, s32[1,128]{1,0:T(1,128)S(1)} %bitcast.16, bf16[9,128,384]{2,1,0:T(8,128)(2,1)S(1)} %bitcast.8, ...), custom_call_target="tpu_custom_call" | custom-call | flops 629145600 | bytes 10485760 | tf_op jit(solution)/shard_map/pallas_call | solution.py:395
  23.0 1.1 %collective-permute-start.1 = (bf16[96,1280]{1,0:T(8,128)(2,1)}, bf16[96,1280]{1,0:T(8,128)(2,1)S(1)}, u32[]{:S(2)}, u32[]{:S(2)}) collective-permute-start(bf16[96,1280]{1,0:T(8,128)(2,1)} %get-tuple-element.18), channel_id=1, source_target_pairs={{0,2},{2,4},{4,6},{6,8},{8,10},{10,12},{12,14},{14,16},{16,18},{18... | collective-permute-start | bytes 737288 | tf_op jit(solution)/shard_map/ppermute | solution.py:492
  24.1 5.9 %collective-permute-start.2 = (bf16[96,1280]{1,0:T(8,128)(2,1)S(1)}, bf16[96,1280]{1,0:T(8,128)(2,1)S(1)}, u32[]{:S(2)}, u32[]{:S(2)}) collective-permute-start(bf16[96,1280]{1,0:T(8,128)(2,1)S(1)} %get-tuple-element.19), channel_id=1, source_target_pairs={{2,0},{4,2},{6,4},{8,6},{10,8},{12,10},{14,12},{16,14},{18,16},{20... | collective-permute-start | bytes 737288 | tf_op jit(solution)/shard_map/ppermute | solution.py:494
  30.0 0.7 %all-to-all-done.parts_ref = bf16[64,16,256]{2,1,0:T(8,128)(2,1)S(1)} async-done(((bf16[64,16,256]{2,1,0:T(8,128)(2,1)}), bf16[64,16,256]{2,1,0:T(8,128)(2,1)S(1)}, u32[]{:S(2)}, u32[]{:S(2)}) %all-to-all-start) | async-done | bytes 524320 | tf_op jit(solution)/shard_map/all_to_all | solution.py:484
  30.7 1.8 %shard_map.107 = bf16[64,16,256]{2,1,0:T(8,128)(2,1)} custom-call(s32[1]{0:T(128)} %bitcast.col_ref, s32[1]{0:T(128)} %get-tuple-element.14.mark_ref, bf16[64,16,256]{2,1,0:T(8,128)(2,1)S(1)} %all-to-all-done.parts_ref, f32[256,256]{1,0:T(8,128)S(1)} %copy-done.2), custom_call_target="tpu_custom_call" | custom-call | flops 16777216 | bytes 1048576 | tf_op jit(solution)/shard_map/pallas_call | solution.py:424
  32.5 4.6 %all-to-all-start.1 = ((bf16[64,16,256]{2,1,0:T(8,128)(2,1)}), bf16[64,16,256]{2,1,0:T(8,128)(2,1)S(1)}, u32[]{:S(2)}, u32[]{:S(2)}) async-start(bf16[64,16,256]{2,1,0:T(8,128)(2,1)} %shard_map.107), calls=%async_computation.1 | async-start | bytes 1048576 | tf_op jit(solution)/shard_map/all_to_all | solution.py:495
  37.1 0.0 copy-done.6
  37.1 0.0 copy-done.7
  37.1 0.0 collective-permute-done.1.rest_0_
  37.2 0.0 collective-permute-done.2.rest_1_
  37.2 10.7 %shard_map.108 = (bf16[7,256,1024]{2,1,0:T(8,128)(2,1)}, bf16[7,256,256]{2,1,0:T(8,128)(2,1)}, s32[1]{0:T(128)}) custom-call(s32[128]{0:T(128)S(1)} %bitcast.15, s32[9,128]{1,0:T(8,128)S(1)} %bitcast.12, s32[1,128]{1,0:T(1,128)S(1)} %bitcast.17, bf16[9,128,384]{2,1,0:T(8,128)(2,1)S(1)} %bitcast.9, bf16[96,1280]{1,0:T(8,128)(2,1)S(1)} %collective-permute-done.1.rest_0_, ...), custom_call_target="tpu_custom_call" | custom-call | flops 4404019200 | bytes 10485760 | tf_op jit(solution)/shard_map/pallas_call | solution.py:395
  47.9 0.6 %all-to-all-done.1 = bf16[64,16,256]{2,1,0:T(8,128)(2,1)S(1)} async-done(((bf16[64,16,256]{2,1,0:T(8,128)(2,1)}), bf16[64,16,256]{2,1,0:T(8,128)(2,1)S(1)}, u32[]{:S(2)}, u32[]{:S(2)}) %all-to-all-start.1) | async-done | bytes 524320 | tf_op jit(solution)/shard_map/all_to_all | solution.py:495
  48.5 7.1 %shard_map.109 = (bf16[2048,1024]{1,0:T(8,128)(2,1)}, f32[64,256]{1,0:T(8,128)S(1)}, f32[64,256]{1,0:T(8,128)S(1)}) custom-call(s32[1]{0:T(128)} %bitcast.col_ref, bf16[1024,256]{1,0:T(8,128)(2,1)S(1)} %bitcast.10, f32[1,1024]{1,0:T(1,128)S(1)} %bitcast.13, bf16[2048,128]{1,0:T(8,128)(2,1)S(1)} %copy-done, ...), custom_call_target="tpu_custom_call" | custom-call | flops 6442450944 | bytes 14680064 | tf_op jit(solution)/shard_map/pallas_call | solution.py:444
  55.6 3.0 %collective-permute-start.3 = (f32[64,256]{1,0:T(8,128)S(1)}, f32[64,256]{1,0:T(8,128)S(1)}, u32[]{:S(2)}, u32[]{:S(2)}) collective-permute-start(f32[64,256]{1,0:T(8,128)S(1)} %get-tuple-element.25), channel_id=1, source_target_pairs={{0,1},{1,0},{2,3},{3,2},{4,5},{5,4},{6,7},{7,6},{8,9},{9,8},{10,11... | collective-permute-start | bytes 196616 | tf_op jit(solution)/shard_map/ppermute | solution.py:503
  58.6 0.9 %collective-permute-done.3 = f32[64,256]{1,0:T(8,128)S(1)} collective-permute-done((f32[64,256]{1,0:T(8,128)S(1)}, f32[64,256]{1,0:T(8,128)S(1)}, u32[]{:S(2)}, u32[]{:S(2)}) %collective-permute-start.3) | collective-permute-done | bytes 65568 | tf_op jit(solution)/shard_map/ppermute | solution.py:503
  59.5 0.6 %add.3 = f32[64,256]{1,0:T(8,128)} add(f32[64,256]{1,0:T(8,128)S(1)} %get-tuple-element.24, f32[64,256]{1,0:T(8,128)S(1)} %collective-permute-done.3) | non-fusion elementwise | flops 16384 | bytes 196608 | tf_op jit(solution)/shard_map/add | solution.py:503
  (4 shorter events, 0.0 us)
Async XLA Ops:
  0.6 4.3 %collective-permute-start = (bf16[2048,128]{1,0:T(8,128)(2,1)}, bf16[2048,128]{1,0:T(8,128)(2,1)S(1)}, u32[]{:S(2)}, u32[]{:S(2)}) collective-permute-start(bf16[2048,128]{1,0:T(8,128)(2,1)} %own_ref.1), channel_id=1, source_target_pairs={{0,1},{1,0},{2,3},{3,2},{4,5},{5,4},{6,7},{7,6},{8,9},{9,8},{10,11... | collective-permute-start | bytes 1572872 | tf_op jit(solution)/shard_map/ppermute | solution.py:482
  4.8 13.0 %copy-start = (bf16[2048,128]{1,0:T(8,128)(2,1)S(1)}, bf16[2048,128]{1,0:T(8,128)(2,1)}, u32[]{:S(2)}) copy-start(bf16[2048,128]{1,0:T(8,128)(2,1)} %own_ref.1) | copy-start | bytes 1572868
  4.8 13.0 %copy-start.1 = (bf16[128,9,384]{2,0,1:T(8,128)(2,1)S(1)}, bf16[128,9,384]{2,0,1:T(8,128)(2,1)}, u32[]{:S(2)}) copy-start(bf16[128,9,384]{2,0,1:T(8,128)(2,1)} %param.14) | copy-start | bytes 2654212
  4.8 13.0 %copy-start.3 = (s32[128,9]{0,1:T(8,128)S(1)}, s32[128,9]{0,1:T(8,128)}, u32[]{:S(2)}) copy-start(s32[128,9]{0,1:T(8,128)} %param.15) | copy-start | bytes 13828
  4.9 13.0 %copy-start.4 = (s32[1,128]{1,0:T(1,128)S(1)}, s32[1,128]{1,0:T(1,128)}, u32[]{:S(2)}) copy-start(s32[1,128]{1,0:T(1,128)} %param.12) | copy-start | bytes 1540
  4.9 13.0 %copy-start.5 = (s32[128]{0:T(128)S(1)}, s32[128]{0:T(128)}, u32[]{:S(2)}) copy-start(s32[128]{0:T(128)} %param.13) | copy-start | bytes 1540
  6.5 24.2 %copy-start.2 = (f32[256,256]{1,0:T(8,128)S(1)}, f32[256,256]{1,0:T(8,128)}, u32[]{:S(2)}) copy-start(f32[256,256]{1,0:T(8,128)} %factor_ref.1) | copy-start | bytes 786436
  6.5 24.2 %all-to-all-start = ((bf16[64,16,256]{2,1,0:T(8,128)(2,1)}), bf16[64,16,256]{2,1,0:T(8,128)(2,1)S(1)}, u32[]{:S(2)}, u32[]{:S(2)}) async-start(bf16[64,16,256]{2,1,0:T(8,128)(2,1)} %bitcast.5), calls=%async_computation | async-start | bytes 1048576 | tf_op jit(solution)/shard_map/all_to_all | solution.py:484
  17.9 19.2 %copy-start.6 = (f32[1024]{0:T(1024)S(1)}, f32[1024]{0:T(1024)}, u32[]{:S(2)}) copy-start(f32[1024]{0:T(1024)} %param.17) | copy-start | bytes 12292
  17.9 19.2 %copy-start.7 = (s32[1024]{0:T(1024)S(1)}, s32[1024]{0:T(1024)}, u32[]{:S(2)}) copy-start(s32[1024]{0:T(1024)} %param.16) | copy-start | bytes 12292
  23.0 14.1 %collective-permute-start.1 = (bf16[96,1280]{1,0:T(8,128)(2,1)}, bf16[96,1280]{1,0:T(8,128)(2,1)S(1)}, u32[]{:S(2)}, u32[]{:S(2)}) collective-permute-start(bf16[96,1280]{1,0:T(8,128)(2,1)} %get-tuple-element.18), channel_id=1, source_target_pairs={{0,2},{2,4},{4,6},{6,8},{8,10},{10,12},{12,14},{14,16},{16,18},{18... | collective-permute-start | bytes 737288 | tf_op jit(solution)/shard_map/ppermute | solution.py:492
  24.1 13.1 %collective-permute-start.2 = (bf16[96,1280]{1,0:T(8,128)(2,1)S(1)}, bf16[96,1280]{1,0:T(8,128)(2,1)S(1)}, u32[]{:S(2)}, u32[]{:S(2)}) collective-permute-start(bf16[96,1280]{1,0:T(8,128)(2,1)S(1)} %get-tuple-element.19), channel_id=1, source_target_pairs={{2,0},{4,2},{6,4},{8,6},{10,8},{12,10},{14,12},{16,14},{18,16},{20... | collective-permute-start | bytes 737288 | tf_op jit(solution)/shard_map/ppermute | solution.py:494
  32.5 16.0 %all-to-all-start.1 = ((bf16[64,16,256]{2,1,0:T(8,128)(2,1)}), bf16[64,16,256]{2,1,0:T(8,128)(2,1)S(1)}, u32[]{:S(2)}, u32[]{:S(2)}) async-start(bf16[64,16,256]{2,1,0:T(8,128)(2,1)} %shard_map.107), calls=%async_computation.1 | async-start | bytes 1048576 | tf_op jit(solution)/shard_map/all_to_all | solution.py:495
  55.6 3.9 %collective-permute-start.3 = (f32[64,256]{1,0:T(8,128)S(1)}, f32[64,256]{1,0:T(8,128)S(1)}, u32[]{:S(2)}, u32[]{:S(2)}) collective-permute-start(f32[64,256]{1,0:T(8,128)S(1)} %get-tuple-element.25), channel_id=1, source_target_pairs={{0,1},{1,0},{2,3},{3,2},{4,5},{5,4},{6,7},{7,6},{8,9},{9,8},{10,11... | collective-permute-start | bytes 196616 | tf_op jit(solution)/shard_map/ppermute | solution.py:503
